TPU v7x, 256 devices: a whole 4x4x8 slice. The times are simulated.
256 devices in a mesh: seg: 4 (over y), rank: 64 (over z, x, core).
Axes of the slice: x: 4, y: 4, z: 8, core: 2. Of those that a mesh axis runs over, the one named last changes fastest.
Arguments:
- parent_nodes: float32 [655360, 375], P(('seg', 'rank')), as said below
- marks: int32 [256, 256], P(('seg', 'rank')), may hold values from 0 to 2559, as said below
- child_owner: int32 [524288, 1], P(('seg', 'rank')), may hold values from 0 to 255; in each aligned block of 2048 rows (0 to 2047, 2048 to 4095, ...) at most 16 rows name the same one
- face_link: int32 [1048576, 6], P(('seg', 'rank')), may hold values from 0 to 12287
Outputs:
- node_mass: float32 [125, 1048576], P(None, ('seg', 'rank'))
- face_mass: float32 [150, 1048576], P(None, ('seg', 'rank'))
Inputs may be any that keep to these rules, and one draw needn't show every extreme that they name: `marks`: each row holds distinct local parent indices of its device. `child_owner`: among the children of one device no owner is named more than 16 times, a bound that some block reaches. `face_link`: the first 4096 values name slots of the previous owner along rank, the next 4096 own slots, the last 4096 slots of the next owner. `parent_nodes`: nodes of a slightly perturbed cube of side 3 to 6 around a point of the box from -8 to 8.
All inputs are finite; a program needn't handle non-finite values.
Results may differ from a plain program's by a relative error of at most 0.0003.
Values sent between devices are 32-bit elements; how exact they have to be, the bound alone decides.
No kernel may reach another device: no remote copies, remote signals or barrier semaphores. Data moves between devices by JAX's collectives and lax.ppermute only.
A program may use at most 192 MiB of HBM per device.

v0:
```python
import math

import jax
import jax.numpy as jnp
import numpy as np
from jax import lax
from jax.sharding import PartitionSpec as P


def shifted(array, axis, by):
    count = lax.axis_size(axis)
    pairs = [(i, i + by) for i in range(count) if 0 <= i + by < count]
    return lax.ppermute(array, axis, pairs)


def gll_tables():
    points = np.array([-1.0, -math.sqrt(3.0 / 7.0), 0.0, math.sqrt(3.0 / 7.0), 1.0])
    weights = np.array([0.1, 49.0 / 90.0, 32.0 / 45.0, 49.0 / 90.0, 0.1])
    barycentric = np.array(
        [1.0 / np.prod([points[j] - points[m] for m in range(5) if m != j]) for j in range(5)]
    )
    slopes = np.zeros((5, 5))
    for i in range(5):
        for j in range(5):
            if i != j:
                slopes[i, j] = barycentric[j] / barycentric[i] / (points[i] - points[j])
        slopes[i, i] = -np.sum(slopes[i])

    def lagrange_at(where):
        table = np.ones((5, 5))
        for a in range(5):
            for j in range(5):
                for m in range(5):
                    if m != j:
                        table[a, j] *= (where[a] - points[m]) / (points[j] - points[m])
        return table

    def blend(value, side):
        return (1.0 - value) / 2.0 if side == 0 else (1.0 + value) / 2.0

    def flat(i, j, k):
        return i * 25 + j * 5 + k

    ends = (0, 4)
    gordon = np.zeros((125, 125))
    for i in range(5):
        for j in range(5):
            for k in range(5):
                r, s, t = (points[i], points[j], points[k])
                target = flat(i, j, k)
                for a in range(2):
                    gordon[target, flat(ends[a], j, k)] += blend(r, a)
                    gordon[target, flat(i, ends[a], k)] += blend(s, a)
                    gordon[target, flat(i, j, ends[a])] += blend(t, a)
                    for b in range(2):
                        gordon[target, flat(ends[a], ends[b], k)] -= blend(r, a) * blend(s, b)
                        gordon[target, flat(ends[a], j, ends[b])] -= blend(r, a) * blend(t, b)
                        gordon[target, flat(i, ends[a], ends[b])] -= blend(s, a) * blend(t, b)
                        for c in range(2):
                            gordon[target, flat(ends[a], ends[b], ends[c])] += (
                                blend(r, a) * blend(s, b) * blend(t, c)
                            )
    children = np.zeros((8, 125, 125))
    for octant in range(8):
        shifts = [2 * (octant >> 2 & 1) - 1, 2 * (octant >> 1 & 1) - 1, 2 * (octant & 1) - 1]
        tables = [lagrange_at((points + shifts[q]) / 2.0) for q in range(3)]
        children[octant] = np.kron(np.kron(tables[0], tables[1]), tables[2]) @ gordon
    identity = np.eye(5)
    derivs = [
        np.kron(np.kron(slopes, identity), identity),
        np.kron(np.kron(identity, slopes), identity),
        np.kron(np.kron(identity, identity), slopes),
    ]
    deriv_table = np.concatenate([derivs[q].T for q in range(3)], axis=1)
    mass_weights = np.kron(np.kron(weights, weights), weights)
    face_weights = np.kron(weights, weights)
    tangents = [(1, 2), (1, 2), (0, 2), (0, 2), (0, 1), (0, 1)]
    boundary = [
        flat(i, j, k)
        for i in range(5)
        for j in range(5)
        for k in range(5)
        if i in ends or j in ends or k in ends
    ]
    children_map = children.transpose(2, 0, 1).reshape(125, 1000)
    return (children_map, deriv_table, mass_weights, face_weights, tangents, np.array(boundary))


def geometry(coords, tables):
    children_map, deriv_table, mass_weights, face_weights, tangents, boundary = tables
    width = coords.shape[0]
    deriv = jnp.einsum(
        "wcn,nm->cmw",
        coords.reshape(width, 3, 125),
        jnp.asarray(deriv_table, jnp.float32),
        precision=lax.Precision.HIGHEST,
        preferred_element_type=jnp.float32,
    )
    deriv = deriv.reshape(3, 3, 5, 5, 5, width)
    jac = [[deriv[c, d] for d in range(3)] for c in range(3)]
    determinant = (
        jac[0][0] * (jac[1][1] * jac[2][2] - jac[1][2] * jac[2][1])
        - jac[0][1] * (jac[1][0] * jac[2][2] - jac[1][2] * jac[2][0])
        + jac[0][2] * (jac[1][0] * jac[2][1] - jac[1][1] * jac[2][0])
    )
    mass = determinant.reshape(125, width) * jnp.asarray(mass_weights, jnp.float32)[:, None]
    areas = []
    for face in range(6):
        first, second = tangents[face]
        direction = face // 2
        side = 0 if face % 2 == 0 else 4
        along = lax.index_in_dim(deriv[:, first], side, axis=1 + direction, keepdims=False)
        across = lax.index_in_dim(deriv[:, second], side, axis=1 + direction, keepdims=False)
        normal_x = along[1] * across[2] - along[2] * across[1]
        normal_y = along[2] * across[0] - along[0] * across[2]
        normal_z = along[0] * across[1] - along[1] * across[0]
        length = jnp.sqrt(normal_x * normal_x + normal_y * normal_y + normal_z * normal_z).reshape(
            25, width
        )
        areas.append(length * jnp.asarray(face_weights, jnp.float32)[:, None])
    return (mass, jnp.concatenate(areas, axis=0))


def blocked_geometry(coords_of, total, tables):
    width = 512
    blocks = total // width

    def run_block(number, carry):
        mass_all, faces_all = carry
        mass, faces = geometry(coords_of(number * width, width), tables)
        mass_all = lax.dynamic_update_slice_in_dim(mass_all, mass, number * width, 1)
        faces_all = lax.dynamic_update_slice_in_dim(faces_all, faces, number * width, 1)
        return (mass_all, faces_all)

    start = (jnp.zeros((125, total), jnp.float32), jnp.zeros((150, total), jnp.float32))
    return lax.fori_loop(0, blocks, run_block, start)


def body(parent_nodes, marks, child_owner, face_link):
    tables = gll_tables()
    children_map = jnp.asarray(tables[0], jnp.float32)
    seg_count = lax.axis_size("seg")
    rank_count = lax.axis_size("rank")
    devices = seg_count * rank_count
    kids = child_owner.shape[0]
    marked = marks.shape[1]
    capacity = max(2, 2 * kids // devices)
    slot_count = devices * capacity
    owners = child_owner[:, 0]
    onehot = (owners[:, None] == jnp.arange(devices, dtype=jnp.int32)[None, :]).astype(jnp.int32)
    position = jnp.sum(jnp.cumsum(onehot, axis=0) * onehot, axis=1) - 1
    target = owners * capacity + position
    picked = parent_nodes[marks[0]]
    made = jnp.dot(
        picked.reshape(marked * 3, 125),
        children_map,
        precision=lax.Precision.HIGHEST,
        preferred_element_type=jnp.float32,
    )
    made = made.reshape(marked, 3, 8, 125).transpose(0, 2, 1, 3).reshape(kids, 375)
    outgoing = jnp.zeros((slot_count, 375), jnp.float32).at[target].set(made)
    outgoing = outgoing.reshape(seg_count, rank_count, capacity, 375)
    arrived = lax.all_to_all(
        lax.all_to_all(outgoing, "seg", split_axis=0, concat_axis=0, tiled=True),
        "rank",
        split_axis=1,
        concat_axis=1,
        tiled=True,
    ).reshape(slot_count, 375)

    def coords_of(start, width):
        return lax.dynamic_slice_in_dim(arrived, start, width, 0)

    mass, faces = blocked_geometry(coords_of, slot_count, tables)
    before = shifted(faces, "rank", 1)
    after = shifted(faces, "rank", -1)
    pool = jnp.concatenate([before, faces, after], axis=1).reshape(6, 25, 3 * slot_count)
    fetched = []
    for face in range(6):
        opposite = face + 1 - 2 * (face % 2)
        fetched.append(jnp.take(pool[opposite], face_link[:, face], axis=1))
    return (mass, faces + jnp.concatenate(fetched, axis=0))


def solution(mesh):
    return jax.shard_map(
        body,
        mesh=mesh,
        in_specs=(
            P(("seg", "rank"), None),
            P(("seg", "rank"), None),
            P(("seg", "rank"), None),
            P(("seg", "rank"), None),
        ),
        out_specs=(P(None, ("seg", "rank")), P(None, ("seg", "rank"))),
        check_vma=False,
    )
```

profile of v0, /device:TPU:32, one launch (start us, length us, event | category | flops | bytes accessed | tf_op | source)
XLA Modules:
  0.0 634.0 jit_solution(6609835828261364974)
XLA Ops:
  4.3 5.4 copy.59
  9.7 3.3 gather_fusion
  13.3 2.7 convolution_bitcast_fusion.1
  16.0 4.1 copy.62
  20.1 4.6 reshape.510
  24.7 12.1 %scatter_custom_fusion = f32[4096,375]{1,0:T(8,128)} fusion(s32[2048]{0:T(1024)S(1)} %bitcast.83, f32[2048,375]{1,0:T(8,128)S(1)} %reshape.510, f32[]{:T(128)} %constant.62.clone.1), kind=kCustom, calls=%fused_computation.33 | custom fusion | bytes 6144004 | tf_op jit(solution)/shard_map/scatter | solution.py:161
  36.8 75.7 %all_to_all.10 = f32[4,64,16,375]{3,2,1,0:T(8,128)S(1)} all-to-all(f32[4,64,16,375]{3,2,1,0:T(8,128)} %bitcast.65), channel_id=1, replica_groups=mesh['seg'=4,'rank'=64] {'seg'}, dimensions={0} | all-to-all | bytes 12288000 | tf_op jit(solution)/shard_map/all_to_all | solution.py:164
  112.6 3.6 copy.63
  116.2 11.9 %all-to-all-start.1 = ((f32[4,64,16,375]{3,2,0,1:T(8,128)}), f32[4,64,16,375]{3,2,0,1:T(8,128)}, u32[]{:S(2)}, u32[]{:S(2)}) async-start(f32[4,64,16,375]{3,2,0,1:T(8,128)} %copy.63), calls=%async_computation.1 | async-start | bytes 12582912 | tf_op jit(solution)/shard_map/all_to_all | solution.py:163
  128.2 140.6 %all-to-all-done.1 = f32[4,64,16,375]{3,2,0,1:T(8,128)} async-done(((f32[4,64,16,375]{3,2,0,1:T(8,128)}), f32[4,64,16,375]{3,2,0,1:T(8,128)}, u32[]{:S(2)}, u32[]{:S(2)}) %all-to-all-start.1) | async-done | bytes 6144032 | tf_op jit(solution)/shard_map/all_to_all | solution.py:163
  268.8 6.0 copy.64
  274.8 6.6 %copy.65 = f32[4096,375]{0,1:T(8,128)} copy(f32[4096,375]{1,0:T(8,128)} %bitcast.66) | data formatting | bytes 12288000
  284.6 130.8 %while.17 = (s32[]{:T(128)}, f32[125,4096]{1,0:T(8,128)}, f32[150,4096]{1,0:T(8,128)}, f32[4096,375]{0,1:T(8,128)}, s32[]{:T(128)}, /*index=5*/s32[]{:T(128)}, s...) while((s32[]{:T(128)}, f32[125,4096]{1,0:T(8,128)}, ...), condition=%wide.region_5.6_spmd.clone.clone, body=%wide.region_4.5_spmd.sunk.clone.clone.sunk | while | flops 866112000 | bytes 26822544 | solution.py:136
  290.2 2.4 fusion.25
  293.5 2.4 slice_bitcast_fusion.5
  306.6 2.4 fusion.25
  309.8 2.4 slice_bitcast_fusion.5
  322.9 2.4 fusion.25
  326.2 2.4 slice_bitcast_fusion.5
  339.2 2.4 fusion.25
  342.5 2.4 slice_bitcast_fusion.5
  355.6 2.4 fusion.25
  358.9 2.4 slice_bitcast_fusion.5
  371.9 2.4 fusion.25
  375.2 2.4 slice_bitcast_fusion.5
  388.3 2.4 fusion.25
  391.6 2.4 slice_bitcast_fusion.5
  404.6 2.4 fusion.25
  407.9 2.4 slice_bitcast_fusion.5
  415.4 2.4 collective-permute-start.1
  420.2 4.9 copy.69
  425.0 20.9 %collective-permute-done.1 = f32[150,4096]{1,0:T(8,128)} collective-permute-done((f32[150,4096]{1,0:T(8,128)}, f32[150,4096]{1,0:T(8,128)}, u32[]{:S(2)}, u32[]{:S(2)}) %collective-permute-start.1) | collective-permute-done | bytes 2457632 | tf_op jit(solution)/shard_map/ppermute | solution.py:13
  445.9 4.8 copy.68
  451.7 3.3 copy.66
  455.0 11.9 %pad_maximum_fusion = f32[150,12288]{0,1:T(8,128)} fusion(f32[150,4096]{0,1:T(8,128)} %copy.68, f32[150,4096]{0,1:T(8,128)} %copy.69, f32[150,4096]{0,1:T(8,128)} %copy.66), kind=kLoop, calls=%fused_computation.32 | loop fusion | flops 3686400 | bytes 14745600 | tf_op jit(solution)/shard_map/concatenate | solution.py:177
  466.9 29.7 %fusion.15 = (f32[25,12288]{0,1:T(8,128)}, f32[25,12288]{0,1:T(8,128)}, f32[25,12288]{0,1:T(8,128)}, f32[25,12288]{0,1:T(8,128)}, f32[25,12288]{0,1:T(8,128)}, /*index=5*/f32[25,12288]{0,1:T(8,128)}) fusion(f32[150,12288]{0,1:T(8,128)} %pad_maximum_fusion), kind=kLoop, calls=%fused_computation.74 | loop fusion | bytes 14745600 | tf_op jit(solution)/shard_map/slice | solution.py:181
  496.6 17.0 %gather_fusion.2 = f32[4096,25]{1,0:T(8,128)} fusion(f32[25,12288]{0,1:T(8,128)} %get-tuple-element.294, s32[4096]{0:T(1024)S(1)} %fusion.10), kind=kCustom, calls=%fused_computation.1.clone | custom fusion | bytes 835584 | tf_op jit(solution)/shard_map/jit(_take)/gather | solution.py:181
  513.6 17.0 %gather_fusion.1 = f32[4096,25]{1,0:T(8,128)} fusion(f32[25,12288]{0,1:T(8,128)} %get-tuple-element.295, s32[4096]{0:T(1024)S(1)} %fusion.9), kind=kCustom, calls=%fused_computation.clone | custom fusion | bytes 835584 | tf_op jit(solution)/shard_map/jit(_take)/gather | solution.py:181
  530.5 17.0 %gather_fusion.4 = f32[4096,25]{1,0:T(8,128)} fusion(f32[25,12288]{0,1:T(8,128)} %get-tuple-element.292, s32[4096]{0:T(1024)S(1)} %fusion.12), kind=kCustom, calls=%fused_computation.3.clone | custom fusion | bytes 835584 | tf_op jit(solution)/shard_map/jit(_take)/gather | solution.py:181
  547.5 17.0 %gather_fusion.3 = f32[4096,25]{1,0:T(8,128)} fusion(f32[25,12288]{0,1:T(8,128)} %get-tuple-element.293, s32[4096]{0:T(1024)S(1)} %fusion.11), kind=kCustom, calls=%fused_computation.2.clone | custom fusion | bytes 835584 | tf_op jit(solution)/shard_map/jit(_take)/gather | solution.py:181
  564.5 16.9 %gather_fusion.6 = f32[4096,25]{1,0:T(8,128)} fusion(f32[25,12288]{0,1:T(8,128)} %get-tuple-element.290, s32[4096]{0:T(1024)S(1)} %fusion.14), kind=kCustom, calls=%fused_computation.5.clone | custom fusion | bytes 835584 | tf_op jit(solution)/shard_map/jit(_take)/gather | solution.py:181
  581.4 17.0 %gather_fusion.5 = f32[4096,25]{1,0:T(8,128)} fusion(f32[25,12288]{0,1:T(8,128)} %get-tuple-element.291, s32[4096]{0:T(1024)S(1)} %fusion.13), kind=kCustom, calls=%fused_computation.4.clone | custom fusion | bytes 835584 | tf_op jit(solution)/shard_map/jit(_take)/gather | solution.py:181
  598.4 6.4 %select_bitcast_fusion.4 = (f32[25,4096]{0,1:T(8,128)S(1)}, f32[25,4096]{0,1:T(8,128)}) fusion(f32[4096,25]{1,0:T(8,128)} %gather_fusion.2, pred[4096]{0:T(1024)(128)(4,1)S(1)} %compare_and_fusion.4, f32[4096,25]{1,0:T(8,128)} %gather_fusion.1, pred[4096]{0:T(1024)(128)(4,1)S(1)} %compare_and_fusion.5), kind=kLoop, calls=%fused_computation.41 | loop fusion | flops 204800 | bytes 1646592 | tf_op jit(solution)/shard_map/jit(_take)/select_n | solution.py:181
  604.8 4.4 select_bitcast_fusion.2
  609.3 4.5 select_bitcast_fusion
  613.7 9.2 %concatenate.14 = f32[150,4096]{0,1:T(8,128)} concatenate(f32[25,4096]{0,1:T(8,128)} %get-tuple-element.307, f32[25,4096]{0,1:T(8,128)S(1)} %get-tuple-element.306, f32[25,4096]{0,1:T(8,128)} %get-tuple-element.305, f32[25,4096]{0,1:T(8,128)} %get-tuple-element.304, f32[25,4096]{0,1:T(8,128)} %get-tuple-element.303, f32[25,4096]{0,1:T(8,128)} %get-tuple-element.302), dimensions={0} | concatenate | bytes 4915200 | tf_op jit(solution)/shard_map/concatenate | solution.py:182
  623.0 6.1 add.194
  629.0 5.0 copy.70
  (212 shorter events, 101.4 us)
Async XLA Ops:
  2.1 1.2 copy-start.7
  4.3 5.4 copy-start.11
  9.7 3.6 copy-start.6
  116.2 11.9 %copy-start.8 = (s32[4096,6]{0,1:T(8,128)S(1)}, s32[4096,6]{0,1:T(8,128)}, u32[]{:S(2)}) copy-start(s32[4096,6]{0,1:T(8,128)} %param.20) | copy-start | bytes 294916
  116.2 152.6 %all-to-all-start.1 = ((f32[4,64,16,375]{3,2,0,1:T(8,128)}), f32[4,64,16,375]{3,2,0,1:T(8,128)}, u32[]{:S(2)}, u32[]{:S(2)}) async-start(f32[4,64,16,375]{3,2,0,1:T(8,128)} %copy.63), calls=%async_computation.1 | async-start | bytes 12582912 | tf_op jit(solution)/shard_map/all_to_all | solution.py:163
  281.4 3.3 copy-start.1
  281.4 3.3 copy-start.9
  281.4 3.3 copy-start.10
  295.9 1.1 copy-start
  312.3 1.1 copy-start
  328.6 1.1 copy-start
  345.0 1.1 copy-start
  361.3 1.1 copy-start
  377.6 1.1 copy-start
  394.0 1.1 copy-start
  410.3 1.1 copy-start
  415.4 30.5 %collective-permute-start.1 = (f32[150,4096]{1,0:T(8,128)}, f32[150,4096]{1,0:T(8,128)}, u32[]{:S(2)}, u32[]{:S(2)}) collective-permute-start(f32[150,4096]{1,0:T(8,128)} %get-tuple-element.204), channel_id=1, source_target_pairs={{1,0},{2,1},{3,2},{4,3},{5,4},{6,5},{7,6},{8,7},{9,8},{10,9},{11,1... | collective-permute-start | bytes 7372808 | tf_op jit(solution)/shard_map/ppermute | solution.py:13
  417.9 33.9 %collective-permute-start = (f32[150,4096]{1,0:T(8,128)}, f32[150,4096]{1,0:T(8,128)S(1)}, u32[]{:S(2)}, u32[]{:S(2)}) collective-permute-start(f32[150,4096]{1,0:T(8,128)} %get-tuple-element.204), channel_id=1, source_target_pairs={{0,1},{1,2},{2,3},{3,4},{4,5},{5,6},{6,7},{7,8},{8,9},{9,10},{10,1... | collective-permute-start | bytes 7372808 | tf_op jit(solution)/shard_map/ppermute | solution.py:13
  598.4 6.4 %copy-start.3 = (f32[4096,25]{1,0:T(8,128)S(1)}, f32[4096,25]{1,0:T(8,128)}, u32[]{:S(2)}) copy-start(f32[4096,25]{1,0:T(8,128)} %gather_fusion.4) | copy-start | bytes 1228804
  598.4 6.4 %copy-start.4 = (f32[4096,25]{1,0:T(8,128)S(1)}, f32[4096,25]{1,0:T(8,128)}, u32[]{:S(2)}) copy-start(f32[4096,25]{1,0:T(8,128)} %gather_fusion.3) | copy-start | bytes 1228804
  604.8 4.4 copy-start.2
  604.8 4.4 copy-start.5
where the time goes:
time: 639 us; the launch traced here: 634 us
  local copies, waits for them, and re-layouts  279 us (44%)
  waiting for transfers between devices  162 us (25%)
  other arithmetic  79.7 us (12%)
  blocking collectives  75.7 us (12%)
  matrix products  19 us (3%)
  starting transfers between devices  16.5 us (3%)
    all_to_all x1, waiting for transfers between devices, body(): lax.all_to_all(lax.all_to_all(outgoing, 'seg', split_axis=0, concat_axis=...  141 us
    gather x6, local copies, waits for them, and re-layouts, body(): fetched.append(jnp.take(pool[opposite], face_link[:, face], axis=1))  102 us
    all_to_all x1, blocking collectives, body(): lax.all_to_all(outgoing, 'seg', split_axis=0, concat_axis=0, tiled=True)  75.7 us
    slice x2, local copies, waits for them, and re-layouts, body(): fetched.append(jnp.take(pool[opposite], face_link[:, face], axis=1))  29.7 us
    ppermute x2, waiting for transfers between devices, shifted(): return lax.ppermute(array, axis, pairs)  21.9 us
    add x8, other arithmetic, geometry(): jac[0][0] * (jac[1][1] * jac[2][2] - jac[1][2] * jac[2][1])  19.4 us
    squeeze x8, local copies, waits for them, and re-layouts, geometry(): deriv[:, first]  19.4 us
    sqrt x24, other arithmetic, geometry(): jnp.sqrt(normal_x * normal_x + normal_y * normal_y + normal_z * normal_z)  18.2 us
  transfers between devices with their start and end apart: 3, of which 3 were waited for; matrix products, arithmetic and copies ran while one was open for 2% of the time, Pallas kernels for 0%

commit v1 on v0

v1 whole, which is shorter than its diff:
```python
import functools
import math

import jax
import jax.numpy as jnp
import numpy as np
from jax import lax
from jax.experimental import pallas as pl
from jax.experimental.pallas import tpu as pltpu
from jax.sharding import PartitionSpec as P

F32 = jnp.float32
BF16 = jnp.bfloat16
GROUPS = 8
FACE_ROWS = 19
FACE_PAD = 24
MASS_ROWS = 16
FACES = GROUPS * FACE_PAD
MASS = GROUPS * MASS_ROWS
CHUNK = 36


def shifted(array, axis, by):
    count = lax.axis_size(axis)
    pairs = [(i, i + by) for i in range(count) if 0 <= i + by < count]
    return lax.ppermute(array, axis, pairs)


def gll_tables():
    points = np.array([-1.0, -math.sqrt(3.0 / 7.0), 0.0, math.sqrt(3.0 / 7.0), 1.0])
    weights = np.array([0.1, 49.0 / 90.0, 32.0 / 45.0, 49.0 / 90.0, 0.1])
    barycentric = np.array(
        [1.0 / np.prod([points[j] - points[m] for m in range(5) if m != j]) for j in range(5)]
    )
    slopes = np.zeros((5, 5))
    for i in range(5):
        for j in range(5):
            if i != j:
                slopes[i, j] = barycentric[j] / barycentric[i] / (points[i] - points[j])
        slopes[i, i] = -np.sum(slopes[i])

    def lagrange_at(where):
        table = np.ones((5, 5))
        for a in range(5):
            for j in range(5):
                for m in range(5):
                    if m != j:
                        table[a, j] *= (where[a] - points[m]) / (points[j] - points[m])
        return table

    def blend(value, side):
        return (1.0 - value) / 2.0 if side == 0 else (1.0 + value) / 2.0

    def flat(i, j, k):
        return i * 25 + j * 5 + k

    ends = (0, 4)
    gordon = np.zeros((125, 125))
    for i in range(5):
        for j in range(5):
            for k in range(5):
                r, s, t = (points[i], points[j], points[k])
                target = flat(i, j, k)
                for a in range(2):
                    gordon[target, flat(ends[a], j, k)] += blend(r, a)
                    gordon[target, flat(i, ends[a], k)] += blend(s, a)
                    gordon[target, flat(i, j, ends[a])] += blend(t, a)
                    for b in range(2):
                        gordon[target, flat(ends[a], ends[b], k)] -= blend(r, a) * blend(s, b)
                        gordon[target, flat(ends[a], j, ends[b])] -= blend(r, a) * blend(t, b)
                        gordon[target, flat(i, ends[a], ends[b])] -= blend(s, a) * blend(t, b)
                        for c in range(2):
                            gordon[target, flat(ends[a], ends[b], ends[c])] += (
                                blend(r, a) * blend(s, b) * blend(t, c)
                            )
    children = np.zeros((8, 125, 125))
    for octant in range(8):
        shifts = [2 * (octant >> 2 & 1) - 1, 2 * (octant >> 1 & 1) - 1, 2 * (octant & 1) - 1]
        tables = [lagrange_at((points + shifts[q]) / 2.0) for q in range(3)]
        children[octant] = np.kron(np.kron(tables[0], tables[1]), tables[2]) @ gordon
    identity = np.eye(5)
    derivs = [
        np.kron(np.kron(slopes, identity), identity),
        np.kron(np.kron(identity, slopes), identity),
        np.kron(np.kron(identity, identity), slopes),
    ]
    deriv_table = np.concatenate([derivs[q].T for q in range(3)], axis=1)
    mass_weights = np.kron(np.kron(weights, weights), weights)
    face_weights = np.kron(weights, weights)
    tangents = [(1, 2), (1, 2), (0, 2), (0, 2), (0, 1), (0, 1)]
    boundary = [
        flat(i, j, k)
        for i in range(5)
        for j in range(5)
        for k in range(5)
        if i in ends or j in ends or k in ends
    ]
    children_map = children.transpose(2, 0, 1).reshape(125, 1000)
    return (children_map, deriv_table, mass_weights, face_weights, tangents, np.array(boundary))


def split(value, parts):
    pieces = []
    for _ in range(parts):
        piece = value.astype(BF16)
        pieces.append(piece)
        value = value - piece.astype(F32)
    return pieces


def flipped(blocks):
    lanes = lax.broadcasted_iota(jnp.int32, blocks[0].shape, 1) // (128 // GROUPS)
    blocks = list(blocks)
    for bit in (1, 2, 4):
        low = (lanes & bit) == 0
        step = bit * (128 // GROUPS)
        for i in range(GROUPS):
            if i & bit == 0:
                a, c = blocks[i], blocks[i | bit]
                blocks[i] = jnp.where(low, a, pltpu.roll(c, step, 1))
                blocks[i | bit] = jnp.where(low, pltpu.roll(a, 128 - step, 1), c)
    return blocks


def face_order():
    return [25 * f + p for f in range(6) for p in range(24)] + [25 * f + 24 for f in range(6)]


def constants():
    children_map, deriv_table, mass_weights, face_weights, tangents, _ = gll_tables()
    child = np.zeros((8, 128, 128))
    child[:, :125, :125] = children_map.reshape(125, 8, 125).transpose(1, 2, 0)
    derivs = deriv_table.reshape(125, 3, 125).transpose(1, 2, 0)
    grid = np.arange(125).reshape(5, 5, 5)
    rows = np.zeros((2 * FACES + 3 * MASS, 128))
    face_scale = np.zeros((FACES, 1))
    for face in range(6):
        nodes = np.take(grid, 0 if face % 2 == 0 else 4, axis=face // 2).reshape(-1)
        for p in range(25):
            n = 24 * face + p if p < 24 else 144 + face
            at = n // FACE_ROWS * FACE_PAD + n % FACE_ROWS
            rows[at, :125] = derivs[tangents[face][0]][nodes[p]]
            rows[FACES + at, :125] = derivs[tangents[face][1]][nodes[p]]
            face_scale[at, 0] = face_weights[p]
    mass_scale = np.zeros((MASS, 1))
    mass_scale[:125, 0] = mass_weights
    for d in range(3):
        start = 2 * FACES + d * MASS
        rows[start : start + 125, :125] = derivs[d]
    as32 = lambda a: jnp.asarray(a, F32)
    return as32(child.reshape(1024, 128)), as32(rows), as32(np.concatenate([face_scale, mass_scale]))


def source_kernel(
    capacity, nodes_ref, marks_ref, owner_ref, child_ref, rows_ref, scale_ref, out_ref,
    pick_ref, x_ref, cc_ref, dd_ref, deriv_ref, vals_ref, natural_ref, target_ref, onehot_ref, y_ref,
):
    elements = nodes_ref.shape[1]
    marked = marks_ref.shape[1]
    kids = 8 * marked
    devices = out_ref.shape[0] // CHUNK * pl.num_programs(0)

    @pl.when(pl.program_id(0) == 0)
    def _():
        pick_ref[...] = jnp.zeros_like(pick_ref)
        marks = marks_ref[...]

        def pick(k, carry):
            start = pl.multiple_of(k * 256, 256)
            where = lax.broadcasted_iota(jnp.int32, (256, marked), 0) + start
            chosen = jnp.where(where == marks, 1.0, 0.0).astype(BF16)
            for piece in split(nodes_ref[:, pl.ds(start, 256)], 3):
                pick_ref[0:375, :] += jnp.dot(piece, chosen, preferred_element_type=F32)
            return carry

        lax.fori_loop(0, elements // 256, pick, 0)
        for c in range(3):
            x = pick_ref[125 * c : 125 * c + 128, :]
            x = x - 0.5 * (x[0:1] + x[124:125])
            a1, a2, a3 = split(x, 3)
            for k, piece in enumerate((a1, a2, a1, a3, a2, a1)):
                x_ref[128 * k : 128 * k + 128, c * marked : (c + 1) * marked] = piece
        c1, c2, c3 = split(child_ref[...], 3)
        for k, piece in enumerate((c1, c1, c2, c1, c2, c3)):
            cc_ref[:, 128 * k : 128 * k + 128] = piece
        d1, d2 = split(rows_ref[...], 2)
        for k, piece in enumerate((d1, d1, d2, d2)):
            dd_ref[:, 128 * k : 128 * k + 128] = piece

        def octant(o, carry):
            coords = jnp.dot(
                cc_ref[pl.ds(pl.multiple_of(o * 128, 128), 128), :], x_ref[...], preferred_element_type=F32
            )
            y1, y2 = split(coords - coords[62:63], 2)
            deriv_ref[...] = jnp.dot(
                dd_ref[...], jnp.concatenate([y1, y2, y1, y2], axis=0), preferred_element_type=F32
            )
            lanes = pl.ds(pl.multiple_of(o * marked, 128), marked)

            def put(row, value):
                v1, v2 = split(value, 2)
                vals_ref[pl.ds(row, 16), lanes] = v1
                vals_ref[pl.ds(FACES + MASS + row, 16), lanes] = v2

            def face_block(i, carry):
                row = pl.multiple_of(i * 16, 16)
                u = [deriv_ref[pl.ds(row, 16), c * marked : (c + 1) * marked] for c in range(3)]
                v = [deriv_ref[pl.ds(FACES + row, 16), c * marked : (c + 1) * marked] for c in range(3)]
                nx = u[1] * v[2] - u[2] * v[1]
                ny = u[2] * v[0] - u[0] * v[2]
                nz = u[0] * v[1] - u[1] * v[0]
                put(row, jnp.sqrt(nx * nx + ny * ny + nz * nz) * scale_ref[pl.ds(row, 16), :])
                return carry

            def mass_block(i, carry):
                row = pl.multiple_of(i * 16, 16)
                j = [
                    [
                        deriv_ref[pl.ds(2 * FACES + d * MASS + row, 16), c * marked : (c + 1) * marked]
                        for d in range(3)
                    ]
                    for c in range(3)
                ]
                determinant = (
                    j[0][0] * (j[1][1] * j[2][2] - j[1][2] * j[2][1])
                    - j[0][1] * (j[1][0] * j[2][2] - j[1][2] * j[2][0])
                    + j[0][2] * (j[1][0] * j[2][1] - j[1][1] * j[2][0])
                )
                put(FACES + row, determinant * scale_ref[pl.ds(FACES + row, 16), :])
                return carry

            lax.fori_loop(0, FACES // 16, face_block, 0)
            lax.fori_loop(0, MASS // 16, mass_block, 0)
            return carry

        lax.fori_loop(0, 8, octant, 0)

        owner_rows = lax.broadcasted_iota(jnp.int32, (devices, 128), 0)
        earlier = lax.broadcasted_iota(jnp.int32, (128, 128), 0) < lax.broadcasted_iota(jnp.int32, (128, 128), 1)
        earlier = jnp.where(earlier, 1.0, 0.0).astype(BF16)
        ones = jnp.ones((128, 128), BF16)

        def slots(b, seen):
            owner = owner_ref[pl.ds(b, 1), :]
            same = owner_rows == owner
            same_b = jnp.where(same, 1.0, 0.0).astype(BF16)
            before = jnp.dot(same_b, earlier, preferred_element_type=F32) + seen
            position = jnp.sum(jnp.where(same, before, 0.0), axis=0, keepdims=True)
            target = owner.astype(F32) * capacity + position
            target = jnp.broadcast_to(target, (128, 128)).T
            natural_ref[pl.ds(pl.multiple_of(b * 128, 128), 128), :] = target.astype(jnp.int32)
            return seen + jnp.dot(same_b, ones, preferred_element_type=F32)

        lax.fori_loop(0, kids // 128, slots, jnp.zeros((devices, 128), F32))
        for o in range(8):
            target_ref[o * marked : (o + 1) * marked, :] = natural_ref[pl.ds(o, marked, stride=8), :]

    columns = lax.broadcasted_iota(jnp.int32, (128, 128), 1) + pl.program_id(0) * 256

    def fill(i, carry):
        rows = pl.ds(pl.multiple_of(i * 128, 128), 128)
        target = target_ref[rows, :]
        onehot_ref[rows, 0:128] = jnp.where(target == columns, 1.0, 0.0).astype(BF16)
        onehot_ref[rows, 128:256] = jnp.where(target == columns + 128, 1.0, 0.0).astype(BF16)
        return carry

    lax.fori_loop(0, kids // 128, fill, 0)
    moved = jnp.dot(vals_ref[...], onehot_ref[...], preferred_element_type=F32)
    y_ref[...] = moved[0 : FACES + MASS] + moved[FACES + MASS :]
    for tile in range(2):
        lanes = slice(128 * tile, 128 * tile + 128)
        faces = flipped([y_ref[FACE_PAD * g : FACE_PAD * (g + 1), lanes] for g in range(GROUPS)])
        masses = flipped(
            [y_ref[FACES + MASS_ROWS * g : FACES + MASS_ROWS * (g + 1), lanes] for g in range(GROUPS)]
        )
        for j in range(GROUPS):
            start = CHUNK * (GROUPS * tile + j)
            out_ref[start : start + MASS_ROWS, :] = masses[j]
            out_ref[start + MASS_ROWS : start + MASS_ROWS + FACE_ROWS, :] = faces[j][0:FACE_ROWS]
            out_ref[start + MASS_ROWS + FACE_ROWS : start + CHUNK, :] = jnp.zeros(
                (CHUNK - MASS_ROWS - FACE_ROWS, 128), F32
            )


def make_outgoing(nodes, marks, owner, devices, capacity):
    marked = marks.shape[1]
    kids = 8 * marked
    child, rows, scale = constants()
    slots = devices * capacity
    whole = lambda a: pl.BlockSpec(a.shape, lambda i: (0, 0))
    operands = (nodes, marks, owner, child, rows, scale)
    height = FACES + MASS
    return pl.pallas_call(
        functools.partial(source_kernel, capacity),
        out_shape=jax.ShapeDtypeStruct((devices * CHUNK, 128), F32),
        grid=(slots // 256,),
        in_specs=[whole(a) for a in operands],
        out_specs=pl.BlockSpec((2 * GROUPS * CHUNK, 128), lambda i: (i, 0)),
        scratch_shapes=[
            pltpu.VMEM((384, marked), F32),
            pltpu.VMEM((768, 3 * marked), BF16),
            pltpu.VMEM((1024, 768), BF16),
            pltpu.VMEM((rows.shape[0], 512), BF16),
            pltpu.VMEM((rows.shape[0], 3 * marked), F32),
            pltpu.VMEM((2 * height, kids), BF16),
            pltpu.VMEM((kids, 128), jnp.int32),
            pltpu.VMEM((kids, 128), jnp.int32),
            pltpu.VMEM((kids, 256), BF16),
            pltpu.VMEM((height, 256), F32),
        ],
        compiler_params=pltpu.CompilerParams(vmem_limit_bytes=48 << 20),
        name="source",
    )(*operands)


def unpack_kernel(in_ref, mass_ref, faces_ref):
    for tile in range(2):
        lanes = slice(128 * tile, 128 * tile + 128)
        starts = [CHUNK * (GROUPS * tile + j) for j in range(GROUPS)]
        masses = flipped([in_ref[s : s + MASS_ROWS, :] for s in starts])
        for g in range(GROUPS):
            count = min(MASS_ROWS, 125 - MASS_ROWS * g)
            mass_ref[MASS_ROWS * g : MASS_ROWS * g + count, lanes] = masses[g][0:count]
        faces = flipped([in_ref[s + MASS_ROWS : s + MASS_ROWS + FACE_ROWS, :] for s in starts])
        for g in range(GROUPS):
            count = min(FACE_ROWS, 150 - FACE_ROWS * g)
            faces_ref[FACE_ROWS * g : FACE_ROWS * g + count, lanes] = faces[g][0:count]


def unpack(arrived, slots):
    return pl.pallas_call(
        unpack_kernel,
        out_shape=(jax.ShapeDtypeStruct((125, slots), F32), jax.ShapeDtypeStruct((150, slots), F32)),
        grid=(slots // 256,),
        in_specs=[pl.BlockSpec((2 * GROUPS * CHUNK, 128), lambda i: (i, 0))],
        out_specs=(pl.BlockSpec((125, 256), lambda i: (0, i)), pl.BlockSpec((150, 256), lambda i: (0, i))),
        name="unpack",
    )(arrived)


def collect_kernel(link_ref, before_ref, faces_ref, after_ref, out_ref, table_ref, tail_ref):
    sources = (before_ref, faces_ref, after_ref)
    per_source = faces_ref.shape[1] // 256
    tiles = 3 * per_source
    body_rows = 24 * tiles

    @pl.when(pl.program_id(0) == 0)
    def _():
        for f in range(6):
            other = f + 1 - 2 * (f % 2)
            for k, source in enumerate(sources):

                def pair(i, carry):
                    lanes = [pl.ds(pl.multiple_of(512 * i + 256 * e, 256), 256) for e in range(2)]
                    values = jnp.concatenate([source[24 * other : 24 * other + 24, l] for l in lanes], axis=0)
                    row = pl.multiple_of(24 * per_source * k + 48 * i, 16)
                    for part, piece in enumerate(split(values, 2)):
                        table_ref[f, pl.ds(row, 48), 256 * part : 256 * part + 256] = piece
                    for e in range(2):
                        tail_ref[pl.ds(per_source * k + 2 * i + e, 1), :] = source[
                            144 + other : 145 + other, lanes[e]
                        ]
                    return carry

                lax.fori_loop(0, per_source // 2, pair, 0)
            for part, piece in enumerate(split(tail_ref[...], 2)):
                table_ref[f, body_rows : body_rows + tiles, 256 * part : 256 * part + 256] = piece

    here = pl.ds(pl.multiple_of(pl.program_id(0) * 256, 256), 256)
    for f in range(6):
        link = link_ref[f : f + 1, here]
        low, high = link & 255, link >> 8
        chosen = jnp.where(lax.broadcasted_iota(jnp.int32, (256, 256), 0) == low, 1.0, 0.0).astype(BF16)
        found = jnp.dot(table_ref[f], jnp.concatenate([chosen, chosen], axis=0), preferred_element_type=F32)
        high24 = jnp.broadcast_to(high, (24, 256))
        picked = jnp.zeros((24, 256), F32)
        for h in range(tiles):
            picked = jnp.where(high24 == h, found[24 * h : 24 * h + 24], picked)
        last = jnp.where(lax.broadcasted_iota(jnp.int32, (tiles, 256), 0) == high, found[body_rows:], 0.0)
        out_ref[25 * f : 25 * f + 24, :] = faces_ref[24 * f : 24 * f + 24, here] + picked
        out_ref[25 * f + 24 : 25 * f + 25, :] = faces_ref[144 + f : 145 + f, here] + jnp.sum(
            last, axis=0, keepdims=True
        )


def collect(before, faces, after, links):
    slots = faces.shape[1]
    tiles = 3 * slots // 256
    whole = lambda a: pl.BlockSpec(a.shape, lambda i: (0, 0))
    operands = (links, before, faces, after)
    return pl.pallas_call(
        collect_kernel,
        out_shape=jax.ShapeDtypeStruct((150, slots), F32),
        grid=(slots // 256,),
        in_specs=[whole(a) for a in operands],
        out_specs=pl.BlockSpec((150, 256), lambda i: (0, i)),
        scratch_shapes=[pltpu.VMEM((6, 25 * tiles, 512), BF16), pltpu.VMEM((tiles, 256), F32)],
        compiler_params=pltpu.CompilerParams(vmem_limit_bytes=48 << 20),
        name="collect",
    )(*operands)


def body(parent_nodes, marks, child_owner, face_link):
    devices = lax.axis_size("seg") * lax.axis_size("rank")
    kids = child_owner.shape[0]
    capacity = max(2, 2 * kids // devices)
    slots = devices * capacity
    outgoing = make_outgoing(parent_nodes.T, marks, child_owner.reshape(kids // 128, 128), devices, capacity)
    arrived = lax.all_to_all(
        outgoing.reshape(devices, CHUNK // 2, 2, 128), ("seg", "rank"), split_axis=0, concat_axis=0, tiled=True
    ).reshape(devices * CHUNK, 128)
    mass, faces = unpack(arrived, slots)
    before = shifted(faces, "rank", 1)
    after = shifted(faces, "rank", -1)
    return (mass, collect(before, faces, after, face_link.T))


def solution(mesh):
    return jax.shard_map(
        body,
        mesh=mesh,
        in_specs=(P(("seg", "rank"), None),) * 4,
        out_specs=(P(None, ("seg", "rank")), P(None, ("seg", "rank"))),
        check_vma=False,
    )
```

time: 639 us -> 273 us (0.43)
  local copies, waits for them, and re-layouts: 279 us -> 8.12 us
  waiting for transfers between devices: 162 us -> 31.6 us
  Pallas kernels: 0 us -> 104 us
  other arithmetic: 79.7 us -> 0 us
  blocking collectives: 75.7 us -> 123 us
  matrix products: 19 us -> 0 us
  starting transfers between devices: 16.5 us -> 4.31 us
    all_to_all x1 -> x0, waiting for transfers between devices: 141 us -> none  [body(): lax.all_to_all(lax.all_to_all(outgoing, 'seg', split_axis=0, concat_axis=...]
    gather x7 -> x0, local copies, waits for them, and re-layouts: 105 us -> none  [the longest x6 102 us: body(): fetched.append(jnp.take(pool[opposite], face_link[:, face], axis=1))]
    pallas_call x0 -> x3, Pallas kernels: none -> 104 us  [the longest x1 52.2 us: make_outgoing(): pl.pallas_call(functools.partial(source_kernel, capacity), out_shape=jax....]
    all_to_all x1, blocking collectives: 75.7 us -> 123 us  [body(): lax.all_to_all(outgoing.reshape(devices, CHUNK // 2, 2, 128), ('seg', 'ra...]
    slice x2 -> x0, local copies, waits for them, and re-layouts: 29.7 us -> none  [body(): fetched.append(jnp.take(pool[opposite], face_link[:, face], axis=1))]
    add x9 -> x0, other arithmetic: 25.5 us -> none  [the longest x8 19.4 us: geometry(): jac[0][0] * (jac[1][1] * jac[2][2] - jac[1][2] * jac[2][1])]
    reshape x17 -> x0, local copies, waits for them, and re-layouts: 23.2 us -> none  [the longest x8 17.9 us: geometry(): deriv = deriv.reshape(3, 3, 5, 5, 5, width)]
    squeeze x8 -> x0, local copies, waits for them, and re-layouts: 19.4 us -> none  [geometry(): deriv[:, first]]
  transfers between devices with their start and end apart: 3 -> 2, of which waited for: 3 -> 2; matrix products, arithmetic and copies ran while one was open for 2% -> 0% of each run, Pallas kernels for 0% -> 0%
where the time goes in v1:
time: 273 us; the launch traced here: 272 us
  blocking collectives  123 us (45%)
  Pallas kernels  104 us (38%)
  waiting for transfers between devices  31.6 us (12%)
  local copies, waits for them, and re-layouts  8.12 us (3%)
  starting transfers between devices  4.31 us (2%)
    all_to_all x1, blocking collectives, body(): lax.all_to_all(outgoing.reshape(devices, CHUNK // 2, 2, 128), ('seg', 'ra...  123 us
    pallas_call x1, Pallas kernels, make_outgoing(): pl.pallas_call(functools.partial(source_kernel, capacity), out_shape=jax....  52.2 us
    pallas_call x1, Pallas kernels, collect(): pl.pallas_call(collect_kernel, out_shape=jax.ShapeDtypeStruct((150, slots...  38.4 us
    ppermute x2, waiting for transfers between devices, shifted(): return lax.ppermute(array, axis, pairs)  31.6 us
    pallas_call x1, Pallas kernels, unpack(): pl.pallas_call(unpack_kernel, out_shape=(jax.ShapeDtypeStruct((125, slots...  13.7 us
    unnamed x18, local copies, waits for them, and re-layouts  8.12 us
  transfers between devices with their start and end apart: 2, of which 2 were waited for; matrix products, arithmetic and copies ran while one was open for 0% of the time, Pallas kernels for 0%

profile of v1, /device:TPU:32, one launch (start us, length us, event | category | flops | bytes accessed | tf_op | source)
XLA Modules:
  0.0 272.1 jit_solution(16008782958532381147)
XLA Ops:
  0.6 0.0 copy-start
  0.6 2.1 copy-done
  2.7 0.0 copy-start.2
  2.7 1.0 copy-done.2
  3.8 0.0 copy-start.3
  3.8 1.0 copy-done.3
  4.8 0.0 copy-start.4
  4.8 0.9 copy-done.4
  5.7 0.0 copy-start.6
  5.7 0.7 copy-done.6
  6.4 0.0 copy-start.7
  6.4 0.7 copy-done.7
  7.1 52.2 %source.1 = f32[9216,128]{1,0:T(8,128)} custom-call(f32[375,2560]{1,0:T(8,128)S(1)} %bitcast.5, s32[1,256]{1,0:T(1,128)S(1)} %copy-done.7, s32[16,128]{1,0:T(8,128)S(1)} %bitcast.7, f32[1024,128]{1,0:T(8,128)S(1)} %copy-done.2, f32[768,128]{1,0:T(8,128)S(1)} %copy-done.3, f32[320,1]{1,0:T(8,128)S(1)} %copy-done.4), custom_call_target="tpu_custom_call" | custom-call | tf_op jit(solution)/shard_map/source/pallas_call | solution.py:293
  59.3 123.0 %all_to_all.5 = f32[256,18,2,128]{3,2,1,0:T(2,128)} all-to-all(f32[256,18,2,128]{3,2,1,0:T(2,128)} %bitcast.8), channel_id=1, replica_groups=mesh['seg'=4,'rank'=64] {'seg','rank'}, dimensions={0} | all-to-all | bytes 9437184 | tf_op jit(solution)/shard_map/all_to_all | solution.py:409
  182.3 0.0 copy-start.5
  182.3 13.7 %unpack.1 = (f32[125,4096]{1,0:T(8,128)}, f32[150,4096]{1,0:T(8,128)}) custom-call(f32[9216,128]{1,0:T(8,128)} %bitcast.9), custom_call_target="tpu_custom_call" | custom-call | tf_op jit(solution)/shard_map/unpack/pallas_call | solution.py:331
  196.0 2.0 collective-permute-start.1
  198.1 2.3 collective-permute-start
  200.4 25.7 %collective-permute-done.1.after_ref = f32[150,4096]{1,0:T(8,128)S(1)} collective-permute-done((f32[150,4096]{1,0:T(8,128)}, f32[150,4096]{1,0:T(8,128)S(1)}, u32[]{:S(2)}, u32[]{:S(2)}) %collective-permute-start.1) | collective-permute-done | bytes 2457632 | tf_op jit(solution)/shard_map/ppermute | solution.py:26
  226.1 0.0 copy-start.8
  226.1 5.8 %collective-permute-done.before_ref = f32[150,4096]{1,0:T(8,128)S(1)} collective-permute-done((f32[150,4096]{1,0:T(8,128)}, f32[150,4096]{1,0:T(8,128)S(1)}, u32[]{:S(2)}, u32[]{:S(2)}) %collective-permute-start) | collective-permute-done | bytes 2457632 | tf_op jit(solution)/shard_map/ppermute | solution.py:26
  231.9 0.0 copy-done.8
  231.9 0.0 copy-done.5
  232.0 0.0 copy-start.1
  232.0 1.7 copy-done.1
  233.7 38.4 %collect.1 = f32[150,4096]{1,0:T(8,128)} custom-call(s32[6,4096]{1,0:T(8,128)S(1)} %bitcast.6, f32[150,4096]{1,0:T(8,128)S(1)} %collective-permute-done.before_ref, f32[150,4096]{1,0:T(8,128)S(1)} %copy-done.1, f32[150,4096]{1,0:T(8,128)} %copy-done.8), custom_call_target="tpu_custom_call" | custom-call | tf_op jit(solution)/shard_map/collect/pallas_call | solution.py:391
Async XLA Ops:
  0.6 2.1 copy-start
  2.7 1.0 copy-start.2
  3.8 1.0 copy-start.3
  4.8 0.9 copy-start.4
  5.7 0.7 copy-start.6
  6.4 0.7 copy-start.7
  182.3 49.7 %copy-start.5 = (s32[4096,6]{0,1:T(8,128)S(1)}, s32[4096,6]{0,1:T(8,128)}, u32[]{:S(2)}) copy-start(s32[4096,6]{0,1:T(8,128)} %param.10) | copy-start | bytes 294916
  196.0 30.1 %collective-permute-start.1 = (f32[150,4096]{1,0:T(8,128)}, f32[150,4096]{1,0:T(8,128)S(1)}, u32[]{:S(2)}, u32[]{:S(2)}) collective-permute-start(f32[150,4096]{1,0:T(8,128)} %get-tuple-element.5.faces_ref), channel_id=1, source_target_pairs={{1,0},{2,1},{3,2},{4,3},{5,4},{6,5},{7,6},{8,7},{9,8},{10,9},{11,1... | collective-permute-start | bytes 7372808 | tf_op jit(solution)/shard_map/ppermute | solution.py:26
  198.1 33.9 %collective-permute-start = (f32[150,4096]{1,0:T(8,128)}, f32[150,4096]{1,0:T(8,128)S(1)}, u32[]{:S(2)}, u32[]{:S(2)}) collective-permute-start(f32[150,4096]{1,0:T(8,128)} %get-tuple-element.5.faces_ref), channel_id=1, source_target_pairs={{0,1},{1,2},{2,3},{3,4},{4,5},{5,6},{6,7},{7,8},{8,9},{9,10},{10,1... | collective-permute-start | bytes 7372808 | tf_op jit(solution)/shard_map/ppermute | solution.py:26
  226.1 5.8 %copy-start.8 = (f32[150,4096]{1,0:T(8,128)}, f32[150,4096]{1,0:T(8,128)S(1)}, u32[]{:S(2)}) copy-start(f32[150,4096]{1,0:T(8,128)S(1)} %collective-permute-done.1.after_ref) | copy-start | bytes 7372804
  232.0 1.7 copy-start.1

commit v2 on v1

--- a/solution.py
+++ b/solution.py
@@ -13,11 +13,10 @@
 BF16 = jnp.bfloat16
 GROUPS = 8
 FACE_ROWS = 19
-FACE_PAD = 24
+FACES = GROUPS * FACE_ROWS
+FACE_CHUNK = 20
 MASS_ROWS = 16
-FACES = GROUPS * FACE_PAD
 MASS = GROUPS * MASS_ROWS
-CHUNK = 36
 
 
 def shifted(array, axis, by):
@@ -132,33 +131,78 @@
     child[:, :125, :125] = children_map.reshape(125, 8, 125).transpose(1, 2, 0)
     derivs = deriv_table.reshape(125, 3, 125).transpose(1, 2, 0)
     grid = np.arange(125).reshape(5, 5, 5)
-    rows = np.zeros((2 * FACES + 3 * MASS, 128))
+    face_rows = np.zeros((2 * FACES, 128))
     face_scale = np.zeros((FACES, 1))
     for face in range(6):
         nodes = np.take(grid, 0 if face % 2 == 0 else 4, axis=face // 2).reshape(-1)
         for p in range(25):
             n = 24 * face + p if p < 24 else 144 + face
-            at = n // FACE_ROWS * FACE_PAD + n % FACE_ROWS
-            rows[at, :125] = derivs[tangents[face][0]][nodes[p]]
-            rows[FACES + at, :125] = derivs[tangents[face][1]][nodes[p]]
-            face_scale[at, 0] = face_weights[p]
+            face_rows[n, :125] = derivs[tangents[face][0]][nodes[p]]
+            face_rows[FACES + n, :125] = derivs[tangents[face][1]][nodes[p]]
+            face_scale[n, 0] = face_weights[p]
+    mass_rows = np.zeros((3 * MASS, 128))
     mass_scale = np.zeros((MASS, 1))
     mass_scale[:125, 0] = mass_weights
     for d in range(3):
-        start = 2 * FACES + d * MASS
-        rows[start : start + 125, :125] = derivs[d]
-    as32 = lambda a: jnp.asarray(a, F32)
-    return as32(child.reshape(1024, 128)), as32(rows), as32(np.concatenate([face_scale, mass_scale]))
-
-
-def source_kernel(
-    capacity, nodes_ref, marks_ref, owner_ref, child_ref, rows_ref, scale_ref, out_ref,
-    pick_ref, x_ref, cc_ref, dd_ref, deriv_ref, vals_ref, natural_ref, target_ref, onehot_ref, y_ref,
+        mass_rows[d * MASS : d * MASS + 125, :125] = derivs[d]
+    arrays = (child.reshape(1024, 128), face_rows, face_scale, mass_rows, mass_scale)
+    return [jnp.asarray(a, F32) for a in arrays]
+
+
+def fill_table(dd_ref, rows_ref):
+    d1, d2 = split(rows_ref[...], 2)
+    for k, piece in enumerate((d1, d1, d2, d2)):
+        dd_ref[:, 128 * k : 128 * k + 128] = piece
+
+
+def slopes_of(dd_ref, deriv_ref, coords):
+    deriv_ref[...] = jnp.dot(
+        dd_ref[...], jnp.concatenate([coords, coords], axis=0), preferred_element_type=F32
+    )
+
+
+def put(vals_ref, row, lanes, value):
+    v1, v2 = split(value, 2)
+    vals_ref[pl.ds(row, 8 * (value.shape[0] // 8)), lanes] = v1
+    vals_ref[pl.ds(vals_ref.shape[0] // 2 + row, 8 * (value.shape[0] // 8)), lanes] = v2
+
+
+def scattered(vals_ref, target_ref, onehot_ref, y_ref):
+    kids = target_ref.shape[0]
+    columns = lax.broadcasted_iota(jnp.int32, (128, 128), 1) + pl.program_id(0) * 256
+
+    def fill(i, carry):
+        rows = pl.ds(pl.multiple_of(i * 128, 128), 128)
+        target = target_ref[rows, :]
+        onehot_ref[rows, 0:128] = jnp.where(target == columns, 1.0, 0.0).astype(BF16)
+        onehot_ref[rows, 128:256] = jnp.where(target == columns + 128, 1.0, 0.0).astype(BF16)
+        return carry
+
+    lax.fori_loop(0, kids // 128, fill, 0, unroll=True)
+    moved = jnp.dot(vals_ref[...], onehot_ref[...], preferred_element_type=F32)
+    height = y_ref.shape[0]
+    y_ref[...] = moved[0:height] + moved[height:]
+
+
+def send(y_ref, out_ref, rows, chunk):
+    for tile in range(2):
+        lanes = slice(128 * tile, 128 * tile + 128)
+        blocks = flipped([y_ref[rows * g : rows * (g + 1), lanes] for g in range(GROUPS)])
+        for j in range(GROUPS):
+            start = chunk * (GROUPS * tile + j)
+            out_ref[start : start + rows, :] = blocks[j]
+            if chunk > rows:
+                out_ref[start + rows : start + chunk, :] = jnp.zeros((chunk - rows, 128), F32)
+
+
+def face_kernel(
+    capacity, nodes_ref, marks_ref, owner_ref, child_ref, rows_ref, scale_ref, out_ref, coords_ref, target_ref,
+    pick_ref, x_ref, cc_ref, dd_ref, deriv_ref, vals_ref, natural_ref, onehot_ref, y_ref,
 ):
     elements = nodes_ref.shape[1]
     marked = marks_ref.shape[1]
     kids = 8 * marked
-    devices = out_ref.shape[0] // CHUNK * pl.num_programs(0)
+    devices = out_ref.shape[0] // FACE_CHUNK * pl.num_programs(0)
 
     @pl.when(pl.program_id(0) == 0)
     def _():
@@ -183,54 +227,27 @@
         c1, c2, c3 = split(child_ref[...], 3)
         for k, piece in enumerate((c1, c1, c2, c1, c2, c3)):
             cc_ref[:, 128 * k : 128 * k + 128] = piece
-        d1, d2 = split(rows_ref[...], 2)
-        for k, piece in enumerate((d1, d1, d2, d2)):
-            dd_ref[:, 128 * k : 128 * k + 128] = piece
+        fill_table(dd_ref, rows_ref)
 
         def octant(o, carry):
             coords = jnp.dot(
                 cc_ref[pl.ds(pl.multiple_of(o * 128, 128), 128), :], x_ref[...], preferred_element_type=F32
             )
-            y1, y2 = split(coords - coords[62:63], 2)
-            deriv_ref[...] = jnp.dot(
-                dd_ref[...], jnp.concatenate([y1, y2, y1, y2], axis=0), preferred_element_type=F32
-            )
+            both = jnp.concatenate(split(coords - coords[62:63], 2), axis=0)
+            coords_ref[pl.ds(pl.multiple_of(o * 256, 256), 256), :] = both
+            slopes_of(dd_ref, deriv_ref, both)
             lanes = pl.ds(pl.multiple_of(o * marked, 128), marked)
 
-            def put(row, value):
-                v1, v2 = split(value, 2)
-                vals_ref[pl.ds(row, 16), lanes] = v1
-                vals_ref[pl.ds(FACES + MASS + row, 16), lanes] = v2
-
-            def face_block(i, carry):
-                row = pl.multiple_of(i * 16, 16)
-                u = [deriv_ref[pl.ds(row, 16), c * marked : (c + 1) * marked] for c in range(3)]
-                v = [deriv_ref[pl.ds(FACES + row, 16), c * marked : (c + 1) * marked] for c in range(3)]
+            def face_block(row, rows):
+                u = [deriv_ref[pl.ds(row, rows), c * marked : (c + 1) * marked] for c in range(3)]
+                v = [deriv_ref[pl.ds(FACES + row, rows), c * marked : (c + 1) * marked] for c in range(3)]
                 nx = u[1] * v[2] - u[2] * v[1]
                 ny = u[2] * v[0] - u[0] * v[2]
                 nz = u[0] * v[1] - u[1] * v[0]
-                put(row, jnp.sqrt(nx * nx + ny * ny + nz * nz) * scale_ref[pl.ds(row, 16), :])
-                return carry
-
-            def mass_block(i, carry):
-                row = pl.multiple_of(i * 16, 16)
-                j = [
-                    [
-                        deriv_ref[pl.ds(2 * FACES + d * MASS + row, 16), c * marked : (c + 1) * marked]
-                        for d in range(3)
-                    ]
-                    for c in range(3)
-                ]
-                determinant = (
-                    j[0][0] * (j[1][1] * j[2][2] - j[1][2] * j[2][1])
-                    - j[0][1] * (j[1][0] * j[2][2] - j[1][2] * j[2][0])
-                    + j[0][2] * (j[1][0] * j[2][1] - j[1][1] * j[2][0])
-                )
-                put(FACES + row, determinant * scale_ref[pl.ds(FACES + row, 16), :])
-                return carry
-
-            lax.fori_loop(0, FACES // 16, face_block, 0)
-            lax.fori_loop(0, MASS // 16, mass_block, 0)
+                put(vals_ref, row, lanes, jnp.sqrt(nx * nx + ny * ny + nz * nz) * scale_ref[pl.ds(row, rows), :])
+
+            for row in range(0, FACES, 8):
+                face_block(row, 8)
             return carry
 
         lax.fori_loop(0, 8, octant, 0)
@@ -255,86 +272,112 @@
         for o in range(8):
             target_ref[o * marked : (o + 1) * marked, :] = natural_ref[pl.ds(o, marked, stride=8), :]
 
-    columns = lax.broadcasted_iota(jnp.int32, (128, 128), 1) + pl.program_id(0) * 256
-
-    def fill(i, carry):
-        rows = pl.ds(pl.multiple_of(i * 128, 128), 128)
-        target = target_ref[rows, :]
-        onehot_ref[rows, 0:128] = jnp.where(target == columns, 1.0, 0.0).astype(BF16)
-        onehot_ref[rows, 128:256] = jnp.where(target == columns + 128, 1.0, 0.0).astype(BF16)
-        return carry
-
-    lax.fori_loop(0, kids // 128, fill, 0)
-    moved = jnp.dot(vals_ref[...], onehot_ref[...], preferred_element_type=F32)
-    y_ref[...] = moved[0 : FACES + MASS] + moved[FACES + MASS :]
-    for tile in range(2):
-        lanes = slice(128 * tile, 128 * tile + 128)
-        faces = flipped([y_ref[FACE_PAD * g : FACE_PAD * (g + 1), lanes] for g in range(GROUPS)])
-        masses = flipped(
-            [y_ref[FACES + MASS_ROWS * g : FACES + MASS_ROWS * (g + 1), lanes] for g in range(GROUPS)]
-        )
-        for j in range(GROUPS):
-            start = CHUNK * (GROUPS * tile + j)
-            out_ref[start : start + MASS_ROWS, :] = masses[j]
-            out_ref[start + MASS_ROWS : start + MASS_ROWS + FACE_ROWS, :] = faces[j][0:FACE_ROWS]
-            out_ref[start + MASS_ROWS + FACE_ROWS : start + CHUNK, :] = jnp.zeros(
-                (CHUNK - MASS_ROWS - FACE_ROWS, 128), F32
-            )
+    scattered(vals_ref, target_ref, onehot_ref, y_ref)
+    send(y_ref, out_ref, FACE_ROWS, FACE_CHUNK)
+
+
+def mass_kernel(coords_ref, target_ref, rows_ref, scale_ref, out_ref, dd_ref, deriv_ref, vals_ref, onehot_ref, y_ref):
+    marked = coords_ref.shape[1] // 3
+
+    @pl.when(pl.program_id(0) == 0)
+    def _():
+        fill_table(dd_ref, rows_ref)
+
+        def octant(o, carry):
+            slopes_of(dd_ref, deriv_ref, coords_ref[pl.ds(pl.multiple_of(o * 256, 256), 256), :])
+            lanes = pl.ds(pl.multiple_of(o * marked, 128), marked)
+            for row in range(0, MASS, 8):
+                j = [
+                    [deriv_ref[d * MASS + row : d * MASS + row + 8, c * marked : (c + 1) * marked] for d in range(3)]
+                    for c in range(3)
+                ]
+                determinant = (
+                    j[0][0] * (j[1][1] * j[2][2] - j[1][2] * j[2][1])
+                    - j[0][1] * (j[1][0] * j[2][2] - j[1][2] * j[2][0])
+                    + j[0][2] * (j[1][0] * j[2][1] - j[1][1] * j[2][0])
+                )
+                put(vals_ref, row, lanes, determinant * scale_ref[row : row + 8, :])
+            return carry
+
+        lax.fori_loop(0, 8, octant, 0)
+
+    scattered(vals_ref, target_ref, onehot_ref, y_ref)
+    send(y_ref, out_ref, MASS_ROWS, MASS_ROWS)
+
+
+def whole(a):
+    return pl.BlockSpec(a.shape, lambda i: (0, 0))
 
 
 def make_outgoing(nodes, marks, owner, devices, capacity):
     marked = marks.shape[1]
     kids = 8 * marked
-    child, rows, scale = constants()
-    slots = devices * capacity
-    whole = lambda a: pl.BlockSpec(a.shape, lambda i: (0, 0))
-    operands = (nodes, marks, owner, child, rows, scale)
-    height = FACES + MASS
-    return pl.pallas_call(
-        functools.partial(source_kernel, capacity),
-        out_shape=jax.ShapeDtypeStruct((devices * CHUNK, 128), F32),
-        grid=(slots // 256,),
+    child, face_rows, face_scale, mass_rows, mass_scale = constants()
+    steps = devices * capacity // 256
+    operands = (nodes, marks, owner, child, face_rows, face_scale)
+    shapes = (
+        jax.ShapeDtypeStruct((devices * FACE_CHUNK, 128), F32),
+        jax.ShapeDtypeStruct((2048, 3 * marked), BF16),
+        jax.ShapeDtypeStruct((kids, 128), jnp.int32),
+    )
+    faces, coords, target = pl.pallas_call(
+        functools.partial(face_kernel, capacity),
+        out_shape=shapes,
+        grid=(steps,),
         in_specs=[whole(a) for a in operands],
-        out_specs=pl.BlockSpec((2 * GROUPS * CHUNK, 128), lambda i: (i, 0)),
+        out_specs=(pl.BlockSpec((2 * GROUPS * FACE_CHUNK, 128), lambda i: (i, 0)), whole(shapes[1]), whole(shapes[2])),
         scratch_shapes=[
             pltpu.VMEM((384, marked), F32),
             pltpu.VMEM((768, 3 * marked), BF16),
             pltpu.VMEM((1024, 768), BF16),
-            pltpu.VMEM((rows.shape[0], 512), BF16),
-            pltpu.VMEM((rows.shape[0], 3 * marked), F32),
-            pltpu.VMEM((2 * height, kids), BF16),
-            pltpu.VMEM((kids, 128), jnp.int32),
+            pltpu.VMEM((2 * FACES, 512), BF16),
+            pltpu.VMEM((2 * FACES, 3 * marked), F32),
+            pltpu.VMEM((2 * FACES, kids), BF16),
             pltpu.VMEM((kids, 128), jnp.int32),
             pltpu.VMEM((kids, 256), BF16),
-            pltpu.VMEM((height, 256), F32),
+            pltpu.VMEM((FACES, 256), F32),
         ],
-        compiler_params=pltpu.CompilerParams(vmem_limit_bytes=48 << 20),
-        name="source",
+        compiler_params=pltpu.CompilerParams(vmem_limit_bytes=40 << 20),
+        name="faces",
     )(*operands)
-
-
-def unpack_kernel(in_ref, mass_ref, faces_ref):
+    operands = (coords, target, mass_rows, mass_scale)
+    masses = pl.pallas_call(
+        mass_kernel,
+        out_shape=jax.ShapeDtypeStruct((devices * MASS_ROWS, 128), F32),
+        grid=(steps,),
+        in_specs=[whole(a) for a in operands],
+        out_specs=pl.BlockSpec((2 * GROUPS * MASS_ROWS, 128), lambda i: (i, 0)),
+        scratch_shapes=[
+            pltpu.VMEM((3 * MASS, 512), BF16),
+            pltpu.VMEM((3 * MASS, 3 * marked), F32),
+            pltpu.VMEM((2 * MASS, kids), BF16),
+            pltpu.VMEM((kids, 256), BF16),
+            pltpu.VMEM((MASS, 256), F32),
+        ],
+        compiler_params=pltpu.CompilerParams(vmem_limit_bytes=32 << 20),
+        name="masses",
+    )(*operands)
+    return faces, masses
+
+
+def unpack_kernel(rows, chunk, height, in_ref, out_ref):
     for tile in range(2):
         lanes = slice(128 * tile, 128 * tile + 128)
-        starts = [CHUNK * (GROUPS * tile + j) for j in range(GROUPS)]
-        masses = flipped([in_ref[s : s + MASS_ROWS, :] for s in starts])
+        starts = [chunk * (GROUPS * tile + j) for j in range(GROUPS)]
+        blocks = flipped([in_ref[s : s + rows, :] for s in starts])
         for g in range(GROUPS):
-            count = min(MASS_ROWS, 125 - MASS_ROWS * g)
-            mass_ref[MASS_ROWS * g : MASS_ROWS * g + count, lanes] = masses[g][0:count]
-        faces = flipped([in_ref[s + MASS_ROWS : s + MASS_ROWS + FACE_ROWS, :] for s in starts])
-        for g in range(GROUPS):
-            count = min(FACE_ROWS, 150 - FACE_ROWS * g)
-            faces_ref[FACE_ROWS * g : FACE_ROWS * g + count, lanes] = faces[g][0:count]
-
-
-def unpack(arrived, slots):
+            count = min(rows, height - rows * g)
+            out_ref[rows * g : rows * g + count, lanes] = blocks[g][0:count]
+
+
+def unpack(arrived, slots, rows, chunk, height, name):
     return pl.pallas_call(
-        unpack_kernel,
-        out_shape=(jax.ShapeDtypeStruct((125, slots), F32), jax.ShapeDtypeStruct((150, slots), F32)),
+        functools.partial(unpack_kernel, rows, chunk, height),
+        out_shape=jax.ShapeDtypeStruct((height, slots), F32),
         grid=(slots // 256,),
-        in_specs=[pl.BlockSpec((2 * GROUPS * CHUNK, 128), lambda i: (i, 0))],
-        out_specs=(pl.BlockSpec((125, 256), lambda i: (0, i)), pl.BlockSpec((150, 256), lambda i: (0, i))),
-        name="unpack",
+        in_specs=[pl.BlockSpec((2 * GROUPS * chunk, 128), lambda i: (i, 0))],
+        out_specs=pl.BlockSpec((height, 256), lambda i: (0, i)),
+        name=name,
     )(arrived)
 
 
@@ -386,7 +429,6 @@
 def collect(before, faces, after, links):
     slots = faces.shape[1]
     tiles = 3 * slots // 256
-    whole = lambda a: pl.BlockSpec(a.shape, lambda i: (0, 0))
     operands = (links, before, faces, after)
     return pl.pallas_call(
         collect_kernel,
@@ -400,19 +442,24 @@
     )(*operands)
 
 
+def exchanged(rows, devices, tile):
+    blocks = rows.reshape(devices, rows.shape[0] // devices // tile, tile, 128)
+    return lax.all_to_all(blocks, ("seg", "rank"), split_axis=0, concat_axis=0, tiled=True).reshape(rows.shape)
+
+
 def body(parent_nodes, marks, child_owner, face_link):
     devices = lax.axis_size("seg") * lax.axis_size("rank")
     kids = child_owner.shape[0]
     capacity = max(2, 2 * kids // devices)
     slots = devices * capacity
-    outgoing = make_outgoing(parent_nodes.T, marks, child_owner.reshape(kids // 128, 128), devices, capacity)
-    arrived = lax.all_to_all(
-        outgoing.reshape(devices, CHUNK // 2, 2, 128), ("seg", "rank"), split_axis=0, concat_axis=0, tiled=True
-    ).reshape(devices * CHUNK, 128)
-    mass, faces = unpack(arrived, slots)
+    faces, masses = make_outgoing(parent_nodes.T, marks, child_owner.reshape(kids // 128, 128), devices, capacity)
+    faces = unpack(exchanged(faces, devices, 4), slots, FACE_ROWS, FACE_CHUNK, 150, "unpack_faces")
+    masses = exchanged(masses, devices, 8)
     before = shifted(faces, "rank", 1)
     after = shifted(faces, "rank", -1)
-    return (mass, collect(before, faces, after, face_link.T))
+    face_mass = collect(before, faces, after, face_link.T)
+    masses, face_mass = lax.optimization_barrier((masses, face_mass))
+    return (unpack(masses, slots, MASS_ROWS, MASS_ROWS, 125, "unpack_masses"), face_mass)
 
 
 def solution(mesh):

time: 273 us -> 252 us (0.923)
  blocking collectives: 123 us -> 0 us
  waiting for transfers between devices: 31.6 us -> 101 us
  starting transfers between devices: 4.31 us -> 28.2 us
  local copies, waits for them, and re-layouts: 8.12 us -> 13.1 us
  Pallas kernels: 104 us -> 107 us
    all_to_all x1 -> x0, blocking collectives: 123 us -> none  [body(): lax.all_to_all(outgoing.reshape(devices, CHUNK // 2, 2, 128), ('seg', 'ra...]
    all_to_all x0 -> x2, waiting for transfers between devices: none -> 44.7 us  [exchanged(): lax.all_to_all(blocks, ('seg', 'rank'), split_axis=0, concat_axis=0, tile...]
    ppermute x2, waiting for transfers between devices: 31.6 us -> 55.9 us  [shifted(): return lax.ppermute(array, axis, pairs)]
    all_to_all x0 -> x2, starting transfers between devices: none -> 22 us  [exchanged(): lax.all_to_all(blocks, ('seg', 'rank'), split_axis=0, concat_axis=0, tile...]
    unnamed x18 -> x30, local copies, waits for them, and re-layouts: 8.12 us -> 13.1 us
    pallas_call x2 -> x4, Pallas kernels: 66 us -> 68.3 us  [the longest x1 28.4 us: make_outgoing(): pl.pallas_call(functools.partial(face_kernel, capacity), out_shape=shapes...]
  transfers between devices with their start and end apart: 2 -> 4, of which waited for: 2 -> 3; matrix products, arithmetic and copies ran while one was open for 0% -> 0% of each run, Pallas kernels for 0% -> 27%
where the time goes in v2:
time: 252 us; the launch traced here: 249 us
  Pallas kernels  107 us (42%)
  waiting for transfers between devices  101 us (40%)
  starting transfers between devices  28.2 us (11%)
  local copies, waits for them, and re-layouts  13.1 us (5%)
    ppermute x2, waiting for transfers between devices, shifted(): return lax.ppermute(array, axis, pairs)  55.9 us
    all_to_all x2, waiting for transfers between devices, exchanged(): lax.all_to_all(blocks, ('seg', 'rank'), split_axis=0, concat_axis=0, tile...  44.7 us
    pallas_call x1, Pallas kernels, collect(): pl.pallas_call(collect_kernel, out_shape=jax.ShapeDtypeStruct((150, slots...  38.4 us
    pallas_call x1, Pallas kernels, make_outgoing(): pl.pallas_call(functools.partial(face_kernel, capacity), out_shape=shapes...  28.4 us
    pallas_call x2, Pallas kernels, unpack(): pl.pallas_call(functools.partial(unpack_kernel, rows, chunk, height), out...  22.5 us
    all_to_all x2, starting transfers between devices, exchanged(): lax.all_to_all(blocks, ('seg', 'rank'), split_axis=0, concat_axis=0, tile...  22 us
    pallas_call x1, Pallas kernels, make_outgoing(): pl.pallas_call(mass_kernel, out_shape=jax.ShapeDtypeStruct((devices * MAS...  17.5 us
    unnamed x30, local copies, waits for them, and re-layouts  13.1 us
  transfers between devices with their start and end apart: 4, of which 3 were waited for; matrix products, arithmetic and copies ran while one was open for 0% of the time, Pallas kernels for 27%

profile of v2, /device:TPU:32, one launch (start us, length us, event | category | flops | bytes accessed | tf_op | source)
XLA Modules:
  0.0 249.3 jit_solution(571082483562206051)
XLA Ops:
  0.6 0.0 copy-start.1
  0.6 2.1 copy-done.1
  2.7 0.0 copy-start.5
  2.7 1.0 copy-done.5
  3.8 0.0 copy-start.7
  3.8 0.9 copy-done.7
  4.7 0.0 copy-start.9
  4.7 0.9 copy-done.9
  5.6 0.0 copy-start.11
  5.6 0.7 copy-done.11
  6.3 0.0 copy-start.12
  6.3 0.7 copy-done.12
  6.9 28.4 %faces.1 = (f32[5120,128]{1,0:T(8,128)S(1)}, bf16[2048,768]{1,0:T(8,128)(2,1)S(1)}, s32[2048,128]{1,0:T(8,128)S(1)}) custom-call(f32[375,2560]{1,0:T(8,128)S(1)} %bitcast.7, s32[1,256]{1,0:T(1,128)S(1)} %copy-done.12, s32[16,128]{1,0:T(8,128)S(1)} %bitcast.10, f32[1024,128]{1,0:T(8,128)S(1)} %copy-done.5, f32[304,128]{1,0:T(8,128)S(1)} %copy-done.7, ...), custom_call_target="tpu_custom_call" | custom-call | tf_op jit(solution)/shard_map/faces/pallas_call | solution.py:323
  35.3 0.0 copy-start.2
  35.3 1.5 copy-done.2
  36.9 0.0 copy-start.3
  36.9 1.0 copy-done.3
  37.8 0.0 copy-start.6
  37.8 0.0 copy-start.10
  37.8 15.3 %all-to-all-start.1 = ((f32[256,5,4,128]{3,2,1,0:T(4,128)}), f32[256,5,4,128]{3,2,1,0:T(4,128)}, u32[]{:S(2)}, u32[]{:S(2)}) async-start(f32[256,5,4,128]{3,2,1,0:T(4,128)} %bitcast.8), calls=%async_computation.1 | async-start | bytes 5242880 | tf_op jit(solution)/shard_map/all_to_all | solution.py:447
  53.1 0.0 copy-done.6
  53.1 0.0 copy-done.10
  53.1 0.0 copy-start.4
  53.1 1.2 copy-done.4
  54.3 17.5 %masses.1 = f32[4096,128]{1,0:T(8,128)} custom-call(bf16[2048,768]{1,0:T(8,128)(2,1)S(1)} %get-tuple-element.7.coords_ref, s32[2048,128]{1,0:T(8,128)S(1)} %copy-done.4, f32[384,128]{1,0:T(8,128)S(1)} %copy-done.6, f32[128,1]{1,0:T(8,128)S(1)} %copy-done.10), custom_call_target="tpu_custom_call" | custom-call | tf_op jit(solution)/shard_map/masses/pallas_call | solution.py:344
  71.8 44.7 %all-to-all-done.1 = f32[256,5,4,128]{3,2,1,0:T(4,128)} async-done(((f32[256,5,4,128]{3,2,1,0:T(4,128)}), f32[256,5,4,128]{3,2,1,0:T(4,128)}, u32[]{:S(2)}, u32[]{:S(2)}) %all-to-all-start.1) | async-done | bytes 2621472 | tf_op jit(solution)/shard_map/all_to_all | solution.py:447
  116.5 6.8 %all-to-all-start = ((f32[256,2,8,128]{3,2,1,0:T(8,128)}), f32[256,2,8,128]{3,2,1,0:T(8,128)S(1)}, u32[]{:S(2)}, u32[]{:S(2)}) async-start(f32[256,2,8,128]{3,2,1,0:T(8,128)} %bitcast.2), calls=%async_computation | async-start | bytes 4194304 | tf_op jit(solution)/shard_map/all_to_all | solution.py:447
  123.3 0.0 copy-start.8
  123.3 11.5 %unpack_faces.1.faces_ref = f32[150,4096]{1,0:T(8,128)} custom-call(f32[5120,128]{1,0:T(8,128)} %bitcast.6.in_ref), custom_call_target="tpu_custom_call" | custom-call | tf_op jit(solution)/shard_map/unpack_faces/pallas_call | solution.py:374
  134.8 4.2 %collective-permute-start.1 = (f32[150,4096]{1,0:T(8,128)}, f32[150,4096]{1,0:T(8,128)S(1)}, u32[]{:S(2)}, u32[]{:S(2)}) collective-permute-start(f32[150,4096]{1,0:T(8,128)} %unpack_faces.1.faces_ref), channel_id=1, source_target_pairs={{1,0},{2,1},{3,2},{4,3},{5,4},{6,5},{7,6},{8,7},{9,8},{10,9},{11,1... | collective-permute-start | bytes 7372808 | tf_op jit(solution)/shard_map/ppermute | solution.py:25
  139.0 1.9 collective-permute-start
  140.9 53.9 %collective-permute-done.1.after_ref = f32[150,4096]{1,0:T(8,128)S(1)} collective-permute-done((f32[150,4096]{1,0:T(8,128)}, f32[150,4096]{1,0:T(8,128)S(1)}, u32[]{:S(2)}, u32[]{:S(2)}) %collective-permute-start.1) | collective-permute-done | bytes 2457632 | tf_op jit(solution)/shard_map/ppermute | solution.py:25
  194.8 0.0 copy-start.14
  194.8 2.0 collective-permute-done.before_ref
  196.8 0.0 copy-done.14
  196.8 0.0 copy-done.8
  196.8 0.0 copy-start
  196.8 1.7 copy-done
  198.5 38.4 %collect.1 = f32[150,4096]{1,0:T(8,128)} custom-call(s32[6,4096]{1,0:T(8,128)S(1)} %bitcast.9, f32[150,4096]{1,0:T(8,128)S(1)} %collective-permute-done.before_ref, f32[150,4096]{1,0:T(8,128)S(1)} %copy-done, f32[150,4096]{1,0:T(8,128)} %copy-done.14), custom_call_target="tpu_custom_call" | custom-call | tf_op jit(solution)/shard_map/collect/pallas_call | solution.py:433
  236.9 0.0 all-to-all-done
  236.9 0.0 copy-start.13
  236.9 1.3 copy-done.13
  238.2 11.0 %unpack_masses.1 = f32[125,4096]{1,0:T(8,128)} custom-call(f32[4096,128]{1,0:T(8,128)} %bitcast.11), custom_call_target="tpu_custom_call" | custom-call | tf_op jit(solution)/shard_map/unpack_masses/pallas_call | solution.py:374
Async XLA Ops:
  0.6 2.1 copy-start.1
  2.7 1.0 copy-start.5
  3.8 0.9 copy-start.7
  4.7 0.9 copy-start.9
  5.6 0.7 copy-start.11
  6.3 0.7 copy-start.12
  35.3 1.5 copy-start.2
  36.9 1.0 copy-start.3
  37.8 15.3 %copy-start.6 = (f32[384,128]{1,0:T(8,128)S(1)}, f32[384,128]{1,0:T(8,128)}, u32[]{:S(2)}) copy-start(f32[384,128]{1,0:T(8,128)} %constant.13.clone.rows_ref) | copy-start | bytes 589828
  37.8 15.3 %copy-start.10 = (f32[128,1]{1,0:T(8,128)S(1)}, f32[128,1]{1,0:T(8,128)}, u32[]{:S(2)}) copy-start(f32[128,1]{1,0:T(8,128)} %constant.14.clone.scale_ref) | copy-start | bytes 1540
  37.8 78.7 %all-to-all-start.1 = ((f32[256,5,4,128]{3,2,1,0:T(4,128)}), f32[256,5,4,128]{3,2,1,0:T(4,128)}, u32[]{:S(2)}, u32[]{:S(2)}) async-start(f32[256,5,4,128]{3,2,1,0:T(4,128)} %bitcast.8), calls=%async_computation.1 | async-start | bytes 5242880 | tf_op jit(solution)/shard_map/all_to_all | solution.py:447
  53.1 1.2 copy-start.4
  116.5 120.4 %all-to-all-start = ((f32[256,2,8,128]{3,2,1,0:T(8,128)}), f32[256,2,8,128]{3,2,1,0:T(8,128)S(1)}, u32[]{:S(2)}, u32[]{:S(2)}) async-start(f32[256,2,8,128]{3,2,1,0:T(8,128)} %bitcast.2), calls=%async_computation | async-start | bytes 4194304 | tf_op jit(solution)/shard_map/all_to_all | solution.py:447
  123.3 73.5 %copy-start.8 = (s32[4096,6]{0,1:T(8,128)S(1)}, s32[4096,6]{0,1:T(8,128)}, u32[]{:S(2)}) copy-start(s32[4096,6]{0,1:T(8,128)} %param.12) | copy-start | bytes 294916
  134.8 60.0 %collective-permute-start.1 = (f32[150,4096]{1,0:T(8,128)}, f32[150,4096]{1,0:T(8,128)S(1)}, u32[]{:S(2)}, u32[]{:S(2)}) collective-permute-start(f32[150,4096]{1,0:T(8,128)} %unpack_faces.1.faces_ref), channel_id=1, source_target_pairs={{1,0},{2,1},{3,2},{4,3},{5,4},{6,5},{7,6},{8,7},{9,8},{10,9},{11,1... | collective-permute-start | bytes 7372808 | tf_op jit(solution)/shard_map/ppermute | solution.py:25
  139.0 57.8 %collective-permute-start = (f32[150,4096]{1,0:T(8,128)}, f32[150,4096]{1,0:T(8,128)S(1)}, u32[]{:S(2)}, u32[]{:S(2)}) collective-permute-start(f32[150,4096]{1,0:T(8,128)} %unpack_faces.1.faces_ref), channel_id=1, source_target_pairs={{0,1},{1,2},{2,3},{3,4},{4,5},{5,6},{6,7},{7,8},{8,9},{9,10},{10,1... | collective-permute-start | bytes 7372808 | tf_op jit(solution)/shard_map/ppermute | solution.py:25
  194.8 2.0 copy-start.14
  196.8 1.7 copy-start
  236.9 1.3 copy-start.13

commit v3 on v2

--- a/solution.py
+++ b/solution.py
@@ -11,6 +11,7 @@
 
 F32 = jnp.float32
 BF16 = jnp.bfloat16
+VMEM = 60 << 20
 GROUPS = 8
 FACE_ROWS = 19
 FACES = GROUPS * FACE_ROWS
@@ -132,25 +133,22 @@
     derivs = deriv_table.reshape(125, 3, 125).transpose(1, 2, 0)
     grid = np.arange(125).reshape(5, 5, 5)
     face_rows = np.zeros((2 * FACES, 128))
-    face_scale = np.zeros((FACES, 1))
     for face in range(6):
         nodes = np.take(grid, 0 if face % 2 == 0 else 4, axis=face // 2).reshape(-1)
         for p in range(25):
             n = 24 * face + p if p < 24 else 144 + face
-            face_rows[n, :125] = derivs[tangents[face][0]][nodes[p]]
+            face_rows[n, :125] = face_weights[p] * derivs[tangents[face][0]][nodes[p]]
             face_rows[FACES + n, :125] = derivs[tangents[face][1]][nodes[p]]
-            face_scale[n, 0] = face_weights[p]
     mass_rows = np.zeros((3 * MASS, 128))
-    mass_scale = np.zeros((MASS, 1))
-    mass_scale[:125, 0] = mass_weights
     for d in range(3):
-        mass_rows[d * MASS : d * MASS + 125, :125] = derivs[d]
-    arrays = (child.reshape(1024, 128), face_rows, face_scale, mass_rows, mass_scale)
-    return [jnp.asarray(a, F32) for a in arrays]
-
-
-def fill_table(dd_ref, rows_ref):
-    d1, d2 = split(rows_ref[...], 2)
+        weights = mass_weights[:, None] if d == 0 else 1.0
+        mass_rows[d * MASS : d * MASS + 125, :125] = weights * derivs[d]
+    first = np.concatenate([child.reshape(1024, 128), face_rows])
+    return jnp.asarray(first, F32), jnp.asarray(mass_rows, F32)
+
+
+def fill_table(dd_ref, rows):
+    d1, d2 = split(rows, 2)
     for k, piece in enumerate((d1, d1, d2, d2)):
         dd_ref[:, 128 * k : 128 * k + 128] = piece
 
@@ -196,8 +194,8 @@
 
 
 def face_kernel(
-    capacity, nodes_ref, marks_ref, owner_ref, child_ref, rows_ref, scale_ref, out_ref, coords_ref, target_ref,
-    pick_ref, x_ref, cc_ref, dd_ref, deriv_ref, vals_ref, natural_ref, onehot_ref, y_ref,
+    capacity, nodes_hbm, marks_hbm, owner_hbm, table_hbm, out_ref, coords_ref, target_ref,
+    nodes_ref, marks_ref, owner_ref, table_ref, sems, pick_ref, x_ref, cc_ref, dd_ref, deriv_ref, vals_ref, natural_ref, onehot_ref, y_ref,
 ):
     elements = nodes_ref.shape[1]
     marked = marks_ref.shape[1]
@@ -206,7 +204,22 @@
 
     @pl.when(pl.program_id(0) == 0)
     def _():
+        copies = [
+            pltpu.make_async_copy(source, kept, sems.at[i])
+            for i, (source, kept) in enumerate(
+                ((marks_hbm, marks_ref), (owner_hbm, owner_ref), (table_hbm, table_ref))
+            )
+        ]
+        chunks = [
+            pltpu.make_async_copy(
+                nodes_hbm.at[:, pl.ds(at, 512)], nodes_ref.at[:, pl.ds(at, 512)], sems.at[3 + at // 512]
+            )
+            for at in range(0, elements, 512)
+        ]
+        for copy in copies[:1] + chunks + copies[1:]:
+            copy.start()
         pick_ref[...] = jnp.zeros_like(pick_ref)
+        copies[0].wait()
         marks = marks_ref[...]
 
         def pick(k, carry):
@@ -217,17 +230,21 @@
                 pick_ref[0:375, :] += jnp.dot(piece, chosen, preferred_element_type=F32)
             return carry
 
-        lax.fori_loop(0, elements // 256, pick, 0)
+        for k, copy in enumerate(chunks):
+            copy.wait()
+            lax.fori_loop(2 * k, 2 * k + 2, pick, 0)
+        for copy in copies[1:]:
+            copy.wait()
         for c in range(3):
             x = pick_ref[125 * c : 125 * c + 128, :]
             x = x - 0.5 * (x[0:1] + x[124:125])
             a1, a2, a3 = split(x, 3)
             for k, piece in enumerate((a1, a2, a1, a3, a2, a1)):
                 x_ref[128 * k : 128 * k + 128, c * marked : (c + 1) * marked] = piece
-        c1, c2, c3 = split(child_ref[...], 3)
+        c1, c2, c3 = split(table_ref[0:1024, :], 3)
         for k, piece in enumerate((c1, c1, c2, c1, c2, c3)):
             cc_ref[:, 128 * k : 128 * k + 128] = piece
-        fill_table(dd_ref, rows_ref)
+        fill_table(dd_ref, table_ref[1024:, :])
 
         def octant(o, carry):
             coords = jnp.dot(
@@ -244,7 +261,7 @@
                 nx = u[1] * v[2] - u[2] * v[1]
                 ny = u[2] * v[0] - u[0] * v[2]
                 nz = u[0] * v[1] - u[1] * v[0]
-                put(vals_ref, row, lanes, jnp.sqrt(nx * nx + ny * ny + nz * nz) * scale_ref[pl.ds(row, rows), :])
+                put(vals_ref, row, lanes, jnp.sqrt(nx * nx + ny * ny + nz * nz))
 
             for row in range(0, FACES, 8):
                 face_block(row, 8)
@@ -276,12 +293,12 @@
     send(y_ref, out_ref, FACE_ROWS, FACE_CHUNK)
 
 
-def mass_kernel(coords_ref, target_ref, rows_ref, scale_ref, out_ref, dd_ref, deriv_ref, vals_ref, onehot_ref, y_ref):
+def mass_kernel(coords_ref, target_ref, rows_ref, out_ref, dd_ref, deriv_ref, vals_ref, onehot_ref, y_ref):
     marked = coords_ref.shape[1] // 3
 
     @pl.when(pl.program_id(0) == 0)
     def _():
-        fill_table(dd_ref, rows_ref)
+        fill_table(dd_ref, rows_ref[...])
 
         def octant(o, carry):
             slopes_of(dd_ref, deriv_ref, coords_ref[pl.ds(pl.multiple_of(o * 256, 256), 256), :])
@@ -296,7 +313,7 @@
                     - j[0][1] * (j[1][0] * j[2][2] - j[1][2] * j[2][0])
                     + j[0][2] * (j[1][0] * j[2][1] - j[1][1] * j[2][0])
                 )
-                put(vals_ref, row, lanes, determinant * scale_ref[row : row + 8, :])
+                put(vals_ref, row, lanes, determinant)
             return carry
 
         lax.fori_loop(0, 8, octant, 0)
@@ -312,9 +329,9 @@
 def make_outgoing(nodes, marks, owner, devices, capacity):
     marked = marks.shape[1]
     kids = 8 * marked
-    child, face_rows, face_scale, mass_rows, mass_scale = constants()
+    table, mass_rows = constants()
     steps = devices * capacity // 256
-    operands = (nodes, marks, owner, child, face_rows, face_scale)
+    operands = (nodes, marks, owner, table)
     shapes = (
         jax.ShapeDtypeStruct((devices * FACE_CHUNK, 128), F32),
         jax.ShapeDtypeStruct((2048, 3 * marked), BF16),
@@ -324,9 +341,11 @@
         functools.partial(face_kernel, capacity),
         out_shape=shapes,
         grid=(steps,),
-        in_specs=[whole(a) for a in operands],
+        in_specs=[pl.BlockSpec(memory_space=pltpu.HBM)] * 4,
         out_specs=(pl.BlockSpec((2 * GROUPS * FACE_CHUNK, 128), lambda i: (i, 0)), whole(shapes[1]), whole(shapes[2])),
         scratch_shapes=[
+            *(pltpu.VMEM(a.shape, a.dtype) for a in operands),
+            pltpu.SemaphoreType.DMA((3 + nodes.shape[1] // 512,)),
             pltpu.VMEM((384, marked), F32),
             pltpu.VMEM((768, 3 * marked), BF16),
             pltpu.VMEM((1024, 768), BF16),
@@ -337,10 +356,10 @@
             pltpu.VMEM((kids, 256), BF16),
             pltpu.VMEM((FACES, 256), F32),
         ],
-        compiler_params=pltpu.CompilerParams(vmem_limit_bytes=40 << 20),
+        compiler_params=pltpu.CompilerParams(vmem_limit_bytes=VMEM),
         name="faces",
     )(*operands)
-    operands = (coords, target, mass_rows, mass_scale)
+    operands = (coords, target, mass_rows)
     masses = pl.pallas_call(
         mass_kernel,
         out_shape=jax.ShapeDtypeStruct((devices * MASS_ROWS, 128), F32),
@@ -354,34 +373,44 @@
             pltpu.VMEM((kids, 256), BF16),
             pltpu.VMEM((MASS, 256), F32),
         ],
-        compiler_params=pltpu.CompilerParams(vmem_limit_bytes=32 << 20),
+        compiler_params=pltpu.CompilerParams(vmem_limit_bytes=VMEM),
         name="masses",
     )(*operands)
     return faces, masses
 
 
+def unpack_tile(rows, chunk, height, in_ref, out_ref, tile):
+    start = pl.multiple_of(tile * (chunk * GROUPS), 8)
+    lanes = pl.ds(pl.multiple_of(tile * 128, 128), 128)
+    arrived = in_ref[pl.ds(start, chunk * GROUPS), :]
+    blocks = flipped([arrived[chunk * j : chunk * j + rows] for j in range(GROUPS)])
+    for g in range(GROUPS):
+        count = min(rows, height - rows * g)
+        out_ref[rows * g : rows * g + count, lanes] = blocks[g][0:count]
+
+
 def unpack_kernel(rows, chunk, height, in_ref, out_ref):
-    for tile in range(2):
-        lanes = slice(128 * tile, 128 * tile + 128)
-        starts = [chunk * (GROUPS * tile + j) for j in range(GROUPS)]
-        blocks = flipped([in_ref[s : s + rows, :] for s in starts])
-        for g in range(GROUPS):
-            count = min(rows, height - rows * g)
-            out_ref[rows * g : rows * g + count, lanes] = blocks[g][0:count]
+    def tiles(i, carry):
+        for k in range(2):
+            unpack_tile(rows, chunk, height, in_ref, out_ref, 2 * i + k)
+        return carry
+
+    lax.fori_loop(0, out_ref.shape[1] // 256, tiles, 0)
 
 
 def unpack(arrived, slots, rows, chunk, height, name):
     return pl.pallas_call(
         functools.partial(unpack_kernel, rows, chunk, height),
         out_shape=jax.ShapeDtypeStruct((height, slots), F32),
-        grid=(slots // 256,),
-        in_specs=[pl.BlockSpec((2 * GROUPS * chunk, 128), lambda i: (i, 0))],
-        out_specs=pl.BlockSpec((height, 256), lambda i: (0, i)),
+        grid=(slots // 1024,),
+        in_specs=[pl.BlockSpec((8 * GROUPS * chunk, 128), lambda i: (i, 0))],
+        out_specs=pl.BlockSpec((height, 1024), lambda i: (0, i)),
+        compiler_params=pltpu.CompilerParams(vmem_limit_bytes=VMEM),
         name=name,
     )(arrived)
 
 
-def collect_kernel(link_ref, before_ref, faces_ref, after_ref, out_ref, table_ref, tail_ref):
+def collect_kernel(link_ref, faces_ref, packed_before, packed_after, out_ref, table_ref, tail_ref, before_ref, after_ref):
     sources = (before_ref, faces_ref, after_ref)
     per_source = faces_ref.shape[1] // 256
     tiles = 3 * per_source
@@ -389,6 +418,12 @@
 
     @pl.when(pl.program_id(0) == 0)
     def _():
+        def tile(i, carry):
+            for packed, unpacked in ((packed_before, before_ref), (packed_after, after_ref)):
+                unpack_tile(FACE_ROWS, FACE_CHUNK, 150, packed, unpacked, i)
+            return carry
+
+        lax.fori_loop(0, faces_ref.shape[1] // 128, tile, 0)
         for f in range(6):
             other = f + 1 - 2 * (f % 2)
             for k, source in enumerate(sources):
@@ -426,18 +461,23 @@
         )
 
 
-def collect(before, faces, after, links):
+def collect(faces, before, after, links):
     slots = faces.shape[1]
     tiles = 3 * slots // 256
-    operands = (links, before, faces, after)
+    operands = (links, faces, before, after)
     return pl.pallas_call(
         collect_kernel,
         out_shape=jax.ShapeDtypeStruct((150, slots), F32),
         grid=(slots // 256,),
         in_specs=[whole(a) for a in operands],
         out_specs=pl.BlockSpec((150, 256), lambda i: (0, i)),
-        scratch_shapes=[pltpu.VMEM((6, 25 * tiles, 512), BF16), pltpu.VMEM((tiles, 256), F32)],
-        compiler_params=pltpu.CompilerParams(vmem_limit_bytes=48 << 20),
+        scratch_shapes=[
+            pltpu.VMEM((6, 25 * tiles, 512), BF16),
+            pltpu.VMEM((tiles, 256), F32),
+            pltpu.VMEM(faces.shape, F32),
+            pltpu.VMEM(faces.shape, F32),
+        ],
+        compiler_params=pltpu.CompilerParams(vmem_limit_bytes=VMEM),
         name="collect",
     )(*operands)
 
@@ -453,11 +493,14 @@
     capacity = max(2, 2 * kids // devices)
     slots = devices * capacity
     faces, masses = make_outgoing(parent_nodes.T, marks, child_owner.reshape(kids // 128, 128), devices, capacity)
-    faces = unpack(exchanged(faces, devices, 4), slots, FACE_ROWS, FACE_CHUNK, 150, "unpack_faces")
+    arrived = exchanged(faces, devices, 4)
+    arrived, masses = lax.optimization_barrier((arrived, masses))
+    before = shifted(arrived, "rank", 1)
+    after = shifted(arrived, "rank", -1)
+    faces = unpack(arrived, slots, FACE_ROWS, FACE_CHUNK, 150, "unpack_faces")
+    masses, before, after, faces = lax.optimization_barrier((masses, before, after, faces))
     masses = exchanged(masses, devices, 8)
-    before = shifted(faces, "rank", 1)
-    after = shifted(faces, "rank", -1)
-    face_mass = collect(before, faces, after, face_link.T)
+    face_mass = collect(faces, before, after, face_link.T)
     masses, face_mass = lax.optimization_barrier((masses, face_mass))
     return (unpack(masses, slots, MASS_ROWS, MASS_ROWS, 125, "unpack_masses"), face_mass)
 

time: 252 us -> 220 us (0.87)
  waiting for transfers between devices: 101 us -> 69.6 us
  local copies, waits for them, and re-layouts: 13.1 us -> 1.35 us
  Pallas kernels: 107 us -> 114 us
  starting transfers between devices: 28.2 us -> 32.1 us
    ppermute x2, waiting for transfers between devices: 55.9 us -> 22.1 us  [shifted(): return lax.ppermute(array, axis, pairs)]
    unnamed x30 -> x4, local copies, waits for them, and re-layouts: 13.1 us -> 1.35 us
    pallas_call x1, Pallas kernels: 38.4 us -> 49.9 us  [collect(): pl.pallas_call(collect_kernel, out_shape=jax.ShapeDtypeStruct((150, slots...]
    pallas_call x2, Pallas kernels: 22.5 us -> 13.1 us  [unpack(): pl.pallas_call(functools.partial(unpack_kernel, rows, chunk, height), out...]
    all_to_all x2, waiting for transfers between devices: 44.7 us -> 47.5 us  [exchanged(): lax.all_to_all(blocks, ('seg', 'rank'), split_axis=0, concat_axis=0, tile...]
    pallas_call x1, Pallas kernels: 28.4 us -> 31 us  [make_outgoing(): pl.pallas_call(functools.partial(face_kernel, capacity), out_shape=shapes...]
  transfers between devices with their start and end apart: 4 -> 4, of which waited for: 3 -> 4; matrix products, arithmetic and copies ran while one was open for 0% -> 0% of each run, Pallas kernels for 27% -> 35%
where the time goes in v3:
time: 220 us; the launch traced here: 217 us
  Pallas kernels  114 us (52%)
  waiting for transfers between devices  69.6 us (32%)
  starting transfers between devices  32.1 us (15%)
    pallas_call x1, Pallas kernels, collect(): pl.pallas_call(collect_kernel, out_shape=jax.ShapeDtypeStruct((150, slots...  49.9 us
    all_to_all x2, waiting for transfers between devices, exchanged(): lax.all_to_all(blocks, ('seg', 'rank'), split_axis=0, concat_axis=0, tile...  47.5 us
    pallas_call x1, Pallas kernels, make_outgoing(): pl.pallas_call(functools.partial(face_kernel, capacity), out_shape=shapes...  31 us
    all_to_all x2, starting transfers between devices, exchanged(): lax.all_to_all(blocks, ('seg', 'rank'), split_axis=0, concat_axis=0, tile...  24.4 us
    ppermute x2, waiting for transfers between devices, shifted(): return lax.ppermute(array, axis, pairs)  22.1 us
    pallas_call x1, Pallas kernels, make_outgoing(): pl.pallas_call(mass_kernel, out_shape=jax.ShapeDtypeStruct((devices * MAS...  19.8 us
    pallas_call x2, Pallas kernels, unpack(): pl.pallas_call(functools.partial(unpack_kernel, rows, chunk, height), out...  13.1 us
    ppermute x2, starting transfers between devices, shifted(): return lax.ppermute(array, axis, pairs)  7.66 us
  transfers between devices with their start and end apart: 4, of which 4 were waited for; matrix products, arithmetic and copies ran while one was open for 0% of the time, Pallas kernels for 35%

profile of v3, /device:TPU:32, one launch (start us, length us, event | category | flops | bytes accessed | tf_op | source)
XLA Modules:
  0.0 217.5 jit_solution(2420062878289396038)
XLA Ops:
  0.6 31.0 %faces.1 = (f32[5120,128]{1,0:T(8,128)}, bf16[2048,768]{1,0:T(8,128)(2,1)}, s32[2048,128]{1,0:T(8,128)}) custom-call(f32[375,2560]{1,0:T(8,128)} %bitcast.12, s32[1,256]{1,0:T(1,128)} %marks_hbm.1, s32[16,128]{1,0:T(8,128)} %bitcast.15, f32[1328,128]{1,0:T(8,128)} %constant.4.clone.table_hbm), custom_call_target="tpu_custom_call" | custom-call | tf_op jit(solution)/shard_map/faces/pallas_call | solution.py:340
  31.6 14.4 %all-to-all-start = ((f32[256,5,4,128]{3,2,1,0:T(4,128)}), f32[256,5,4,128]{3,2,1,0:T(4,128)S(1)}, u32[]{:S(2)}, u32[]{:S(2)}) async-start(f32[256,5,4,128]{3,2,1,0:T(4,128)} %bitcast.13), calls=%async_computation | async-start | bytes 5242880 | tf_op jit(solution)/shard_map/all_to_all | solution.py:487
  46.0 19.8 %masses.1 = f32[4096,128]{1,0:T(8,128)} custom-call(bf16[2048,768]{1,0:T(8,128)(2,1)} %get-tuple-element.14.coords_ref, s32[2048,128]{1,0:T(8,128)} %get-tuple-element.15.target_ref, f32[384,128]{1,0:T(8,128)} %constant.5.clone.rows_ref), custom_call_target="tpu_custom_call" | custom-call | tf_op jit(solution)/shard_map/masses/pallas_call | solution.py:363
  65.8 44.4 %all-to-all-done = f32[256,5,4,128]{3,2,1,0:T(4,128)S(1)} async-done(((f32[256,5,4,128]{3,2,1,0:T(4,128)}), f32[256,5,4,128]{3,2,1,0:T(4,128)S(1)}, u32[]{:S(2)}, u32[]{:S(2)}) %all-to-all-start) | async-done | bytes 2621472 | tf_op jit(solution)/shard_map/all_to_all | solution.py:487
  110.2 0.0 copy-start
  110.2 1.9 collective-permute-start
  112.1 5.8 %collective-permute-start.1 = (f32[5120,128]{1,0:T(8,128)S(1)}, f32[5120,128]{1,0:T(8,128)}, u32[]{:S(2)}, u32[]{:S(2)}) collective-permute-start(f32[5120,128]{1,0:T(8,128)S(1)} %bitcast.8), channel_id=1, source_target_pairs={{1,0},{2,1},{3,2},{4,3},{5,4},{6,5},{7,6},{8,7},{9,8},{10,9},{11,1... | collective-permute-start | bytes 7864328 | tf_op jit(solution)/shard_map/ppermute | solution.py:26
  117.9 0.0 copy-done
  117.9 7.0 %unpack_faces.1.faces_ref = f32[150,4096]{1,0:T(8,128)} custom-call(f32[5120,128]{1,0:T(8,128)} %bitcast.9), custom_call_target="tpu_custom_call" | custom-call | tf_op jit(solution)/shard_map/unpack_faces/pallas_call | solution.py:402
  124.9 20.5 %collective-permute-done.packed_before = f32[5120,128]{1,0:T(8,128)} collective-permute-done((f32[5120,128]{1,0:T(8,128)S(1)}, f32[5120,128]{1,0:T(8,128)}, u32[]{:S(2)}, u32[]{:S(2)}) %collective-permute-start) | collective-permute-done | bytes 2621472 | tf_op jit(solution)/shard_map/ppermute | solution.py:26
  145.4 1.7 collective-permute-done.1.packed_after
  147.0 10.0 %all-to-all-start.1 = ((f32[256,2,8,128]{3,2,1,0:T(8,128)}), f32[256,2,8,128]{3,2,1,0:T(8,128)S(1)}, u32[]{:S(2)}, u32[]{:S(2)}) async-start(f32[256,2,8,128]{3,2,1,0:T(8,128)} %bitcast.10), calls=%async_computation.1 | async-start | bytes 4194304 | tf_op jit(solution)/shard_map/all_to_all | solution.py:487
  157.1 49.9 %collect.1 = f32[150,4096]{1,0:T(8,128)} custom-call(s32[6,4096]{1,0:T(8,128)} %bitcast.14, f32[150,4096]{1,0:T(8,128)} %unpack_faces.1.faces_ref, f32[5120,128]{1,0:T(8,128)} %collective-permute-done.packed_before, f32[5120,128]{1,0:T(8,128)} %collective-permute-done.1.packed_after), custom_call_target="tpu_custom_call" | custom-call | tf_op jit(solution)/shard_map/collect/pallas_call | solution.py:468
  206.9 3.1 %all-to-all-done.1 = f32[256,2,8,128]{3,2,1,0:T(8,128)S(1)} async-done(((f32[256,2,8,128]{3,2,1,0:T(8,128)}), f32[256,2,8,128]{3,2,1,0:T(8,128)S(1)}, u32[]{:S(2)}, u32[]{:S(2)}) %all-to-all-start.1) | async-done | bytes 2097184 | tf_op jit(solution)/shard_map/all_to_all | solution.py:487
  210.0 0.0 copy-start.1
  210.0 1.3 copy-done.1
  211.4 6.1 %unpack_masses.1 = f32[125,4096]{1,0:T(8,128)} custom-call(f32[4096,128]{1,0:T(8,128)} %bitcast.11), custom_call_target="tpu_custom_call" | custom-call | tf_op jit(solution)/shard_map/unpack_masses/pallas_call | solution.py:402
Async XLA Ops:
  31.6 78.6 %all-to-all-start = ((f32[256,5,4,128]{3,2,1,0:T(4,128)}), f32[256,5,4,128]{3,2,1,0:T(4,128)S(1)}, u32[]{:S(2)}, u32[]{:S(2)}) async-start(f32[256,5,4,128]{3,2,1,0:T(4,128)} %bitcast.13), calls=%async_computation | async-start | bytes 5242880 | tf_op jit(solution)/shard_map/all_to_all | solution.py:487
  110.2 7.7 %copy-start = (f32[256,5,4,128]{3,2,1,0:T(4,128)}, f32[256,5,4,128]{3,2,1,0:T(4,128)S(1)}, u32[]{:S(2)}) copy-start(f32[256,5,4,128]{3,2,1,0:T(4,128)S(1)} %all-to-all-done) | copy-start | bytes 7864324
  110.2 35.2 %collective-permute-start = (f32[5120,128]{1,0:T(8,128)S(1)}, f32[5120,128]{1,0:T(8,128)}, u32[]{:S(2)}, u32[]{:S(2)}) collective-permute-start(f32[5120,128]{1,0:T(8,128)S(1)} %bitcast.7), channel_id=1, source_target_pairs={{0,1},{1,2},{2,3},{3,4},{4,5},{5,6},{6,7},{7,8},{8,9},{9,10},{10,1... | collective-permute-start | bytes 7864328 | tf_op jit(solution)/shard_map/ppermute | solution.py:26
  112.1 34.9 %collective-permute-start.1 = (f32[5120,128]{1,0:T(8,128)S(1)}, f32[5120,128]{1,0:T(8,128)}, u32[]{:S(2)}, u32[]{:S(2)}) collective-permute-start(f32[5120,128]{1,0:T(8,128)S(1)} %bitcast.8), channel_id=1, source_target_pairs={{1,0},{2,1},{3,2},{4,3},{5,4},{6,5},{7,6},{8,7},{9,8},{10,9},{11,1... | collective-permute-start | bytes 7864328 | tf_op jit(solution)/shard_map/ppermute | solution.py:26
  147.0 63.0 %all-to-all-start.1 = ((f32[256,2,8,128]{3,2,1,0:T(8,128)}), f32[256,2,8,128]{3,2,1,0:T(8,128)S(1)}, u32[]{:S(2)}, u32[]{:S(2)}) async-start(f32[256,2,8,128]{3,2,1,0:T(8,128)} %bitcast.10), calls=%async_computation.1 | async-start | bytes 4194304 | tf_op jit(solution)/shard_map/all_to_all | solution.py:487
  210.0 1.3 copy-start.1

commit v4 on v3

--- a/solution.py
+++ b/solution.py
@@ -410,76 +410,115 @@
     )(arrived)
 
 
-def collect_kernel(link_ref, faces_ref, packed_before, packed_after, out_ref, table_ref, tail_ref, before_ref, after_ref):
-    sources = (before_ref, faces_ref, after_ref)
+def fill_face_table(table_ref, tail_ref, sources):
+    per_source = sources[0].shape[1] // 256
+    tiles = len(sources) * per_source
+    body_rows = 24 * tiles
+    for f in range(6):
+        other = f + 1 - 2 * (f % 2)
+        for k, source in enumerate(sources):
+
+            def pair(i, carry):
+                lanes = [pl.ds(pl.multiple_of(512 * i + 256 * e, 256), 256) for e in range(2)]
+                values = jnp.concatenate([source[24 * other : 24 * other + 24, l] for l in lanes], axis=0)
+                row = pl.multiple_of(24 * per_source * k + 48 * i, 16)
+                for part, piece in enumerate(split(values, 2)):
+                    table_ref[f, pl.ds(row, 48), 256 * part : 256 * part + 256] = piece
+                for e in range(2):
+                    tail_ref[pl.ds(per_source * k + 2 * i + e, 1), :] = source[144 + other : 145 + other, lanes[e]]
+                return carry
+
+            lax.fori_loop(0, per_source // 2, pair, 0)
+        for part, piece in enumerate(split(tail_ref[...], 2)):
+            table_ref[f, body_rows : body_rows + tiles, 256 * part : 256 * part + 256] = piece
+
+
+def look_up(table_ref, f, low, high):
+    tiles = table_ref.shape[1] // 25
+    chosen = jnp.where(lax.broadcasted_iota(jnp.int32, (256, 256), 0) == low, 1.0, 0.0).astype(BF16)
+    found = jnp.dot(table_ref[f], jnp.concatenate([chosen, chosen], axis=0), preferred_element_type=F32)
+    high24 = jnp.broadcast_to(high, (24, 256))
+    picked = jnp.zeros((24, 256), F32)
+    for h in range(tiles):
+        picked = jnp.where(high24 == h, found[24 * h : 24 * h + 24], picked)
+    last = jnp.where(lax.broadcasted_iota(jnp.int32, (tiles, 256), 0) == high, found[24 * tiles :], 0.0)
+    return picked, jnp.sum(last, axis=0, keepdims=True)
+
+
+def own_kernel(link_ref, faces_ref, out_ref, table_ref, tail_ref):
     per_source = faces_ref.shape[1] // 256
-    tiles = 3 * per_source
-    body_rows = 24 * tiles
+
+    @pl.when(pl.program_id(0) == 0)
+    def _():
+        fill_face_table(table_ref, tail_ref, (faces_ref,))
+
+    here = pl.ds(pl.multiple_of(pl.program_id(0) * 256, 256), 256)
+    for f in range(6):
+        link = link_ref[f : f + 1, here]
+        picked, last = look_up(table_ref, f, link & 255, (link >> 8) - per_source)
+        out_ref[25 * f : 25 * f + 24, :] = faces_ref[24 * f : 24 * f + 24, here] + picked
+        out_ref[25 * f + 24 : 25 * f + 25, :] = faces_ref[144 + f : 145 + f, here] + last
+
+
+def neighbour_kernel(link_ref, before_ref, after_ref, part_ref, out_ref, table_ref, tail_ref, unpacked_before, unpacked_after):
+    per_source = unpacked_before.shape[1] // 256
 
     @pl.when(pl.program_id(0) == 0)
     def _():
         def tile(i, carry):
-            for packed, unpacked in ((packed_before, before_ref), (packed_after, after_ref)):
+            for packed, unpacked in ((before_ref, unpacked_before), (after_ref, unpacked_after)):
                 unpack_tile(FACE_ROWS, FACE_CHUNK, 150, packed, unpacked, i)
             return carry
 
-        lax.fori_loop(0, faces_ref.shape[1] // 128, tile, 0)
-        for f in range(6):
-            other = f + 1 - 2 * (f % 2)
-            for k, source in enumerate(sources):
-
-                def pair(i, carry):
-                    lanes = [pl.ds(pl.multiple_of(512 * i + 256 * e, 256), 256) for e in range(2)]
-                    values = jnp.concatenate([source[24 * other : 24 * other + 24, l] for l in lanes], axis=0)
-                    row = pl.multiple_of(24 * per_source * k + 48 * i, 16)
-                    for part, piece in enumerate(split(values, 2)):
-                        table_ref[f, pl.ds(row, 48), 256 * part : 256 * part + 256] = piece
-                    for e in range(2):
-                        tail_ref[pl.ds(per_source * k + 2 * i + e, 1), :] = source[
-                            144 + other : 145 + other, lanes[e]
-                        ]
-                    return carry
-
-                lax.fori_loop(0, per_source // 2, pair, 0)
-            for part, piece in enumerate(split(tail_ref[...], 2)):
-                table_ref[f, body_rows : body_rows + tiles, 256 * part : 256 * part + 256] = piece
+        lax.fori_loop(0, unpacked_before.shape[1] // 128, tile, 0)
+        fill_face_table(table_ref, tail_ref, (unpacked_before, unpacked_after))
 
     here = pl.ds(pl.multiple_of(pl.program_id(0) * 256, 256), 256)
     for f in range(6):
         link = link_ref[f : f + 1, here]
-        low, high = link & 255, link >> 8
-        chosen = jnp.where(lax.broadcasted_iota(jnp.int32, (256, 256), 0) == low, 1.0, 0.0).astype(BF16)
-        found = jnp.dot(table_ref[f], jnp.concatenate([chosen, chosen], axis=0), preferred_element_type=F32)
-        high24 = jnp.broadcast_to(high, (24, 256))
-        picked = jnp.zeros((24, 256), F32)
-        for h in range(tiles):
-            picked = jnp.where(high24 == h, found[24 * h : 24 * h + 24], picked)
-        last = jnp.where(lax.broadcasted_iota(jnp.int32, (tiles, 256), 0) == high, found[body_rows:], 0.0)
-        out_ref[25 * f : 25 * f + 24, :] = faces_ref[24 * f : 24 * f + 24, here] + picked
-        out_ref[25 * f + 24 : 25 * f + 25, :] = faces_ref[144 + f : 145 + f, here] + jnp.sum(
-            last, axis=0, keepdims=True
-        )
-
-
-def collect(faces, before, after, links):
+        high = link >> 8
+        high = jnp.where(high < per_source, high, jnp.where(high < 2 * per_source, -1, high - per_source))
+        picked, last = look_up(table_ref, f, link & 255, high)
+        out_ref[25 * f : 25 * f + 24, :] = part_ref[25 * f : 25 * f + 24, :] + picked
+        out_ref[25 * f + 24 : 25 * f + 25, :] = part_ref[25 * f + 24 : 25 * f + 25, :] + last
+
+
+def collect_own(faces, links):
     slots = faces.shape[1]
-    tiles = 3 * slots // 256
-    operands = (links, faces, before, after)
+    tiles = slots // 256
     return pl.pallas_call(
-        collect_kernel,
+        own_kernel,
+        out_shape=jax.ShapeDtypeStruct((150, slots), F32),
+        grid=(tiles,),
+        in_specs=[whole(links), whole(faces)],
+        out_specs=pl.BlockSpec((150, 256), lambda i: (0, i)),
+        scratch_shapes=[pltpu.VMEM((6, 25 * tiles, 512), BF16), pltpu.VMEM((tiles, 256), F32)],
+        compiler_params=pltpu.CompilerParams(vmem_limit_bytes=VMEM),
+        cost_estimate=pl.CostEstimate(flops=0, bytes_accessed=1024, transcendentals=0),
+        name="collect_own",
+    )(links, faces)
+
+
+def collect_neighbours(part, before, after, links):
+    slots = part.shape[1]
+    tiles = 2 * slots // 256
+    block = pl.BlockSpec((150, 256), lambda i: (0, i))
+    return pl.pallas_call(
+        neighbour_kernel,
         out_shape=jax.ShapeDtypeStruct((150, slots), F32),
         grid=(slots // 256,),
-        in_specs=[whole(a) for a in operands],
-        out_specs=pl.BlockSpec((150, 256), lambda i: (0, i)),
+        in_specs=[whole(links), whole(before), whole(after), block],
+        out_specs=block,
         scratch_shapes=[
             pltpu.VMEM((6, 25 * tiles, 512), BF16),
             pltpu.VMEM((tiles, 256), F32),
-            pltpu.VMEM(faces.shape, F32),
-            pltpu.VMEM(faces.shape, F32),
+            pltpu.VMEM((150, slots), F32),
+            pltpu.VMEM((150, slots), F32),
         ],
         compiler_params=pltpu.CompilerParams(vmem_limit_bytes=VMEM),
-        name="collect",
-    )(*operands)
+        cost_estimate=pl.CostEstimate(flops=10**12, bytes_accessed=10**9, transcendentals=0),
+        name="collect_neighbours",
+    )(links, before, after, part)
 
 
 def exchanged(rows, devices, tile):
@@ -498,9 +537,11 @@
     before = shifted(arrived, "rank", 1)
     after = shifted(arrived, "rank", -1)
     faces = unpack(arrived, slots, FACE_ROWS, FACE_CHUNK, 150, "unpack_faces")
-    masses, before, after, faces = lax.optimization_barrier((masses, before, after, faces))
+    masses, faces = lax.optimization_barrier((masses, faces))
     masses = exchanged(masses, devices, 8)
-    face_mass = collect(faces, before, after, face_link.T)
+    part = collect_own(faces, face_link.T)
+    part, before, after = lax.optimization_barrier((part, before, after))
+    face_mass = collect_neighbours(part, before, after, face_link.T)
     masses, face_mass = lax.optimization_barrier((masses, face_mass))
     return (unpack(masses, slots, MASS_ROWS, MASS_ROWS, 125, "unpack_masses"), face_mass)
 

time: 220 us -> 224 us (1.018)
  Pallas kernels: 114 us -> 120 us
  waiting for transfers between devices: 69.6 us -> 73.1 us
  starting transfers between devices: 32.1 us -> 29.5 us
    pallas_call x1 -> x2, Pallas kernels: 49.9 us -> 56.5 us  [the longest x1 38.5 us: collect_neighbours(): pl.pallas_call(neighbour_kernel, out_shape=jax.ShapeDtypeStruct((150, slo...]
    ppermute x2, waiting for transfers between devices: 22.1 us -> 28.7 us  [shifted(): return lax.ppermute(array, axis, pairs)]
    all_to_all x2, waiting for transfers between devices: 47.5 us -> 44.4 us  [exchanged(): lax.all_to_all(blocks, ('seg', 'rank'), split_axis=0, concat_axis=0, tile...]
    ppermute x2, starting transfers between devices: 7.66 us -> 5.2 us  [shifted(): return lax.ppermute(array, axis, pairs)]
  transfers between devices with their start and end apart: 4 -> 4, of which waited for: 4 -> 3; matrix products, arithmetic and copies ran while one was open for 0% -> 0% of each run, Pallas kernels for 35% -> 37%
where the time goes in v4:
time: 224 us
  Pallas kernels  120 us (54%)
  waiting for transfers between devices  73.1 us (33%)
  starting transfers between devices  29.5 us (13%)
    all_to_all x2, waiting for transfers between devices, exchanged(): lax.all_to_all(blocks, ('seg', 'rank'), split_axis=0, concat_axis=0, tile...  44.4 us
    pallas_call x1, Pallas kernels, collect_neighbours(): pl.pallas_call(neighbour_kernel, out_shape=jax.ShapeDtypeStruct((150, slo...  38.5 us
    pallas_call x1, Pallas kernels, make_outgoing(): pl.pallas_call(functools.partial(face_kernel, capacity), out_shape=shapes...  31 us
    ppermute x2, waiting for transfers between devices, shifted(): return lax.ppermute(array, axis, pairs)  28.7 us
    all_to_all x2, starting transfers between devices, exchanged(): lax.all_to_all(blocks, ('seg', 'rank'), split_axis=0, concat_axis=0, tile...  24.3 us
    pallas_call x1, Pallas kernels, make_outgoing(): pl.pallas_call(mass_kernel, out_shape=jax.ShapeDtypeStruct((devices * MAS...  19.8 us
    pallas_call x1, Pallas kernels, collect_own(): pl.pallas_call(own_kernel, out_shape=jax.ShapeDtypeStruct((150, slots), F...  18 us
    pallas_call x2, Pallas kernels, unpack(): pl.pallas_call(functools.partial(unpack_kernel, rows, chunk, height), out...  13 us
  transfers between devices with their start and end apart: 4, of which 3 were waited for; matrix products, arithmetic and copies ran while one was open for 0% of the time, Pallas kernels for 37%

profile of v4, /device:TPU:32, one launch (start us, length us, event | category | flops | bytes accessed | tf_op | source)
XLA Modules:
  0.0 223.5 jit_solution(2987527960458018279)
XLA Ops:
  0.6 31.0 %faces.1 = (f32[5120,128]{1,0:T(8,128)}, bf16[2048,768]{1,0:T(8,128)(2,1)}, s32[2048,128]{1,0:T(8,128)}) custom-call(f32[375,2560]{1,0:T(8,128)} %bitcast.11, s32[1,256]{1,0:T(1,128)} %marks_hbm.1, s32[16,128]{1,0:T(8,128)} %bitcast.15, f32[1328,128]{1,0:T(8,128)} %constant.4.clone.table_hbm), custom_call_target="tpu_custom_call" | custom-call | tf_op jit(solution)/shard_map/faces/pallas_call | solution.py:340
  31.6 14.4 %all-to-all-start = ((f32[256,5,4,128]{3,2,1,0:T(4,128)}), f32[256,5,4,128]{3,2,1,0:T(4,128)S(1)}, u32[]{:S(2)}, u32[]{:S(2)}) async-start(f32[256,5,4,128]{3,2,1,0:T(4,128)} %bitcast.12), calls=%async_computation | async-start | bytes 5242880 | tf_op jit(solution)/shard_map/all_to_all | solution.py:526
  46.0 19.8 %masses.1 = f32[4096,128]{1,0:T(8,128)} custom-call(bf16[2048,768]{1,0:T(8,128)(2,1)} %get-tuple-element.15.coords_ref, s32[2048,128]{1,0:T(8,128)} %get-tuple-element.16.target_ref, f32[384,128]{1,0:T(8,128)} %constant.5.clone.rows_ref), custom_call_target="tpu_custom_call" | custom-call | tf_op jit(solution)/shard_map/masses/pallas_call | solution.py:363
  65.8 44.4 %all-to-all-done = f32[256,5,4,128]{3,2,1,0:T(4,128)S(1)} async-done(((f32[256,5,4,128]{3,2,1,0:T(4,128)}), f32[256,5,4,128]{3,2,1,0:T(4,128)S(1)}, u32[]{:S(2)}, u32[]{:S(2)}) %all-to-all-start) | async-done | bytes 2621472 | tf_op jit(solution)/shard_map/all_to_all | solution.py:526
  110.2 0.0 copy-start
  110.2 3.3 %collective-permute-start.1 = (f32[5120,128]{1,0:T(8,128)S(1)}, f32[5120,128]{1,0:T(8,128)}, u32[]{:S(2)}, u32[]{:S(2)}) collective-permute-start(f32[5120,128]{1,0:T(8,128)S(1)} %bitcast.7), channel_id=1, source_target_pairs={{1,0},{2,1},{3,2},{4,3},{5,4},{6,5},{7,6},{8,7},{9,8},{10,9},{11,1... | collective-permute-start | bytes 7864328 | tf_op jit(solution)/shard_map/ppermute | solution.py:26
  113.5 1.9 collective-permute-start
  115.4 0.0 copy-done
  115.4 6.9 %unpack_faces.1.faces_ref = f32[150,4096]{1,0:T(8,128)} custom-call(f32[5120,128]{1,0:T(8,128)} %bitcast.9), custom_call_target="tpu_custom_call" | custom-call | tf_op jit(solution)/shard_map/unpack_faces/pallas_call | solution.py:402
  122.3 9.9 %all-to-all-start.1 = ((f32[256,2,8,128]{3,2,1,0:T(8,128)}), f32[256,2,8,128]{3,2,1,0:T(8,128)}, u32[]{:S(2)}, u32[]{:S(2)}) async-start(f32[256,2,8,128]{3,2,1,0:T(8,128)} %bitcast.10), calls=%async_computation.1 | async-start | bytes 4194304 | tf_op jit(solution)/shard_map/all_to_all | solution.py:526
  132.2 18.0 %collect_own.1.part_ref = f32[150,4096]{1,0:T(8,128)} custom-call(s32[6,4096]{1,0:T(8,128)} %bitcast.13, f32[150,4096]{1,0:T(8,128)} %unpack_faces.1.faces_ref), custom_call_target="tpu_custom_call" | custom-call | bytes 1024 | tf_op jit(solution)/shard_map/collect_own/pallas_call | solution.py:489
  150.2 14.5 %collective-permute-done.1.after_ref = f32[5120,128]{1,0:T(8,128)} collective-permute-done((f32[5120,128]{1,0:T(8,128)S(1)}, f32[5120,128]{1,0:T(8,128)}, u32[]{:S(2)}, u32[]{:S(2)}) %collective-permute-start.1) | collective-permute-done | bytes 2621472 | tf_op jit(solution)/shard_map/ppermute | solution.py:26
  164.7 14.2 %collective-permute-done.before_ref = f32[5120,128]{1,0:T(8,128)} collective-permute-done((f32[5120,128]{1,0:T(8,128)S(1)}, f32[5120,128]{1,0:T(8,128)}, u32[]{:S(2)}, u32[]{:S(2)}) %collective-permute-start) | collective-permute-done | bytes 2621472 | tf_op jit(solution)/shard_map/ppermute | solution.py:26
  178.9 38.5 %collect_neighbours.1 = f32[150,4096]{1,0:T(8,128)} custom-call(s32[6,4096]{1,0:T(8,128)} %bitcast.14, f32[5120,128]{1,0:T(8,128)} %collective-permute-done.before_ref, f32[5120,128]{1,0:T(8,128)} %collective-permute-done.1.after_ref, f32[150,4096]{1,0:T(8,128)} %collect_own.1.part_ref), custom_call_target="tpu_custom_call" | custom-call | flops 999999995904 | bytes 1000000000 | tf_op jit(solution)/shard_map/collect_neighbours/pallas_call | solution.py:506
  217.4 0.0 all-to-all-done.1
  217.4 6.1 %unpack_masses.1 = f32[125,4096]{1,0:T(8,128)} custom-call(f32[4096,128]{1,0:T(8,128)} %bitcast.5.in_ref), custom_call_target="tpu_custom_call" | custom-call | tf_op jit(solution)/shard_map/unpack_masses/pallas_call | solution.py:402
Async XLA Ops:
  31.6 78.6 %all-to-all-start = ((f32[256,5,4,128]{3,2,1,0:T(4,128)}), f32[256,5,4,128]{3,2,1,0:T(4,128)S(1)}, u32[]{:S(2)}, u32[]{:S(2)}) async-start(f32[256,5,4,128]{3,2,1,0:T(4,128)} %bitcast.12), calls=%async_computation | async-start | bytes 5242880 | tf_op jit(solution)/shard_map/all_to_all | solution.py:526
  110.2 5.2 %copy-start = (f32[256,5,4,128]{3,2,1,0:T(4,128)}, f32[256,5,4,128]{3,2,1,0:T(4,128)S(1)}, u32[]{:S(2)}) copy-start(f32[256,5,4,128]{3,2,1,0:T(4,128)S(1)} %all-to-all-done) | copy-start | bytes 7864324
  110.2 54.5 %collective-permute-start.1 = (f32[5120,128]{1,0:T(8,128)S(1)}, f32[5120,128]{1,0:T(8,128)}, u32[]{:S(2)}, u32[]{:S(2)}) collective-permute-start(f32[5120,128]{1,0:T(8,128)S(1)} %bitcast.7), channel_id=1, source_target_pairs={{1,0},{2,1},{3,2},{4,3},{5,4},{6,5},{7,6},{8,7},{9,8},{10,9},{11,1... | collective-permute-start | bytes 7864328 | tf_op jit(solution)/shard_map/ppermute | solution.py:26
  113.5 65.4 %collective-permute-start = (f32[5120,128]{1,0:T(8,128)S(1)}, f32[5120,128]{1,0:T(8,128)}, u32[]{:S(2)}, u32[]{:S(2)}) collective-permute-start(f32[5120,128]{1,0:T(8,128)S(1)} %bitcast.8), channel_id=1, source_target_pairs={{0,1},{1,2},{2,3},{3,4},{4,5},{5,6},{6,7},{7,8},{8,9},{9,10},{10,1... | collective-permute-start | bytes 7864328 | tf_op jit(solution)/shard_map/ppermute | solution.py:26
  122.3 95.1 %all-to-all-start.1 = ((f32[256,2,8,128]{3,2,1,0:T(8,128)}), f32[256,2,8,128]{3,2,1,0:T(8,128)}, u32[]{:S(2)}, u32[]{:S(2)}) async-start(f32[256,2,8,128]{3,2,1,0:T(8,128)} %bitcast.10), calls=%async_computation.1 | async-start | bytes 4194304 | tf_op jit(solution)/shard_map/all_to_all | solution.py:526

commit v5 on v4

--- a/solution.py
+++ b/solution.py
@@ -143,71 +143,50 @@
     for d in range(3):
         weights = mass_weights[:, None] if d == 0 else 1.0
         mass_rows[d * MASS : d * MASS + 125, :125] = weights * derivs[d]
-    first = np.concatenate([child.reshape(1024, 128), face_rows])
-    return jnp.asarray(first, F32), jnp.asarray(mass_rows, F32)
-
-
-def fill_table(dd_ref, rows):
-    d1, d2 = split(rows, 2)
-    for k, piece in enumerate((d1, d1, d2, d2)):
-        dd_ref[:, 128 * k : 128 * k + 128] = piece
-
-
-def slopes_of(dd_ref, deriv_ref, coords):
-    deriv_ref[...] = jnp.dot(
-        dd_ref[...], jnp.concatenate([coords, coords], axis=0), preferred_element_type=F32
+    child = child.reshape(1024, 128)
+    return [jnp.asarray(np.concatenate([child, rows]), F32) for rows in (face_rows, mass_rows)]
+
+
+def face_values(deriv_ref, row, marked):
+    u = [deriv_ref[row : row + 8, c * marked : (c + 1) * marked] for c in range(3)]
+    v = [deriv_ref[FACES + row : FACES + row + 8, c * marked : (c + 1) * marked] for c in range(3)]
+    nx = u[1] * v[2] - u[2] * v[1]
+    ny = u[2] * v[0] - u[0] * v[2]
+    nz = u[0] * v[1] - u[1] * v[0]
+    return jnp.sqrt(nx * nx + ny * ny + nz * nz)
+
+
+def mass_values(deriv_ref, row, marked):
+    j = [
+        [deriv_ref[d * MASS + row : d * MASS + row + 8, c * marked : (c + 1) * marked] for d in range(3)]
+        for c in range(3)
+    ]
+    return (
+        j[0][0] * (j[1][1] * j[2][2] - j[1][2] * j[2][1])
+        - j[0][1] * (j[1][0] * j[2][2] - j[1][2] * j[2][0])
+        + j[0][2] * (j[1][0] * j[2][1] - j[1][1] * j[2][0])
     )
 
 
-def put(vals_ref, row, lanes, value):
-    v1, v2 = split(value, 2)
-    vals_ref[pl.ds(row, 8 * (value.shape[0] // 8)), lanes] = v1
-    vals_ref[pl.ds(vals_ref.shape[0] // 2 + row, 8 * (value.shape[0] // 8)), lanes] = v2
-
-
-def scattered(vals_ref, target_ref, onehot_ref, y_ref):
-    kids = target_ref.shape[0]
-    columns = lax.broadcasted_iota(jnp.int32, (128, 128), 1) + pl.program_id(0) * 256
-
-    def fill(i, carry):
-        rows = pl.ds(pl.multiple_of(i * 128, 128), 128)
-        target = target_ref[rows, :]
-        onehot_ref[rows, 0:128] = jnp.where(target == columns, 1.0, 0.0).astype(BF16)
-        onehot_ref[rows, 128:256] = jnp.where(target == columns + 128, 1.0, 0.0).astype(BF16)
-        return carry
-
-    lax.fori_loop(0, kids // 128, fill, 0, unroll=True)
-    moved = jnp.dot(vals_ref[...], onehot_ref[...], preferred_element_type=F32)
-    height = y_ref.shape[0]
-    y_ref[...] = moved[0:height] + moved[height:]
-
-
-def send(y_ref, out_ref, rows, chunk):
-    for tile in range(2):
-        lanes = slice(128 * tile, 128 * tile + 128)
-        blocks = flipped([y_ref[rows * g : rows * (g + 1), lanes] for g in range(GROUPS)])
-        for j in range(GROUPS):
-            start = chunk * (GROUPS * tile + j)
-            out_ref[start : start + rows, :] = blocks[j]
-            if chunk > rows:
-                out_ref[start + rows : start + chunk, :] = jnp.zeros((chunk - rows, 128), F32)
-
-
-def face_kernel(
-    capacity, nodes_hbm, marks_hbm, owner_hbm, table_hbm, out_ref, coords_ref, target_ref,
-    nodes_ref, marks_ref, owner_ref, table_ref, sems, pick_ref, x_ref, cc_ref, dd_ref, deriv_ref, vals_ref, natural_ref, onehot_ref, y_ref,
+def child_kernel(
+    values, rows, chunk, capacity, nodes_hbm, marks_hbm, owner_hbm, table_hbm, out_ref,
+    nodes_ref, marks_ref, owner_ref, table_ref, sems, pick_ref, x_ref, cc_ref, dd_ref, deriv_a, deriv_b,
+    vals_ref, natural_ref, target_ref, onehot_ref, y_ref,
 ):
     elements = nodes_ref.shape[1]
     marked = marks_ref.shape[1]
     kids = 8 * marked
-    devices = out_ref.shape[0] // FACE_CHUNK * pl.num_programs(0)
+    height = GROUPS * rows
+    columns = onehot_ref.shape[1]
+    destinations = columns // capacity
+    devices = out_ref.shape[0] // chunk * pl.num_programs(0)
 
     @pl.when(pl.program_id(0) == 0)
     def _():
         copies = [
             pltpu.make_async_copy(source, kept, sems.at[i])
             for i, (source, kept) in enumerate(
-                ((marks_hbm, marks_ref), (owner_hbm, owner_ref), (table_hbm, table_ref))
+                ((owner_hbm, owner_ref), (marks_hbm, marks_ref), (table_hbm, table_ref))
             )
         ]
         chunks = [
@@ -216,10 +195,29 @@
             )
             for at in range(0, elements, 512)
         ]
-        for copy in copies[:1] + chunks + copies[1:]:
+        for copy in copies[:2] + chunks + copies[2:]:
             copy.start()
+
+        owner_rows = lax.broadcasted_iota(jnp.int32, (devices, 128), 0)
+        earlier = lax.broadcasted_iota(jnp.int32, (128, 128), 0) < lax.broadcasted_iota(jnp.int32, (128, 128), 1)
+        earlier = jnp.where(earlier, 1.0, 0.0).astype(BF16)
+        ones = jnp.ones((128, 128), BF16)
+        copies[0].wait()
+        seen = jnp.zeros((devices, 128), F32)
+        for b in range(kids // 128):
+            owner = owner_ref[b : b + 1, :]
+            same = owner_rows == owner
+            same_b = jnp.where(same, 1.0, 0.0).astype(BF16)
+            before = jnp.dot(same_b, earlier, preferred_element_type=F32) + seen
+            position = jnp.sum(jnp.where(same, before, 0.0), axis=0, keepdims=True)
+            target = owner.astype(F32) * capacity + position
+            natural_ref[128 * b : 128 * b + 128, :] = jnp.broadcast_to(target, (128, 128)).T.astype(jnp.int32)
+            seen = seen + jnp.dot(same_b, ones, preferred_element_type=F32)
+        for o in range(8):
+            target_ref[o * marked : (o + 1) * marked, :] = natural_ref[pl.ds(o, marked, stride=8), :]
+
         pick_ref[...] = jnp.zeros_like(pick_ref)
-        copies[0].wait()
+        copies[1].wait()
         marks = marks_ref[...]
 
         def pick(k, carry):
@@ -233,8 +231,7 @@
         for k, copy in enumerate(chunks):
             copy.wait()
             lax.fori_loop(2 * k, 2 * k + 2, pick, 0)
-        for copy in copies[1:]:
-            copy.wait()
+        copies[2].wait()
         for c in range(3):
             x = pick_ref[125 * c : 125 * c + 128, :]
             x = x - 0.5 * (x[0:1] + x[124:125])
@@ -244,139 +241,96 @@
         c1, c2, c3 = split(table_ref[0:1024, :], 3)
         for k, piece in enumerate((c1, c1, c2, c1, c2, c3)):
             cc_ref[:, 128 * k : 128 * k + 128] = piece
-        fill_table(dd_ref, table_ref[1024:, :])
-
-        def octant(o, carry):
-            coords = jnp.dot(
-                cc_ref[pl.ds(pl.multiple_of(o * 128, 128), 128), :], x_ref[...], preferred_element_type=F32
-            )
-            both = jnp.concatenate(split(coords - coords[62:63], 2), axis=0)
-            coords_ref[pl.ds(pl.multiple_of(o * 256, 256), 256), :] = both
-            slopes_of(dd_ref, deriv_ref, both)
-            lanes = pl.ds(pl.multiple_of(o * marked, 128), marked)
-
-            def face_block(row, rows):
-                u = [deriv_ref[pl.ds(row, rows), c * marked : (c + 1) * marked] for c in range(3)]
-                v = [deriv_ref[pl.ds(FACES + row, rows), c * marked : (c + 1) * marked] for c in range(3)]
-                nx = u[1] * v[2] - u[2] * v[1]
-                ny = u[2] * v[0] - u[0] * v[2]
-                nz = u[0] * v[1] - u[1] * v[0]
-                put(vals_ref, row, lanes, jnp.sqrt(nx * nx + ny * ny + nz * nz))
-
-            for row in range(0, FACES, 8):
-                face_block(row, 8)
+        d1, d2 = split(table_ref[1024:, :], 2)
+        for k, piece in enumerate((d1, d1, d2, d2)):
+            dd_ref[:, 128 * k : 128 * k + 128] = piece
+
+        def octants(i, carry):
+            for e, deriv_ref in enumerate((deriv_a, deriv_b)):
+                o = 2 * i + e
+                coords = jnp.dot(
+                    cc_ref[pl.ds(pl.multiple_of(o * 128, 128), 128), :], x_ref[...], preferred_element_type=F32
+                )
+                y1, y2 = split(coords - coords[62:63], 2)
+                deriv_ref[...] = jnp.dot(
+                    dd_ref[...], jnp.concatenate([y1, y2, y1, y2], axis=0), preferred_element_type=F32
+                )
+                lanes = pl.ds(pl.multiple_of(o * marked, 128), marked)
+                for row in range(0, height, 8):
+                    v1, v2 = split(values(deriv_ref, row, marked), 2)
+                    vals_ref[row : row + 8, lanes] = v1
+                    vals_ref[height + row : height + row + 8, lanes] = v2
             return carry
 
-        lax.fori_loop(0, 8, octant, 0)
-
-        owner_rows = lax.broadcasted_iota(jnp.int32, (devices, 128), 0)
-        earlier = lax.broadcasted_iota(jnp.int32, (128, 128), 0) < lax.broadcasted_iota(jnp.int32, (128, 128), 1)
-        earlier = jnp.where(earlier, 1.0, 0.0).astype(BF16)
-        ones = jnp.ones((128, 128), BF16)
-
-        def slots(b, seen):
-            owner = owner_ref[pl.ds(b, 1), :]
-            same = owner_rows == owner
-            same_b = jnp.where(same, 1.0, 0.0).astype(BF16)
-            before = jnp.dot(same_b, earlier, preferred_element_type=F32) + seen
-            position = jnp.sum(jnp.where(same, before, 0.0), axis=0, keepdims=True)
-            target = owner.astype(F32) * capacity + position
-            target = jnp.broadcast_to(target, (128, 128)).T
-            natural_ref[pl.ds(pl.multiple_of(b * 128, 128), 128), :] = target.astype(jnp.int32)
-            return seen + jnp.dot(same_b, ones, preferred_element_type=F32)
-
-        lax.fori_loop(0, kids // 128, slots, jnp.zeros((devices, 128), F32))
-        for o in range(8):
-            target_ref[o * marked : (o + 1) * marked, :] = natural_ref[pl.ds(o, marked, stride=8), :]
-
-    scattered(vals_ref, target_ref, onehot_ref, y_ref)
-    send(y_ref, out_ref, FACE_ROWS, FACE_CHUNK)
-
-
-def mass_kernel(coords_ref, target_ref, rows_ref, out_ref, dd_ref, deriv_ref, vals_ref, onehot_ref, y_ref):
-    marked = coords_ref.shape[1] // 3
-
-    @pl.when(pl.program_id(0) == 0)
-    def _():
-        fill_table(dd_ref, rows_ref[...])
-
-        def octant(o, carry):
-            slopes_of(dd_ref, deriv_ref, coords_ref[pl.ds(pl.multiple_of(o * 256, 256), 256), :])
-            lanes = pl.ds(pl.multiple_of(o * marked, 128), marked)
-            for row in range(0, MASS, 8):
-                j = [
-                    [deriv_ref[d * MASS + row : d * MASS + row + 8, c * marked : (c + 1) * marked] for d in range(3)]
-                    for c in range(3)
-                ]
-                determinant = (
-                    j[0][0] * (j[1][1] * j[2][2] - j[1][2] * j[2][1])
-                    - j[0][1] * (j[1][0] * j[2][2] - j[1][2] * j[2][0])
-                    + j[0][2] * (j[1][0] * j[2][1] - j[1][1] * j[2][0])
-                )
-                put(vals_ref, row, lanes, determinant)
-            return carry
-
-        lax.fori_loop(0, 8, octant, 0)
-
-    scattered(vals_ref, target_ref, onehot_ref, y_ref)
-    send(y_ref, out_ref, MASS_ROWS, MASS_ROWS)
+        lax.fori_loop(0, 4, octants, 0)
+
+    numbers = lax.broadcasted_iota(jnp.int32, (128, 128), 1)
+
+    def part(i, carry):
+        first = pl.program_id(0) * (out_ref.shape[0] // chunk * capacity) + i * columns
+        for at in range(0, kids, 128):
+            target = target_ref[at : at + 128, :] - first
+            for tile in range(columns // 128):
+                onehot_ref[at : at + 128, 128 * tile : 128 * tile + 128] = jnp.where(
+                    target == numbers + 128 * tile, 1.0, 0.0
+                ).astype(BF16)
+        moved = jnp.dot(vals_ref[...], onehot_ref[...], preferred_element_type=F32)
+        y_ref[...] = moved[0:height] + moved[height:]
+        for tile in range(columns // 128):
+            lanes = slice(128 * tile, 128 * tile + 128)
+            blocks = flipped([y_ref[rows * g : rows * (g + 1), lanes] for g in range(GROUPS)])
+            if chunk > rows:
+                blocks = [jnp.concatenate([b, jnp.zeros((chunk - rows, 128), F32)], axis=0) for b in blocks]
+            start = pl.multiple_of(i * (destinations * chunk) + tile * (GROUPS * chunk), 8)
+            out_ref[pl.ds(start, GROUPS * chunk), :] = jnp.concatenate(blocks, axis=0)
+        return carry
+
+    lax.fori_loop(0, out_ref.shape[0] // (chunk * destinations), part, 0)
 
 
 def whole(a):
     return pl.BlockSpec(a.shape, lambda i: (0, 0))
 
 
-def make_outgoing(nodes, marks, owner, devices, capacity):
+def outgoing(values, rows, chunk, table, nodes, marks, owner, devices, capacity, name):
     marked = marks.shape[1]
     kids = 8 * marked
-    table, mass_rows = constants()
-    steps = devices * capacity // 256
     operands = (nodes, marks, owner, table)
-    shapes = (
-        jax.ShapeDtypeStruct((devices * FACE_CHUNK, 128), F32),
-        jax.ShapeDtypeStruct((2048, 3 * marked), BF16),
-        jax.ShapeDtypeStruct((kids, 128), jnp.int32),
-    )
-    faces, coords, target = pl.pallas_call(
-        functools.partial(face_kernel, capacity),
-        out_shape=shapes,
+    steps = 4
+    height = GROUPS * rows
+    return pl.pallas_call(
+        functools.partial(child_kernel, values, rows, chunk, capacity),
+        out_shape=jax.ShapeDtypeStruct((devices * chunk, 128), F32),
         grid=(steps,),
         in_specs=[pl.BlockSpec(memory_space=pltpu.HBM)] * 4,
-        out_specs=(pl.BlockSpec((2 * GROUPS * FACE_CHUNK, 128), lambda i: (i, 0)), whole(shapes[1]), whole(shapes[2])),
+        out_specs=pl.BlockSpec((devices * chunk // steps, 128), lambda i: (i, 0)),
         scratch_shapes=[
             *(pltpu.VMEM(a.shape, a.dtype) for a in operands),
             pltpu.SemaphoreType.DMA((3 + nodes.shape[1] // 512,)),
             pltpu.VMEM((384, marked), F32),
             pltpu.VMEM((768, 3 * marked), BF16),
             pltpu.VMEM((1024, 768), BF16),
-            pltpu.VMEM((2 * FACES, 512), BF16),
-            pltpu.VMEM((2 * FACES, 3 * marked), F32),
-            pltpu.VMEM((2 * FACES, kids), BF16),
+            pltpu.VMEM((table.shape[0] - 1024, 512), BF16),
+            pltpu.VMEM((table.shape[0] - 1024, 3 * marked), F32),
+            pltpu.VMEM((table.shape[0] - 1024, 3 * marked), F32),
+            pltpu.VMEM((2 * height, kids), BF16),
             pltpu.VMEM((kids, 128), jnp.int32),
-            pltpu.VMEM((kids, 256), BF16),
-            pltpu.VMEM((FACES, 256), F32),
+            pltpu.VMEM((kids, 128), jnp.int32),
+            pltpu.VMEM((kids, 512), BF16),
+            pltpu.VMEM((height, 512), F32),
         ],
         compiler_params=pltpu.CompilerParams(vmem_limit_bytes=VMEM),
-        name="faces",
+        name=name,
     )(*operands)
-    operands = (coords, target, mass_rows)
-    masses = pl.pallas_call(
-        mass_kernel,
-        out_shape=jax.ShapeDtypeStruct((devices * MASS_ROWS, 128), F32),
-        grid=(steps,),
-        in_specs=[whole(a) for a in operands],
-        out_specs=pl.BlockSpec((2 * GROUPS * MASS_ROWS, 128), lambda i: (i, 0)),
-        scratch_shapes=[
-            pltpu.VMEM((3 * MASS, 512), BF16),
-            pltpu.VMEM((3 * MASS, 3 * marked), F32),
-            pltpu.VMEM((2 * MASS, kids), BF16),
-            pltpu.VMEM((kids, 256), BF16),
-            pltpu.VMEM((MASS, 256), F32),
-        ],
-        compiler_params=pltpu.CompilerParams(vmem_limit_bytes=VMEM),
-        name="masses",
-    )(*operands)
-    return faces, masses
+
+
+def make_outgoing(nodes, marks, owner, devices, capacity):
+    face_table, mass_table = constants()
+    args = (nodes, marks, owner, devices, capacity)
+    return (
+        outgoing(face_values, FACE_ROWS, FACE_CHUNK, face_table, *args, "faces"),
+        outgoing(mass_values, MASS_ROWS, MASS_ROWS, mass_table, *args, "masses"),
+    )
 
 
 def unpack_tile(rows, chunk, height, in_ref, out_ref, tile):
@@ -537,9 +491,9 @@
     before = shifted(arrived, "rank", 1)
     after = shifted(arrived, "rank", -1)
     faces = unpack(arrived, slots, FACE_ROWS, FACE_CHUNK, 150, "unpack_faces")
-    masses, faces = lax.optimization_barrier((masses, faces))
+    part = collect_own(faces, face_link.T)
+    masses, part = lax.optimization_barrier((masses, part))
     masses = exchanged(masses, devices, 8)
-    part = collect_own(faces, face_link.T)
     part, before, after = lax.optimization_barrier((part, before, after))
     face_mass = collect_neighbours(part, before, after, face_link.T)
     masses, face_mass = lax.optimization_barrier((masses, face_mass))

time: 224 us -> 201 us (0.90)
  waiting for transfers between devices: 73.1 us -> 56.6 us
  Pallas kernels: 120 us -> 112 us
    ppermute x2, waiting for transfers between devices: 28.7 us -> 0.01 us  [shifted(): return lax.ppermute(array, axis, pairs)]
    all_to_all x2, waiting for transfers between devices: 44.4 us -> 56.5 us  [exchanged(): lax.all_to_all(blocks, ('seg', 'rank'), split_axis=0, concat_axis=0, tile...]
    pallas_call x2, Pallas kernels: 50.7 us -> 42.8 us  [outgoing(): pl.pallas_call(functools.partial(child_kernel, values, rows, chunk, capac...]
  transfers between devices with their start and end apart: 4 -> 4, of which waited for: 3 -> 2; matrix products, arithmetic and copies ran while one was open for 0% -> 0% of each run, Pallas kernels for 37% -> 42%
where the time goes in v5:
time: 201 us; the launch traced here: 199 us
  Pallas kernels  112 us (56%)
  waiting for transfers between devices  56.6 us (28%)
  starting transfers between devices  29.7 us (15%)
    all_to_all x2, waiting for transfers between devices, exchanged(): lax.all_to_all(blocks, ('seg', 'rank'), split_axis=0, concat_axis=0, tile...  56.5 us
    pallas_call x2, Pallas kernels, outgoing(): pl.pallas_call(functools.partial(child_kernel, values, rows, chunk, capac...  42.8 us
    pallas_call x1, Pallas kernels, collect_neighbours(): pl.pallas_call(neighbour_kernel, out_shape=jax.ShapeDtypeStruct((150, slo...  38.5 us
    all_to_all x2, starting transfers between devices, exchanged(): lax.all_to_all(blocks, ('seg', 'rank'), split_axis=0, concat_axis=0, tile...  24.3 us
    pallas_call x1, Pallas kernels, collect_own(): pl.pallas_call(own_kernel, out_shape=jax.ShapeDtypeStruct((150, slots), F...  17.9 us
    pallas_call x2, Pallas kernels, unpack(): pl.pallas_call(functools.partial(unpack_kernel, rows, chunk, height), out...  13 us
    ppermute x2, starting transfers between devices, shifted(): return lax.ppermute(array, axis, pairs)  5.38 us
  transfers between devices with their start and end apart: 4, of which 2 were waited for; matrix products, arithmetic and copies ran while one was open for 0% of the time, Pallas kernels for 42%

profile of v5, /device:TPU:32, one launch (start us, length us, event | category | flops | bytes accessed | tf_op | source)
XLA Modules:
  0.0 199.2 jit_solution(18154876269974473883)
XLA Ops:
  0.6 21.7 %faces.1 = f32[5120,128]{1,0:T(8,128)} custom-call(f32[375,2560]{1,0:T(8,128)} %bitcast.7, s32[1,256]{1,0:T(1,128)} %marks_hbm.3, s32[16,128]{1,0:T(8,128)} %bitcast.16, f32[1328,128]{1,0:T(8,128)} %constant.4.clone.table_hbm), custom_call_target="tpu_custom_call" | custom-call | tf_op jit(solution)/shard_map/faces/pallas_call | solution.py:301
  22.3 14.4 %all-to-all-start = ((f32[256,5,4,128]{3,2,1,0:T(4,128)}), f32[256,5,4,128]{3,2,1,0:T(4,128)S(1)}, u32[]{:S(2)}, u32[]{:S(2)}) async-start(f32[256,5,4,128]{3,2,1,0:T(4,128)} %bitcast.12), calls=%async_computation | async-start | bytes 5242880 | tf_op jit(solution)/shard_map/all_to_all | solution.py:480
  36.7 21.1 %masses.1 = f32[4096,128]{1,0:T(8,128)} custom-call(f32[375,2560]{1,0:T(8,128)} %bitcast.8, s32[1,256]{1,0:T(1,128)} %marks_hbm.3, s32[16,128]{1,0:T(8,128)} %bitcast.17, f32[1408,128]{1,0:T(8,128)} %constant.5.clone.table_hbm), custom_call_target="tpu_custom_call" | custom-call | tf_op jit(solution)/shard_map/masses/pallas_call | solution.py:301
  57.8 43.0 %all-to-all-done = f32[256,5,4,128]{3,2,1,0:T(4,128)S(1)} async-done(((f32[256,5,4,128]{3,2,1,0:T(4,128)}), f32[256,5,4,128]{3,2,1,0:T(4,128)S(1)}, u32[]{:S(2)}, u32[]{:S(2)}) %all-to-all-start) | async-done | bytes 2621472 | tf_op jit(solution)/shard_map/all_to_all | solution.py:480
  100.9 0.0 copy-start
  100.9 3.3 %collective-permute-start.1 = (f32[5120,128]{1,0:T(8,128)S(1)}, f32[5120,128]{1,0:T(8,128)}, u32[]{:S(2)}, u32[]{:S(2)}) collective-permute-start(f32[5120,128]{1,0:T(8,128)S(1)} %bitcast.9), channel_id=1, source_target_pairs={{1,0},{2,1},{3,2},{4,3},{5,4},{6,5},{7,6},{8,7},{9,8},{10,9},{11,1... | collective-permute-start | bytes 7864328 | tf_op jit(solution)/shard_map/ppermute | solution.py:26
  104.2 2.1 %collective-permute-start = (f32[5120,128]{1,0:T(8,128)S(1)}, f32[5120,128]{1,0:T(8,128)}, u32[]{:S(2)}, u32[]{:S(2)}) collective-permute-start(f32[5120,128]{1,0:T(8,128)S(1)} %bitcast.10), channel_id=1, source_target_pairs={{0,1},{1,2},{2,3},{3,4},{4,5},{5,6},{6,7},{7,8},{8,9},{9,10},{10,1... | collective-permute-start | bytes 7864328 | tf_op jit(solution)/shard_map/ppermute | solution.py:26
  106.3 0.0 copy-done
  106.3 6.9 %unpack_faces.1.faces_ref = f32[150,4096]{1,0:T(8,128)} custom-call(f32[5120,128]{1,0:T(8,128)} %bitcast.11), custom_call_target="tpu_custom_call" | custom-call | tf_op jit(solution)/shard_map/unpack_faces/pallas_call | solution.py:356
  113.2 17.9 %collect_own.1.part_ref = f32[150,4096]{1,0:T(8,128)} custom-call(s32[6,4096]{1,0:T(8,128)} %bitcast.14, f32[150,4096]{1,0:T(8,128)} %unpack_faces.1.faces_ref), custom_call_target="tpu_custom_call" | custom-call | bytes 1024 | tf_op jit(solution)/shard_map/collect_own/pallas_call | solution.py:443
  131.1 9.9 %all-to-all-start.1 = ((f32[256,2,8,128]{3,2,1,0:T(8,128)}), f32[256,2,8,128]{3,2,1,0:T(8,128)}, u32[]{:S(2)}, u32[]{:S(2)}) async-start(f32[256,2,8,128]{3,2,1,0:T(8,128)} %bitcast.13), calls=%async_computation.1 | async-start | bytes 4194304 | tf_op jit(solution)/shard_map/all_to_all | solution.py:480
  141.0 0.0 collective-permute-done.1.after_ref
  141.0 0.0 collective-permute-done.before_ref
  141.0 38.5 %collect_neighbours.1 = f32[150,4096]{1,0:T(8,128)} custom-call(s32[6,4096]{1,0:T(8,128)} %bitcast.15, f32[5120,128]{1,0:T(8,128)} %collective-permute-done.before_ref, f32[5120,128]{1,0:T(8,128)} %collective-permute-done.1.after_ref, f32[150,4096]{1,0:T(8,128)} %collect_own.1.part_ref), custom_call_target="tpu_custom_call" | custom-call | flops 999999995904 | bytes 1000000000 | tf_op jit(solution)/shard_map/collect_neighbours/pallas_call | solution.py:460
  179.6 13.5 %all-to-all-done.1 = f32[256,2,8,128]{3,2,1,0:T(8,128)} async-done(((f32[256,2,8,128]{3,2,1,0:T(8,128)}), f32[256,2,8,128]{3,2,1,0:T(8,128)}, u32[]{:S(2)}, u32[]{:S(2)}) %all-to-all-start.1) | async-done | bytes 2097184 | tf_op jit(solution)/shard_map/all_to_all | solution.py:480
  193.1 6.1 %unpack_masses.1 = f32[125,4096]{1,0:T(8,128)} custom-call(f32[4096,128]{1,0:T(8,128)} %bitcast.6.in_ref), custom_call_target="tpu_custom_call" | custom-call | tf_op jit(solution)/shard_map/unpack_masses/pallas_call | solution.py:356
Async XLA Ops:
  22.3 78.6 %all-to-all-start = ((f32[256,5,4,128]{3,2,1,0:T(4,128)}), f32[256,5,4,128]{3,2,1,0:T(4,128)S(1)}, u32[]{:S(2)}, u32[]{:S(2)}) async-start(f32[256,5,4,128]{3,2,1,0:T(4,128)} %bitcast.12), calls=%async_computation | async-start | bytes 5242880 | tf_op jit(solution)/shard_map/all_to_all | solution.py:480
  100.9 5.4 %copy-start = (f32[256,5,4,128]{3,2,1,0:T(4,128)}, f32[256,5,4,128]{3,2,1,0:T(4,128)S(1)}, u32[]{:S(2)}) copy-start(f32[256,5,4,128]{3,2,1,0:T(4,128)S(1)} %all-to-all-done) | copy-start | bytes 7864324
  100.9 40.1 %collective-permute-start.1 = (f32[5120,128]{1,0:T(8,128)S(1)}, f32[5120,128]{1,0:T(8,128)}, u32[]{:S(2)}, u32[]{:S(2)}) collective-permute-start(f32[5120,128]{1,0:T(8,128)S(1)} %bitcast.9), channel_id=1, source_target_pairs={{1,0},{2,1},{3,2},{4,3},{5,4},{6,5},{7,6},{8,7},{9,8},{10,9},{11,1... | collective-permute-start | bytes 7864328 | tf_op jit(solution)/shard_map/ppermute | solution.py:26
  104.2 36.9 %collective-permute-start = (f32[5120,128]{1,0:T(8,128)S(1)}, f32[5120,128]{1,0:T(8,128)}, u32[]{:S(2)}, u32[]{:S(2)}) collective-permute-start(f32[5120,128]{1,0:T(8,128)S(1)} %bitcast.10), channel_id=1, source_target_pairs={{0,1},{1,2},{2,3},{3,4},{4,5},{5,6},{6,7},{7,8},{8,9},{9,10},{10,1... | collective-permute-start | bytes 7864328 | tf_op jit(solution)/shard_map/ppermute | solution.py:26
  131.1 62.0 %all-to-all-start.1 = ((f32[256,2,8,128]{3,2,1,0:T(8,128)}), f32[256,2,8,128]{3,2,1,0:T(8,128)}, u32[]{:S(2)}, u32[]{:S(2)}) async-start(f32[256,2,8,128]{3,2,1,0:T(8,128)} %bitcast.13), calls=%async_computation.1 | async-start | bytes 4194304 | tf_op jit(solution)/shard_map/all_to_all | solution.py:480

commit v6 on v5

--- a/solution.py
+++ b/solution.py
@@ -11,6 +11,7 @@
 
 F32 = jnp.float32
 BF16 = jnp.bfloat16
+PARTS = 2
 VMEM = 60 << 20
 GROUPS = 8
 FACE_ROWS = 19
@@ -171,13 +172,14 @@
 def child_kernel(
     values, rows, chunk, capacity, nodes_hbm, marks_hbm, owner_hbm, table_hbm, out_ref,
     nodes_ref, marks_ref, owner_ref, table_ref, sems, pick_ref, x_ref, cc_ref, dd_ref, deriv_a, deriv_b,
-    vals_ref, natural_ref, target_ref, onehot_ref, y_ref,
+    vals_ref, natural_ref, target_ref, *buffers,
 ):
     elements = nodes_ref.shape[1]
     marked = marks_ref.shape[1]
     kids = 8 * marked
     height = GROUPS * rows
-    columns = onehot_ref.shape[1]
+    onehots, ys = buffers[: len(buffers) // 2], buffers[len(buffers) // 2 :]
+    columns = onehots[0].shape[1]
     destinations = columns // capacity
     devices = out_ref.shape[0] // chunk * pl.num_programs(0)
 
@@ -266,26 +268,25 @@
 
     numbers = lax.broadcasted_iota(jnp.int32, (128, 128), 1)
 
-    def part(i, carry):
-        first = pl.program_id(0) * (out_ref.shape[0] // chunk * capacity) + i * columns
+    base = pl.program_id(0) * (out_ref.shape[0] // chunk * capacity)
+    parts = list(enumerate(zip(onehots, ys)))
+    for i, (onehot_ref, y_ref) in parts:
         for at in range(0, kids, 128):
-            target = target_ref[at : at + 128, :] - first
+            target = target_ref[at : at + 128, :] - (base + i * columns)
             for tile in range(columns // 128):
                 onehot_ref[at : at + 128, 128 * tile : 128 * tile + 128] = jnp.where(
                     target == numbers + 128 * tile, 1.0, 0.0
                 ).astype(BF16)
         moved = jnp.dot(vals_ref[...], onehot_ref[...], preferred_element_type=F32)
         y_ref[...] = moved[0:height] + moved[height:]
+    for i, (_, y_ref) in parts:
         for tile in range(columns // 128):
             lanes = slice(128 * tile, 128 * tile + 128)
             blocks = flipped([y_ref[rows * g : rows * (g + 1), lanes] for g in range(GROUPS)])
             if chunk > rows:
                 blocks = [jnp.concatenate([b, jnp.zeros((chunk - rows, 128), F32)], axis=0) for b in blocks]
-            start = pl.multiple_of(i * (destinations * chunk) + tile * (GROUPS * chunk), 8)
-            out_ref[pl.ds(start, GROUPS * chunk), :] = jnp.concatenate(blocks, axis=0)
-        return carry
-
-    lax.fori_loop(0, out_ref.shape[0] // (chunk * destinations), part, 0)
+            start = (i * destinations + tile * GROUPS) * chunk
+            out_ref[start : start + GROUPS * chunk, :] = jnp.concatenate(blocks, axis=0)
 
 
 def whole(a):
@@ -316,8 +317,8 @@
             pltpu.VMEM((2 * height, kids), BF16),
             pltpu.VMEM((kids, 128), jnp.int32),
             pltpu.VMEM((kids, 128), jnp.int32),
-            pltpu.VMEM((kids, 512), BF16),
-            pltpu.VMEM((height, 512), F32),
+            *(pltpu.VMEM((kids, 1024 // PARTS), BF16) for _ in range(PARTS)),
+            *(pltpu.VMEM((height, 1024 // PARTS), F32) for _ in range(PARTS)),
         ],
         compiler_params=pltpu.CompilerParams(vmem_limit_bytes=VMEM),
         name=name,
@@ -345,11 +346,11 @@
 
 def unpack_kernel(rows, chunk, height, in_ref, out_ref):
     def tiles(i, carry):
-        for k in range(2):
-            unpack_tile(rows, chunk, height, in_ref, out_ref, 2 * i + k)
+        for k in range(4):
+            unpack_tile(rows, chunk, height, in_ref, out_ref, 4 * i + k)
         return carry
 
-    lax.fori_loop(0, out_ref.shape[1] // 256, tiles, 0)
+    lax.fori_loop(0, out_ref.shape[1] // 512, tiles, 0)
 
 
 def unpack(arrived, slots, rows, chunk, height, name):

time: 201 us -> 199 us (0.990)
  Pallas kernels: 112 us -> 108 us
    pallas_call x2, Pallas kernels: 42.8 us -> 39 us  [outgoing(): pl.pallas_call(functools.partial(child_kernel, values, rows, chunk, capac...]
    all_to_all x2, waiting for transfers between devices: 56.5 us -> 58.6 us  [exchanged(): lax.all_to_all(blocks, ('seg', 'rank'), split_axis=0, concat_axis=0, tile...]
where the time goes in v6:
time: 199 us; the launch traced here: 197 us
  Pallas kernels  108 us (54%)
  waiting for transfers between devices  58.6 us (29%)
  starting transfers between devices  29.5 us (15%)
    all_to_all x2, waiting for transfers between devices, exchanged(): lax.all_to_all(blocks, ('seg', 'rank'), split_axis=0, concat_axis=0, tile...  58.6 us
    pallas_call x2, Pallas kernels, outgoing(): pl.pallas_call(functools.partial(child_kernel, values, rows, chunk, capac...  39 us
    pallas_call x1, Pallas kernels, collect_neighbours(): pl.pallas_call(neighbour_kernel, out_shape=jax.ShapeDtypeStruct((150, slo...  38.5 us
    all_to_all x2, starting transfers between devices, exchanged(): lax.all_to_all(blocks, ('seg', 'rank'), split_axis=0, concat_axis=0, tile...  24.3 us
    pallas_call x1, Pallas kernels, collect_own(): pl.pallas_call(own_kernel, out_shape=jax.ShapeDtypeStruct((150, slots), F...  17.9 us
    pallas_call x2, Pallas kernels, unpack(): pl.pallas_call(functools.partial(unpack_kernel, rows, chunk, height), out...  12.5 us
    ppermute x2, starting transfers between devices, shifted(): return lax.ppermute(array, axis, pairs)  5.2 us
  transfers between devices with their start and end apart: 4, of which 2 were waited for; matrix products, arithmetic and copies ran while one was open for 0% of the time, Pallas kernels for 42%

profile of v6, /device:TPU:32, one launch (start us, length us, event | category | flops | bytes accessed | tf_op | source)
XLA Modules:
  0.0 196.7 jit_solution(9547939273136342195)
XLA Ops:
  0.6 20.0 %faces.1 = f32[5120,128]{1,0:T(8,128)} custom-call(f32[375,2560]{1,0:T(8,128)} %bitcast.7, s32[1,256]{1,0:T(1,128)} %marks_hbm.3, s32[16,128]{1,0:T(8,128)} %bitcast.16, f32[1328,128]{1,0:T(8,128)} %constant.4.clone.table_hbm), custom_call_target="tpu_custom_call" | custom-call | tf_op jit(solution)/shard_map/faces/pallas_call | solution.py:302
  20.6 14.4 %all-to-all-start = ((f32[256,5,4,128]{3,2,1,0:T(4,128)}), f32[256,5,4,128]{3,2,1,0:T(4,128)S(1)}, u32[]{:S(2)}, u32[]{:S(2)}) async-start(f32[256,5,4,128]{3,2,1,0:T(4,128)} %bitcast.12), calls=%async_computation | async-start | bytes 5242880 | tf_op jit(solution)/shard_map/all_to_all | solution.py:481
  35.0 19.0 %masses.1 = f32[4096,128]{1,0:T(8,128)} custom-call(f32[375,2560]{1,0:T(8,128)} %bitcast.8, s32[1,256]{1,0:T(1,128)} %marks_hbm.3, s32[16,128]{1,0:T(8,128)} %bitcast.17, f32[1408,128]{1,0:T(8,128)} %constant.5.clone.table_hbm), custom_call_target="tpu_custom_call" | custom-call | tf_op jit(solution)/shard_map/masses/pallas_call | solution.py:302
  54.0 45.1 %all-to-all-done = f32[256,5,4,128]{3,2,1,0:T(4,128)S(1)} async-done(((f32[256,5,4,128]{3,2,1,0:T(4,128)}), f32[256,5,4,128]{3,2,1,0:T(4,128)S(1)}, u32[]{:S(2)}, u32[]{:S(2)}) %all-to-all-start) | async-done | bytes 2621472 | tf_op jit(solution)/shard_map/all_to_all | solution.py:481
  99.2 0.0 copy-start
  99.2 3.3 %collective-permute-start.1 = (f32[5120,128]{1,0:T(8,128)S(1)}, f32[5120,128]{1,0:T(8,128)}, u32[]{:S(2)}, u32[]{:S(2)}) collective-permute-start(f32[5120,128]{1,0:T(8,128)S(1)} %bitcast.9), channel_id=1, source_target_pairs={{1,0},{2,1},{3,2},{4,3},{5,4},{6,5},{7,6},{8,7},{9,8},{10,9},{11,1... | collective-permute-start | bytes 7864328 | tf_op jit(solution)/shard_map/ppermute | solution.py:27
  102.4 1.9 collective-permute-start
  104.4 0.0 copy-done
  104.4 7.0 %unpack_faces.1.faces_ref = f32[150,4096]{1,0:T(8,128)} custom-call(f32[5120,128]{1,0:T(8,128)} %bitcast.11), custom_call_target="tpu_custom_call" | custom-call | tf_op jit(solution)/shard_map/unpack_faces/pallas_call | solution.py:357
  111.4 17.9 %collect_own.1.part_ref = f32[150,4096]{1,0:T(8,128)} custom-call(s32[6,4096]{1,0:T(8,128)} %bitcast.14, f32[150,4096]{1,0:T(8,128)} %unpack_faces.1.faces_ref), custom_call_target="tpu_custom_call" | custom-call | bytes 1024 | tf_op jit(solution)/shard_map/collect_own/pallas_call | solution.py:444
  129.3 9.9 %all-to-all-start.1 = ((f32[256,2,8,128]{3,2,1,0:T(8,128)}), f32[256,2,8,128]{3,2,1,0:T(8,128)}, u32[]{:S(2)}, u32[]{:S(2)}) async-start(f32[256,2,8,128]{3,2,1,0:T(8,128)} %bitcast.13), calls=%async_computation.1 | async-start | bytes 4194304 | tf_op jit(solution)/shard_map/all_to_all | solution.py:481
  139.2 0.0 collective-permute-done.1.after_ref
  139.2 0.0 collective-permute-done.before_ref
  139.2 38.5 %collect_neighbours.1 = f32[150,4096]{1,0:T(8,128)} custom-call(s32[6,4096]{1,0:T(8,128)} %bitcast.15, f32[5120,128]{1,0:T(8,128)} %collective-permute-done.before_ref, f32[5120,128]{1,0:T(8,128)} %collective-permute-done.1.after_ref, f32[150,4096]{1,0:T(8,128)} %collect_own.1.part_ref), custom_call_target="tpu_custom_call" | custom-call | flops 999999995904 | bytes 1000000000 | tf_op jit(solution)/shard_map/collect_neighbours/pallas_call | solution.py:461
  177.8 13.5 %all-to-all-done.1 = f32[256,2,8,128]{3,2,1,0:T(8,128)} async-done(((f32[256,2,8,128]{3,2,1,0:T(8,128)}), f32[256,2,8,128]{3,2,1,0:T(8,128)}, u32[]{:S(2)}, u32[]{:S(2)}) %all-to-all-start.1) | async-done | bytes 2097184 | tf_op jit(solution)/shard_map/all_to_all | solution.py:481
  191.3 5.4 %unpack_masses.1 = f32[125,4096]{1,0:T(8,128)} custom-call(f32[4096,128]{1,0:T(8,128)} %bitcast.6.in_ref), custom_call_target="tpu_custom_call" | custom-call | tf_op jit(solution)/shard_map/unpack_masses/pallas_call | solution.py:357
Async XLA Ops:
  20.6 78.6 %all-to-all-start = ((f32[256,5,4,128]{3,2,1,0:T(4,128)}), f32[256,5,4,128]{3,2,1,0:T(4,128)S(1)}, u32[]{:S(2)}, u32[]{:S(2)}) async-start(f32[256,5,4,128]{3,2,1,0:T(4,128)} %bitcast.12), calls=%async_computation | async-start | bytes 5242880 | tf_op jit(solution)/shard_map/all_to_all | solution.py:481
  99.2 5.2 %copy-start = (f32[256,5,4,128]{3,2,1,0:T(4,128)}, f32[256,5,4,128]{3,2,1,0:T(4,128)S(1)}, u32[]{:S(2)}) copy-start(f32[256,5,4,128]{3,2,1,0:T(4,128)S(1)} %all-to-all-done) | copy-start | bytes 7864324
  99.2 40.1 %collective-permute-start.1 = (f32[5120,128]{1,0:T(8,128)S(1)}, f32[5120,128]{1,0:T(8,128)}, u32[]{:S(2)}, u32[]{:S(2)}) collective-permute-start(f32[5120,128]{1,0:T(8,128)S(1)} %bitcast.9), channel_id=1, source_target_pairs={{1,0},{2,1},{3,2},{4,3},{5,4},{6,5},{7,6},{8,7},{9,8},{10,9},{11,1... | collective-permute-start | bytes 7864328 | tf_op jit(solution)/shard_map/ppermute | solution.py:27
  102.4 36.8 %collective-permute-start = (f32[5120,128]{1,0:T(8,128)S(1)}, f32[5120,128]{1,0:T(8,128)}, u32[]{:S(2)}, u32[]{:S(2)}) collective-permute-start(f32[5120,128]{1,0:T(8,128)S(1)} %bitcast.10), channel_id=1, source_target_pairs={{0,1},{1,2},{2,3},{3,4},{4,5},{5,6},{6,7},{7,8},{8,9},{9,10},{10,1... | collective-permute-start | bytes 7864328 | tf_op jit(solution)/shard_map/ppermute | solution.py:27
  129.3 62.0 %all-to-all-start.1 = ((f32[256,2,8,128]{3,2,1,0:T(8,128)}), f32[256,2,8,128]{3,2,1,0:T(8,128)}, u32[]{:S(2)}, u32[]{:S(2)}) async-start(f32[256,2,8,128]{3,2,1,0:T(8,128)} %bitcast.13), calls=%async_computation.1 | async-start | bytes 4194304 | tf_op jit(solution)/shard_map/all_to_all | solution.py:481

commit v7 on v6

--- a/solution.py
+++ b/solution.py
@@ -16,7 +16,7 @@
 GROUPS = 8
 FACE_ROWS = 19
 FACES = GROUPS * FACE_ROWS
-FACE_CHUNK = 20
+FACE_CHUNK = 19
 MASS_ROWS = 16
 MASS = GROUPS * MASS_ROWS
 
@@ -487,7 +487,7 @@
     capacity = max(2, 2 * kids // devices)
     slots = devices * capacity
     faces, masses = make_outgoing(parent_nodes.T, marks, child_owner.reshape(kids // 128, 128), devices, capacity)
-    arrived = exchanged(faces, devices, 4)
+    arrived = exchanged(faces, devices, 1)
     arrived, masses = lax.optimization_barrier((arrived, masses))
     before = shifted(arrived, "rank", 1)
     after = shifted(arrived, "rank", -1)

time: 199 us -> 196 us (0.985)
  waiting for transfers between devices: 58.6 us -> 55.5 us
    all_to_all x2, waiting for transfers between devices: 58.6 us -> 55.5 us  [exchanged(): lax.all_to_all(blocks, ('seg', 'rank'), split_axis=0, concat_axis=0, tile...]
  transfers between devices with their start and end apart: 4 -> 4, of which waited for: 2 -> 2; matrix products, arithmetic and copies ran while one was open for 0% -> 0% of each run, Pallas kernels for 42% -> 43%
where the time goes in v7:
time: 196 us; the launch traced here: 194 us
  Pallas kernels  108 us (55%)
  waiting for transfers between devices  55.5 us (28%)
  starting transfers between devices  29.6 us (15%)
    all_to_all x2, waiting for transfers between devices, exchanged(): lax.all_to_all(blocks, ('seg', 'rank'), split_axis=0, concat_axis=0, tile...  55.5 us
    pallas_call x2, Pallas kernels, outgoing(): pl.pallas_call(functools.partial(child_kernel, values, rows, chunk, capac...  38.9 us
    pallas_call x1, Pallas kernels, collect_neighbours(): pl.pallas_call(neighbour_kernel, out_shape=jax.ShapeDtypeStruct((150, slo...  38.8 us
    all_to_all x2, starting transfers between devices, exchanged(): lax.all_to_all(blocks, ('seg', 'rank'), split_axis=0, concat_axis=0, tile...  24.3 us
    pallas_call x1, Pallas kernels, collect_own(): pl.pallas_call(own_kernel, out_shape=jax.ShapeDtypeStruct((150, slots), F...  17.9 us
    pallas_call x2, Pallas kernels, unpack(): pl.pallas_call(functools.partial(unpack_kernel, rows, chunk, height), out...  12.3 us
    ppermute x2, starting transfers between devices, shifted(): return lax.ppermute(array, axis, pairs)  5.25 us
  transfers between devices with their start and end apart: 4, of which 2 were waited for; matrix products, arithmetic and copies ran while one was open for 0% of the time, Pallas kernels for 43%

profile of v7, /device:TPU:32, one launch (start us, length us, event | category | flops | bytes accessed | tf_op | source)
XLA Modules:
  0.0 193.8 jit_solution(14236557100224333570)
XLA Ops:
  0.6 19.9 %faces.1 = f32[4864,128]{1,0:T(8,128)} custom-call(f32[375,2560]{1,0:T(8,128)} %bitcast.7, s32[1,256]{1,0:T(1,128)} %marks_hbm.3, s32[16,128]{1,0:T(8,128)} %bitcast.16, f32[1328,128]{1,0:T(8,128)} %constant.4.clone.table_hbm), custom_call_target="tpu_custom_call" | custom-call | tf_op jit(solution)/shard_map/faces/pallas_call | solution.py:302
  20.5 14.4 %all-to-all-start = ((f32[256,19,1,128]{3,2,1,0:T(1,128)}), f32[256,19,1,128]{3,2,1,0:T(1,128)S(1)}, u32[]{:S(2)}, u32[]{:S(2)}) async-start(f32[256,19,1,128]{3,2,1,0:T(1,128)} %bitcast.12), calls=%async_computation | async-start | bytes 4980736 | tf_op jit(solution)/shard_map/all_to_all | solution.py:481
  34.9 19.0 %masses.1 = f32[4096,128]{1,0:T(8,128)} custom-call(f32[375,2560]{1,0:T(8,128)} %bitcast.8, s32[1,256]{1,0:T(1,128)} %marks_hbm.3, s32[16,128]{1,0:T(8,128)} %bitcast.17, f32[1408,128]{1,0:T(8,128)} %constant.5.clone.table_hbm), custom_call_target="tpu_custom_call" | custom-call | tf_op jit(solution)/shard_map/masses/pallas_call | solution.py:302
  54.0 42.3 %all-to-all-done = f32[256,19,1,128]{3,2,1,0:T(1,128)S(1)} async-done(((f32[256,19,1,128]{3,2,1,0:T(1,128)}), f32[256,19,1,128]{3,2,1,0:T(1,128)S(1)}, u32[]{:S(2)}, u32[]{:S(2)}) %all-to-all-start) | async-done | bytes 2490400 | tf_op jit(solution)/shard_map/all_to_all | solution.py:481
  96.3 0.0 copy-start
  96.3 3.3 %collective-permute-start.1 = (f32[4864,128]{1,0:T(8,128)S(1)}, f32[4864,128]{1,0:T(8,128)}, u32[]{:S(2)}, u32[]{:S(2)}) collective-permute-start(f32[4864,128]{1,0:T(8,128)S(1)} %bitcast.9), channel_id=1, source_target_pairs={{1,0},{2,1},{3,2},{4,3},{5,4},{6,5},{7,6},{8,7},{9,8},{10,9},{11,1... | collective-permute-start | bytes 7471112 | tf_op jit(solution)/shard_map/ppermute | solution.py:27
  99.6 1.9 collective-permute-start
  101.6 0.0 copy-done
  101.6 6.9 %unpack_faces.1.faces_ref = f32[150,4096]{1,0:T(8,128)} custom-call(f32[4864,128]{1,0:T(8,128)} %bitcast.11), custom_call_target="tpu_custom_call" | custom-call | tf_op jit(solution)/shard_map/unpack_faces/pallas_call | solution.py:357
  108.4 17.9 %collect_own.1.part_ref = f32[150,4096]{1,0:T(8,128)} custom-call(s32[6,4096]{1,0:T(8,128)} %bitcast.14, f32[150,4096]{1,0:T(8,128)} %unpack_faces.1.faces_ref), custom_call_target="tpu_custom_call" | custom-call | bytes 1024 | tf_op jit(solution)/shard_map/collect_own/pallas_call | solution.py:444
  126.4 9.9 %all-to-all-start.1 = ((f32[256,2,8,128]{3,2,1,0:T(8,128)}), f32[256,2,8,128]{3,2,1,0:T(8,128)}, u32[]{:S(2)}, u32[]{:S(2)}) async-start(f32[256,2,8,128]{3,2,1,0:T(8,128)} %bitcast.13), calls=%async_computation.1 | async-start | bytes 4194304 | tf_op jit(solution)/shard_map/all_to_all | solution.py:481
  136.3 0.0 collective-permute-done.1.after_ref
  136.3 0.0 collective-permute-done.before_ref
  136.3 38.8 %collect_neighbours.1 = f32[150,4096]{1,0:T(8,128)} custom-call(s32[6,4096]{1,0:T(8,128)} %bitcast.15, f32[4864,128]{1,0:T(8,128)} %collective-permute-done.before_ref, f32[4864,128]{1,0:T(8,128)} %collective-permute-done.1.after_ref, f32[150,4096]{1,0:T(8,128)} %collect_own.1.part_ref), custom_call_target="tpu_custom_call" | custom-call | flops 999999995904 | bytes 1000000000 | tf_op jit(solution)/shard_map/collect_neighbours/pallas_call | solution.py:461
  175.1 13.2 %all-to-all-done.1 = f32[256,2,8,128]{3,2,1,0:T(8,128)} async-done(((f32[256,2,8,128]{3,2,1,0:T(8,128)}), f32[256,2,8,128]{3,2,1,0:T(8,128)}, u32[]{:S(2)}, u32[]{:S(2)}) %all-to-all-start.1) | async-done | bytes 2097184 | tf_op jit(solution)/shard_map/all_to_all | solution.py:481
  188.4 5.4 %unpack_masses.1 = f32[125,4096]{1,0:T(8,128)} custom-call(f32[4096,128]{1,0:T(8,128)} %bitcast.6.in_ref), custom_call_target="tpu_custom_call" | custom-call | tf_op jit(solution)/shard_map/unpack_masses/pallas_call | solution.py:357
Async XLA Ops:
  20.5 75.8 %all-to-all-start = ((f32[256,19,1,128]{3,2,1,0:T(1,128)}), f32[256,19,1,128]{3,2,1,0:T(1,128)S(1)}, u32[]{:S(2)}, u32[]{:S(2)}) async-start(f32[256,19,1,128]{3,2,1,0:T(1,128)} %bitcast.12), calls=%async_computation | async-start | bytes 4980736 | tf_op jit(solution)/shard_map/all_to_all | solution.py:481
  96.3 5.3 %copy-start = (f32[256,19,1,128]{3,2,1,0:T(1,128)}, f32[256,19,1,128]{3,2,1,0:T(1,128)S(1)}, u32[]{:S(2)}) copy-start(f32[256,19,1,128]{3,2,1,0:T(1,128)S(1)} %all-to-all-done) | copy-start | bytes 7471108
  96.3 40.0 %collective-permute-start.1 = (f32[4864,128]{1,0:T(8,128)S(1)}, f32[4864,128]{1,0:T(8,128)}, u32[]{:S(2)}, u32[]{:S(2)}) collective-permute-start(f32[4864,128]{1,0:T(8,128)S(1)} %bitcast.9), channel_id=1, source_target_pairs={{1,0},{2,1},{3,2},{4,3},{5,4},{6,5},{7,6},{8,7},{9,8},{10,9},{11,1... | collective-permute-start | bytes 7471112 | tf_op jit(solution)/shard_map/ppermute | solution.py:27
  99.6 36.7 %collective-permute-start = (f32[4864,128]{1,0:T(8,128)S(1)}, f32[4864,128]{1,0:T(8,128)}, u32[]{:S(2)}, u32[]{:S(2)}) collective-permute-start(f32[4864,128]{1,0:T(8,128)S(1)} %bitcast.10), channel_id=1, source_target_pairs={{0,1},{1,2},{2,3},{3,4},{4,5},{5,6},{6,7},{7,8},{8,9},{9,10},{10,1... | collective-permute-start | bytes 7471112 | tf_op jit(solution)/shard_map/ppermute | solution.py:27
  126.4 62.0 %all-to-all-start.1 = ((f32[256,2,8,128]{3,2,1,0:T(8,128)}), f32[256,2,8,128]{3,2,1,0:T(8,128)}, u32[]{:S(2)}, u32[]{:S(2)}) async-start(f32[256,2,8,128]{3,2,1,0:T(8,128)} %bitcast.13), calls=%async_computation.1 | async-start | bytes 4194304 | tf_op jit(solution)/shard_map/all_to_all | solution.py:481

commit v8 on v7

--- a/solution.py
+++ b/solution.py
@@ -11,6 +11,7 @@
 
 F32 = jnp.float32
 BF16 = jnp.bfloat16
+FIRST, SECOND = (0, 1, 2), (3, 4, 5)
 PARTS = 2
 VMEM = 60 << 20
 GROUPS = 8
@@ -365,11 +366,12 @@
     )(arrived)
 
 
-def fill_face_table(table_ref, tail_ref, sources):
+def fill_face_table(table_ref, tail_ref, sources, faces):
     per_source = sources[0].shape[1] // 256
     tiles = len(sources) * per_source
     body_rows = 24 * tiles
-    for f in range(6):
+    for f in faces:
+        at = f if table_ref.shape[0] == 6 else faces.index(f)
         other = f + 1 - 2 * (f % 2)
         for k, source in enumerate(sources):
 
@@ -378,20 +380,19 @@
                 values = jnp.concatenate([source[24 * other : 24 * other + 24, l] for l in lanes], axis=0)
                 row = pl.multiple_of(24 * per_source * k + 48 * i, 16)
                 for part, piece in enumerate(split(values, 2)):
-                    table_ref[f, pl.ds(row, 48), 256 * part : 256 * part + 256] = piece
+                    table_ref[at, pl.ds(row, 48), 256 * part : 256 * part + 256] = piece
                 for e in range(2):
                     tail_ref[pl.ds(per_source * k + 2 * i + e, 1), :] = source[144 + other : 145 + other, lanes[e]]
                 return carry
 
             lax.fori_loop(0, per_source // 2, pair, 0)
-        for part, piece in enumerate(split(tail_ref[...], 2)):
-            table_ref[f, body_rows : body_rows + tiles, 256 * part : 256 * part + 256] = piece
-
-
-def look_up(table_ref, f, low, high):
-    tiles = table_ref.shape[1] // 25
+        for part, piece in enumerate(split(tail_ref[0:tiles, :], 2)):
+            table_ref[at, body_rows : body_rows + tiles, 256 * part : 256 * part + 256] = piece
+
+
+def look_up(table_ref, at, tiles, low, high):
     chosen = jnp.where(lax.broadcasted_iota(jnp.int32, (256, 256), 0) == low, 1.0, 0.0).astype(BF16)
-    found = jnp.dot(table_ref[f], jnp.concatenate([chosen, chosen], axis=0), preferred_element_type=F32)
+    found = jnp.dot(table_ref[at, 0 : 25 * tiles], jnp.concatenate([chosen, chosen], axis=0), preferred_element_type=F32)
     high24 = jnp.broadcast_to(high, (24, 256))
     picked = jnp.zeros((24, 256), F32)
     for h in range(tiles):
@@ -400,22 +401,22 @@
     return picked, jnp.sum(last, axis=0, keepdims=True)
 
 
-def own_kernel(link_ref, faces_ref, out_ref, table_ref, tail_ref):
+def own_kernel(faces, link_ref, faces_ref, out_ref, table_ref, tail_ref):
     per_source = faces_ref.shape[1] // 256
 
     @pl.when(pl.program_id(0) == 0)
     def _():
-        fill_face_table(table_ref, tail_ref, (faces_ref,))
+        fill_face_table(table_ref, tail_ref, (faces_ref,), faces)
 
     here = pl.ds(pl.multiple_of(pl.program_id(0) * 256, 256), 256)
-    for f in range(6):
+    for at, f in enumerate(faces):
         link = link_ref[f : f + 1, here]
-        picked, last = look_up(table_ref, f, link & 255, (link >> 8) - per_source)
-        out_ref[25 * f : 25 * f + 24, :] = faces_ref[24 * f : 24 * f + 24, here] + picked
-        out_ref[25 * f + 24 : 25 * f + 25, :] = faces_ref[144 + f : 145 + f, here] + last
-
-
-def neighbour_kernel(link_ref, before_ref, after_ref, part_ref, out_ref, table_ref, tail_ref, unpacked_before, unpacked_after):
+        picked, last = look_up(table_ref, at, per_source, link & 255, (link >> 8) - per_source)
+        out_ref[25 * at : 25 * at + 24, :] = faces_ref[24 * f : 24 * f + 24, here] + picked
+        out_ref[25 * at + 24 : 25 * at + 25, :] = faces_ref[144 + f : 145 + f, here] + last
+
+
+def neighbour_kernel(link_ref, before_ref, after_ref, faces_ref, first_ref, out_ref, table_ref, tail_ref, unpacked_before, unpacked_after):
     per_source = unpacked_before.shape[1] // 256
 
     @pl.when(pl.program_id(0) == 0)
@@ -426,44 +427,52 @@
             return carry
 
         lax.fori_loop(0, unpacked_before.shape[1] // 128, tile, 0)
-        fill_face_table(table_ref, tail_ref, (unpacked_before, unpacked_after))
+        fill_face_table(table_ref, tail_ref, (unpacked_before, unpacked_after), FIRST)
+        fill_face_table(table_ref, tail_ref, (unpacked_before, faces_ref, unpacked_after), SECOND)
 
     here = pl.ds(pl.multiple_of(pl.program_id(0) * 256, 256), 256)
     for f in range(6):
         link = link_ref[f : f + 1, here]
         high = link >> 8
-        high = jnp.where(high < per_source, high, jnp.where(high < 2 * per_source, -1, high - per_source))
-        picked, last = look_up(table_ref, f, link & 255, high)
-        out_ref[25 * f : 25 * f + 24, :] = part_ref[25 * f : 25 * f + 24, :] + picked
-        out_ref[25 * f + 24 : 25 * f + 25, :] = part_ref[25 * f + 24 : 25 * f + 25, :] + last
-
-
-def collect_own(faces, links):
+        if f in FIRST:
+            high = jnp.where(high < per_source, high, jnp.where(high < 2 * per_source, -1, high - per_source))
+            picked, last = look_up(table_ref, f, 2 * per_source, link & 255, high)
+            row = 25 * FIRST.index(f)
+            added, added_last = first_ref[row : row + 24, :], first_ref[row + 24 : row + 25, :]
+        else:
+            picked, last = look_up(table_ref, f, 3 * per_source, link & 255, high)
+            added, added_last = faces_ref[24 * f : 24 * f + 24, here], faces_ref[144 + f : 145 + f, here]
+        out_ref[25 * f : 25 * f + 24, :] = added + picked
+        out_ref[25 * f + 24 : 25 * f + 25, :] = added_last + last
+
+
+def collect_own(faces, links, chosen, name):
     slots = faces.shape[1]
     tiles = slots // 256
+    height = 25 * len(chosen)
     return pl.pallas_call(
-        own_kernel,
-        out_shape=jax.ShapeDtypeStruct((150, slots), F32),
+        functools.partial(own_kernel, chosen),
+        out_shape=jax.ShapeDtypeStruct((height, slots), F32),
         grid=(tiles,),
         in_specs=[whole(links), whole(faces)],
-        out_specs=pl.BlockSpec((150, 256), lambda i: (0, i)),
-        scratch_shapes=[pltpu.VMEM((6, 25 * tiles, 512), BF16), pltpu.VMEM((tiles, 256), F32)],
+        out_specs=pl.BlockSpec((height, 256), lambda i: (0, i)),
+        scratch_shapes=[pltpu.VMEM((len(chosen), 25 * tiles, 512), BF16), pltpu.VMEM((tiles, 256), F32)],
         compiler_params=pltpu.CompilerParams(vmem_limit_bytes=VMEM),
         cost_estimate=pl.CostEstimate(flops=0, bytes_accessed=1024, transcendentals=0),
-        name="collect_own",
+        name=name,
     )(links, faces)
 
 
-def collect_neighbours(part, before, after, links):
-    slots = part.shape[1]
-    tiles = 2 * slots // 256
-    block = pl.BlockSpec((150, 256), lambda i: (0, i))
+def collect_neighbours(first, faces, before, after, links):
+    slots = first.shape[1]
+    tiles = 3 * slots // 256
+    block = pl.BlockSpec((first.shape[0], 256), lambda i: (0, i))
     return pl.pallas_call(
         neighbour_kernel,
         out_shape=jax.ShapeDtypeStruct((150, slots), F32),
         grid=(slots // 256,),
-        in_specs=[whole(links), whole(before), whole(after), block],
-        out_specs=block,
+        in_specs=[whole(links), whole(before), whole(after), whole(faces), block],
+        out_specs=pl.BlockSpec((150, 256), lambda i: (0, i)),
         scratch_shapes=[
             pltpu.VMEM((6, 25 * tiles, 512), BF16),
             pltpu.VMEM((tiles, 256), F32),
@@ -473,7 +482,7 @@
         compiler_params=pltpu.CompilerParams(vmem_limit_bytes=VMEM),
         cost_estimate=pl.CostEstimate(flops=10**12, bytes_accessed=10**9, transcendentals=0),
         name="collect_neighbours",
-    )(links, before, after, part)
+    )(links, before, after, faces, first)
 
 
 def exchanged(rows, devices, tile):
@@ -492,11 +501,12 @@
     before = shifted(arrived, "rank", 1)
     after = shifted(arrived, "rank", -1)
     faces = unpack(arrived, slots, FACE_ROWS, FACE_CHUNK, 150, "unpack_faces")
-    part = collect_own(faces, face_link.T)
-    masses, part = lax.optimization_barrier((masses, part))
+    links = face_link.T
+    first = collect_own(faces, links, FIRST, "collect_first")
+    masses, first = lax.optimization_barrier((masses, first))
     masses = exchanged(masses, devices, 8)
-    part, before, after = lax.optimization_barrier((part, before, after))
-    face_mass = collect_neighbours(part, before, after, face_link.T)
+    first, before, after = lax.optimization_barrier((first, before, after))
+    face_mass = collect_neighbours(first, faces, before, after, links)
     masses, face_mass = lax.optimization_barrier((masses, face_mass))
     return (unpack(masses, slots, MASS_ROWS, MASS_ROWS, 125, "unpack_masses"), face_mass)
 

time: 196 us -> 190 us (0.969)
  waiting for transfers between devices: 55.5 us -> 49.3 us
    all_to_all x2, waiting for transfers between devices: 55.5 us -> 44.8 us  [exchanged(): lax.all_to_all(blocks, ('seg', 'rank'), split_axis=0, concat_axis=0, tile...]
    pallas_call x1, Pallas kernels: 38.8 us -> 45.1 us  [collect_neighbours(): pl.pallas_call(neighbour_kernel, out_shape=jax.ShapeDtypeStruct((150, slo...]
    pallas_call x1, Pallas kernels: 17.9 us -> 12.1 us  [collect_own(): pl.pallas_call(functools.partial(own_kernel, chosen), out_shape=jax.Shape...]
    ppermute x2, waiting for transfers between devices: 0.01 us -> 4.49 us  [shifted(): return lax.ppermute(array, axis, pairs)]
  transfers between devices with their start and end apart: 4 -> 4, of which waited for: 2 -> 3; matrix products, arithmetic and copies ran while one was open for 0% -> 0% of each run, Pallas kernels for 43% -> 44%
where the time goes in v8:
time: 190 us; the launch traced here: 188 us
  Pallas kernels  108 us (57%)
  waiting for transfers between devices  49.3 us (26%)
  starting transfers between devices  29.6 us (16%)
    pallas_call x1, Pallas kernels, collect_neighbours(): pl.pallas_call(neighbour_kernel, out_shape=jax.ShapeDtypeStruct((150, slo...  45.1 us
    all_to_all x2, waiting for transfers between devices, exchanged(): lax.all_to_all(blocks, ('seg', 'rank'), split_axis=0, concat_axis=0, tile...  44.8 us
    pallas_call x2, Pallas kernels, outgoing(): pl.pallas_call(functools.partial(child_kernel, values, rows, chunk, capac...  38.9 us
    all_to_all x2, starting transfers between devices, exchanged(): lax.all_to_all(blocks, ('seg', 'rank'), split_axis=0, concat_axis=0, tile...  24.3 us
    pallas_call x2, Pallas kernels, unpack(): pl.pallas_call(functools.partial(unpack_kernel, rows, chunk, height), out...  12.3 us
    pallas_call x1, Pallas kernels, collect_own(): pl.pallas_call(functools.partial(own_kernel, chosen), out_shape=jax.Shape...  12.1 us
    ppermute x2, starting transfers between devices, shifted(): return lax.ppermute(array, axis, pairs)  5.25 us
    ppermute x2, waiting for transfers between devices, shifted(): return lax.ppermute(array, axis, pairs)  4.49 us
  transfers between devices with their start and end apart: 4, of which 3 were waited for; matrix products, arithmetic and copies ran while one was open for 0% of the time, Pallas kernels for 44%

profile of v8, /device:TPU:32, one launch (start us, length us, event | category | flops | bytes accessed | tf_op | source)
XLA Modules:
  0.0 188.0 jit_solution(6403237733559508655)
XLA Ops:
  0.6 19.9 %faces.1 = f32[4864,128]{1,0:T(8,128)} custom-call(f32[375,2560]{1,0:T(8,128)} %bitcast.7, s32[1,256]{1,0:T(1,128)} %marks_hbm.3, s32[16,128]{1,0:T(8,128)} %bitcast.16, f32[1328,128]{1,0:T(8,128)} %constant.4.clone.table_hbm), custom_call_target="tpu_custom_call" | custom-call | tf_op jit(solution)/shard_map/faces/pallas_call | solution.py:303
  20.5 14.4 %all-to-all-start = ((f32[256,19,1,128]{3,2,1,0:T(1,128)}), f32[256,19,1,128]{3,2,1,0:T(1,128)S(1)}, u32[]{:S(2)}, u32[]{:S(2)}) async-start(f32[256,19,1,128]{3,2,1,0:T(1,128)} %bitcast.12), calls=%async_computation | async-start | bytes 4980736 | tf_op jit(solution)/shard_map/all_to_all | solution.py:490
  34.9 19.0 %masses.1 = f32[4096,128]{1,0:T(8,128)} custom-call(f32[375,2560]{1,0:T(8,128)} %bitcast.8, s32[1,256]{1,0:T(1,128)} %marks_hbm.3, s32[16,128]{1,0:T(8,128)} %bitcast.17, f32[1408,128]{1,0:T(8,128)} %constant.5.clone.table_hbm), custom_call_target="tpu_custom_call" | custom-call | tf_op jit(solution)/shard_map/masses/pallas_call | solution.py:303
  54.0 42.3 %all-to-all-done = f32[256,19,1,128]{3,2,1,0:T(1,128)S(1)} async-done(((f32[256,19,1,128]{3,2,1,0:T(1,128)}), f32[256,19,1,128]{3,2,1,0:T(1,128)S(1)}, u32[]{:S(2)}, u32[]{:S(2)}) %all-to-all-start) | async-done | bytes 2490400 | tf_op jit(solution)/shard_map/all_to_all | solution.py:490
  96.3 0.0 copy-start
  96.3 3.3 %collective-permute-start.1 = (f32[4864,128]{1,0:T(8,128)S(1)}, f32[4864,128]{1,0:T(8,128)}, u32[]{:S(2)}, u32[]{:S(2)}) collective-permute-start(f32[4864,128]{1,0:T(8,128)S(1)} %bitcast.9), channel_id=1, source_target_pairs={{1,0},{2,1},{3,2},{4,3},{5,4},{6,5},{7,6},{8,7},{9,8},{10,9},{11,1... | collective-permute-start | bytes 7471112 | tf_op jit(solution)/shard_map/ppermute | solution.py:28
  99.6 1.9 %collective-permute-start = (f32[4864,128]{1,0:T(8,128)S(1)}, f32[4864,128]{1,0:T(8,128)}, u32[]{:S(2)}, u32[]{:S(2)}) collective-permute-start(f32[4864,128]{1,0:T(8,128)S(1)} %bitcast.10), channel_id=1, source_target_pairs={{0,1},{1,2},{2,3},{3,4},{4,5},{5,6},{6,7},{7,8},{8,9},{9,10},{10,1... | collective-permute-start | bytes 7471112 | tf_op jit(solution)/shard_map/ppermute | solution.py:28
  101.6 0.0 copy-done
  101.6 6.9 %unpack_faces.1.faces_ref = f32[150,4096]{1,0:T(8,128)} custom-call(f32[4864,128]{1,0:T(8,128)} %bitcast.11), custom_call_target="tpu_custom_call" | custom-call | tf_op jit(solution)/shard_map/unpack_faces/pallas_call | solution.py:358
  108.5 12.1 %collect_first.1.first_ref = f32[75,4096]{1,0:T(8,128)} custom-call(s32[6,4096]{1,0:T(8,128)} %bitcast.14, f32[150,4096]{1,0:T(8,128)} %unpack_faces.1.faces_ref), custom_call_target="tpu_custom_call" | custom-call | bytes 1024 | tf_op jit(solution)/shard_map/collect_first/pallas_call | solution.py:453
  120.6 9.9 %all-to-all-start.1 = ((f32[256,2,8,128]{3,2,1,0:T(8,128)}), f32[256,2,8,128]{3,2,1,0:T(8,128)}, u32[]{:S(2)}, u32[]{:S(2)}) async-start(f32[256,2,8,128]{3,2,1,0:T(8,128)} %bitcast.13), calls=%async_computation.1 | async-start | bytes 4194304 | tf_op jit(solution)/shard_map/all_to_all | solution.py:490
  130.5 0.0 collective-permute-done.1.after_ref
  130.5 4.5 %collective-permute-done.before_ref = f32[4864,128]{1,0:T(8,128)} collective-permute-done((f32[4864,128]{1,0:T(8,128)S(1)}, f32[4864,128]{1,0:T(8,128)}, u32[]{:S(2)}, u32[]{:S(2)}) %collective-permute-start) | collective-permute-done | bytes 2490400 | tf_op jit(solution)/shard_map/ppermute | solution.py:28
  135.0 45.1 %collect_neighbours.1 = f32[150,4096]{1,0:T(8,128)} custom-call(s32[6,4096]{1,0:T(8,128)} %bitcast.15, f32[4864,128]{1,0:T(8,128)} %collective-permute-done.before_ref, f32[4864,128]{1,0:T(8,128)} %collective-permute-done.1.after_ref, f32[150,4096]{1,0:T(8,128)} %unpack_faces.1.faces_ref, f32[75,4096]{1,0:T(8,128)} %collect_first.1.first_ref), custom_call_target="tpu_custom_call" | custom-call | flops 999999995904 | bytes 1000000000 | tf_op jit(solution)/shard_map/collect_neighbours/pallas_call | solution.py:470
  180.1 2.5 %all-to-all-done.1 = f32[256,2,8,128]{3,2,1,0:T(8,128)} async-done(((f32[256,2,8,128]{3,2,1,0:T(8,128)}), f32[256,2,8,128]{3,2,1,0:T(8,128)}, u32[]{:S(2)}, u32[]{:S(2)}) %all-to-all-start.1) | async-done | bytes 2097184 | tf_op jit(solution)/shard_map/all_to_all | solution.py:490
  182.6 5.4 %unpack_masses.1 = f32[125,4096]{1,0:T(8,128)} custom-call(f32[4096,128]{1,0:T(8,128)} %bitcast.6.in_ref), custom_call_target="tpu_custom_call" | custom-call | tf_op jit(solution)/shard_map/unpack_masses/pallas_call | solution.py:358
Async XLA Ops:
  20.5 75.8 %all-to-all-start = ((f32[256,19,1,128]{3,2,1,0:T(1,128)}), f32[256,19,1,128]{3,2,1,0:T(1,128)S(1)}, u32[]{:S(2)}, u32[]{:S(2)}) async-start(f32[256,19,1,128]{3,2,1,0:T(1,128)} %bitcast.12), calls=%async_computation | async-start | bytes 4980736 | tf_op jit(solution)/shard_map/all_to_all | solution.py:490
  96.3 5.3 %copy-start = (f32[256,19,1,128]{3,2,1,0:T(1,128)}, f32[256,19,1,128]{3,2,1,0:T(1,128)S(1)}, u32[]{:S(2)}) copy-start(f32[256,19,1,128]{3,2,1,0:T(1,128)S(1)} %all-to-all-done) | copy-start | bytes 7471108
  96.3 34.2 %collective-permute-start.1 = (f32[4864,128]{1,0:T(8,128)S(1)}, f32[4864,128]{1,0:T(8,128)}, u32[]{:S(2)}, u32[]{:S(2)}) collective-permute-start(f32[4864,128]{1,0:T(8,128)S(1)} %bitcast.9), channel_id=1, source_target_pairs={{1,0},{2,1},{3,2},{4,3},{5,4},{6,5},{7,6},{8,7},{9,8},{10,9},{11,1... | collective-permute-start | bytes 7471112 | tf_op jit(solution)/shard_map/ppermute | solution.py:28
  99.6 35.4 %collective-permute-start = (f32[4864,128]{1,0:T(8,128)S(1)}, f32[4864,128]{1,0:T(8,128)}, u32[]{:S(2)}, u32[]{:S(2)}) collective-permute-start(f32[4864,128]{1,0:T(8,128)S(1)} %bitcast.10), channel_id=1, source_target_pairs={{0,1},{1,2},{2,3},{3,4},{4,5},{5,6},{6,7},{7,8},{8,9},{9,10},{10,1... | collective-permute-start | bytes 7471112 | tf_op jit(solution)/shard_map/ppermute | solution.py:28
  120.6 62.0 %all-to-all-start.1 = ((f32[256,2,8,128]{3,2,1,0:T(8,128)}), f32[256,2,8,128]{3,2,1,0:T(8,128)}, u32[]{:S(2)}, u32[]{:S(2)}) async-start(f32[256,2,8,128]{3,2,1,0:T(8,128)} %bitcast.13), calls=%async_computation.1 | async-start | bytes 4194304 | tf_op jit(solution)/shard_map/all_to_all | solution.py:490

commit v9 on v8

--- a/solution.py
+++ b/solution.py
@@ -11,7 +11,7 @@
 
 F32 = jnp.float32
 BF16 = jnp.bfloat16
-FIRST, SECOND = (0, 1, 2), (3, 4, 5)
+FIRST, SECOND = (0, 1), (2, 3, 4, 5)
 PARTS = 2
 VMEM = 60 << 20
 GROUPS = 8
@@ -408,12 +408,17 @@
     def _():
         fill_face_table(table_ref, tail_ref, (faces_ref,), faces)
 
-    here = pl.ds(pl.multiple_of(pl.program_id(0) * 256, 256), 256)
-    for at, f in enumerate(faces):
-        link = link_ref[f : f + 1, here]
-        picked, last = look_up(table_ref, at, per_source, link & 255, (link >> 8) - per_source)
-        out_ref[25 * at : 25 * at + 24, :] = faces_ref[24 * f : 24 * f + 24, here] + picked
-        out_ref[25 * at + 24 : 25 * at + 25, :] = faces_ref[144 + f : 145 + f, here] + last
+    def columns(k, carry):
+        here = pl.ds(pl.multiple_of(pl.program_id(0) * 1024 + 256 * k, 256), 256)
+        lanes = pl.ds(pl.multiple_of(256 * k, 256), 256)
+        for at, f in enumerate(faces):
+            link = link_ref[f : f + 1, here]
+            picked, last = look_up(table_ref, at, per_source, link & 255, (link >> 8) - per_source)
+            out_ref[25 * at : 25 * at + 24, lanes] = faces_ref[24 * f : 24 * f + 24, here] + picked
+            out_ref[25 * at + 24 : 25 * at + 25, lanes] = faces_ref[144 + f : 145 + f, here] + last
+        return carry
+
+    lax.fori_loop(0, out_ref.shape[1] // 256, columns, 0)
 
 
 def neighbour_kernel(link_ref, before_ref, after_ref, faces_ref, first_ref, out_ref, table_ref, tail_ref, unpacked_before, unpacked_after):
@@ -422,28 +427,34 @@
     @pl.when(pl.program_id(0) == 0)
     def _():
         def tile(i, carry):
-            for packed, unpacked in ((before_ref, unpacked_before), (after_ref, unpacked_after)):
-                unpack_tile(FACE_ROWS, FACE_CHUNK, 150, packed, unpacked, i)
+            for k in range(2):
+                for packed, unpacked in ((before_ref, unpacked_before), (after_ref, unpacked_after)):
+                    unpack_tile(FACE_ROWS, FACE_CHUNK, 150, packed, unpacked, 2 * i + k)
             return carry
 
-        lax.fori_loop(0, unpacked_before.shape[1] // 128, tile, 0)
+        lax.fori_loop(0, unpacked_before.shape[1] // 256, tile, 0)
         fill_face_table(table_ref, tail_ref, (unpacked_before, unpacked_after), FIRST)
         fill_face_table(table_ref, tail_ref, (unpacked_before, faces_ref, unpacked_after), SECOND)
 
-    here = pl.ds(pl.multiple_of(pl.program_id(0) * 256, 256), 256)
-    for f in range(6):
-        link = link_ref[f : f + 1, here]
-        high = link >> 8
-        if f in FIRST:
-            high = jnp.where(high < per_source, high, jnp.where(high < 2 * per_source, -1, high - per_source))
-            picked, last = look_up(table_ref, f, 2 * per_source, link & 255, high)
-            row = 25 * FIRST.index(f)
-            added, added_last = first_ref[row : row + 24, :], first_ref[row + 24 : row + 25, :]
-        else:
-            picked, last = look_up(table_ref, f, 3 * per_source, link & 255, high)
-            added, added_last = faces_ref[24 * f : 24 * f + 24, here], faces_ref[144 + f : 145 + f, here]
-        out_ref[25 * f : 25 * f + 24, :] = added + picked
-        out_ref[25 * f + 24 : 25 * f + 25, :] = added_last + last
+    def columns(k, carry):
+        here = pl.ds(pl.multiple_of(pl.program_id(0) * 1024 + 256 * k, 256), 256)
+        lanes = pl.ds(pl.multiple_of(256 * k, 256), 256)
+        for f in range(6):
+            link = link_ref[f : f + 1, here]
+            high = link >> 8
+            if f in FIRST:
+                high = jnp.where(high < per_source, high, jnp.where(high < 2 * per_source, -1, high - per_source))
+                picked, last = look_up(table_ref, f, 2 * per_source, link & 255, high)
+                row = 25 * FIRST.index(f)
+                added, added_last = first_ref[row : row + 24, lanes], first_ref[row + 24 : row + 25, lanes]
+            else:
+                picked, last = look_up(table_ref, f, 3 * per_source, link & 255, high)
+                added, added_last = faces_ref[24 * f : 24 * f + 24, here], faces_ref[144 + f : 145 + f, here]
+            out_ref[25 * f : 25 * f + 24, lanes] = added + picked
+            out_ref[25 * f + 24 : 25 * f + 25, lanes] = added_last + last
+        return carry
+
+    lax.fori_loop(0, out_ref.shape[1] // 256, columns, 0)
 
 
 def collect_own(faces, links, chosen, name):
@@ -453,9 +464,9 @@
     return pl.pallas_call(
         functools.partial(own_kernel, chosen),
         out_shape=jax.ShapeDtypeStruct((height, slots), F32),
-        grid=(tiles,),
+        grid=(slots // 1024,),
         in_specs=[whole(links), whole(faces)],
-        out_specs=pl.BlockSpec((height, 256), lambda i: (0, i)),
+        out_specs=pl.BlockSpec((height, 1024), lambda i: (0, i)),
         scratch_shapes=[pltpu.VMEM((len(chosen), 25 * tiles, 512), BF16), pltpu.VMEM((tiles, 256), F32)],
         compiler_params=pltpu.CompilerParams(vmem_limit_bytes=VMEM),
         cost_estimate=pl.CostEstimate(flops=0, bytes_accessed=1024, transcendentals=0),
@@ -466,13 +477,13 @@
 def collect_neighbours(first, faces, before, after, links):
     slots = first.shape[1]
     tiles = 3 * slots // 256
-    block = pl.BlockSpec((first.shape[0], 256), lambda i: (0, i))
+    block = pl.BlockSpec((first.shape[0], 1024), lambda i: (0, i))
     return pl.pallas_call(
         neighbour_kernel,
         out_shape=jax.ShapeDtypeStruct((150, slots), F32),
-        grid=(slots // 256,),
+        grid=(slots // 1024,),
         in_specs=[whole(links), whole(before), whole(after), whole(faces), block],
-        out_specs=pl.BlockSpec((150, 256), lambda i: (0, i)),
+        out_specs=pl.BlockSpec((150, 1024), lambda i: (0, i)),
         scratch_shapes=[
             pltpu.VMEM((6, 25 * tiles, 512), BF16),
             pltpu.VMEM((tiles, 256), F32),

time: 190 us -> 193 us (1.016); the launches traced: 188 us -> 193 us
  waiting for transfers between devices: 49.3 us -> 56.1 us
    ppermute x2, waiting for transfers between devices: 4.49 us -> 13.8 us  [shifted(): return lax.ppermute(array, axis, pairs)]
    pallas_call x1, Pallas kernels: 12.1 us -> 9.34 us  [collect_own(): pl.pallas_call(functools.partial(own_kernel, chosen), out_shape=jax.Shape...]
    all_to_all x2, waiting for transfers between devices: 44.8 us -> 42.3 us  [exchanged(): lax.all_to_all(blocks, ('seg', 'rank'), split_axis=0, concat_axis=0, tile...]
  transfers between devices with their start and end apart: 4 -> 4, of which waited for: 3 -> 3; matrix products, arithmetic and copies ran while one was open for 0% -> 0% of each run, Pallas kernels for 44% -> 42%
where the time goes in v9:
time: 193 us
  Pallas kernels  107 us (55%)
  waiting for transfers between devices  56.1 us (29%)
  starting transfers between devices  29.6 us (15%)
    pallas_call x1, Pallas kernels, collect_neighbours(): pl.pallas_call(neighbour_kernel, out_shape=jax.ShapeDtypeStruct((150, slo...  46.1 us
    all_to_all x2, waiting for transfers between devices, exchanged(): lax.all_to_all(blocks, ('seg', 'rank'), split_axis=0, concat_axis=0, tile...  42.3 us
    pallas_call x2, Pallas kernels, outgoing(): pl.pallas_call(functools.partial(child_kernel, values, rows, chunk, capac...  38.9 us
    all_to_all x2, starting transfers between devices, exchanged(): lax.all_to_all(blocks, ('seg', 'rank'), split_axis=0, concat_axis=0, tile...  24.3 us
    ppermute x2, waiting for transfers between devices, shifted(): return lax.ppermute(array, axis, pairs)  13.8 us
    pallas_call x2, Pallas kernels, unpack(): pl.pallas_call(functools.partial(unpack_kernel, rows, chunk, height), out...  12.3 us
    pallas_call x1, Pallas kernels, collect_own(): pl.pallas_call(functools.partial(own_kernel, chosen), out_shape=jax.Shape...  9.34 us
    ppermute x2, starting transfers between devices, shifted(): return lax.ppermute(array, axis, pairs)  5.25 us
  transfers between devices with their start and end apart: 4, of which 3 were waited for; matrix products, arithmetic and copies ran while one was open for 0% of the time, Pallas kernels for 42%

profile of v9, /device:TPU:32, one launch (start us, length us, event | category | flops | bytes accessed | tf_op | source)
XLA Modules:
  0.0 193.0 jit_solution(8462009892758264898)
XLA Ops:
  0.6 19.9 %faces.1 = f32[4864,128]{1,0:T(8,128)} custom-call(f32[375,2560]{1,0:T(8,128)} %bitcast.7, s32[1,256]{1,0:T(1,128)} %marks_hbm.3, s32[16,128]{1,0:T(8,128)} %bitcast.16, f32[1328,128]{1,0:T(8,128)} %constant.4.clone.table_hbm), custom_call_target="tpu_custom_call" | custom-call | tf_op jit(solution)/shard_map/faces/pallas_call | solution.py:303
  20.5 14.4 %all-to-all-start = ((f32[256,19,1,128]{3,2,1,0:T(1,128)}), f32[256,19,1,128]{3,2,1,0:T(1,128)S(1)}, u32[]{:S(2)}, u32[]{:S(2)}) async-start(f32[256,19,1,128]{3,2,1,0:T(1,128)} %bitcast.12), calls=%async_computation | async-start | bytes 4980736 | tf_op jit(solution)/shard_map/all_to_all | solution.py:501
  34.9 19.0 %masses.1 = f32[4096,128]{1,0:T(8,128)} custom-call(f32[375,2560]{1,0:T(8,128)} %bitcast.8, s32[1,256]{1,0:T(1,128)} %marks_hbm.3, s32[16,128]{1,0:T(8,128)} %bitcast.17, f32[1408,128]{1,0:T(8,128)} %constant.5.clone.table_hbm), custom_call_target="tpu_custom_call" | custom-call | tf_op jit(solution)/shard_map/masses/pallas_call | solution.py:303
  54.0 42.3 %all-to-all-done = f32[256,19,1,128]{3,2,1,0:T(1,128)S(1)} async-done(((f32[256,19,1,128]{3,2,1,0:T(1,128)}), f32[256,19,1,128]{3,2,1,0:T(1,128)S(1)}, u32[]{:S(2)}, u32[]{:S(2)}) %all-to-all-start) | async-done | bytes 2490400 | tf_op jit(solution)/shard_map/all_to_all | solution.py:501
  96.3 0.0 copy-start
  96.3 3.3 %collective-permute-start.1 = (f32[4864,128]{1,0:T(8,128)S(1)}, f32[4864,128]{1,0:T(8,128)}, u32[]{:S(2)}, u32[]{:S(2)}) collective-permute-start(f32[4864,128]{1,0:T(8,128)S(1)} %bitcast.9), channel_id=1, source_target_pairs={{1,0},{2,1},{3,2},{4,3},{5,4},{6,5},{7,6},{8,7},{9,8},{10,9},{11,1... | collective-permute-start | bytes 7471112 | tf_op jit(solution)/shard_map/ppermute | solution.py:28
  99.6 1.9 collective-permute-start
  101.6 0.0 copy-done
  101.6 6.9 %unpack_faces.1.faces_ref = f32[150,4096]{1,0:T(8,128)} custom-call(f32[4864,128]{1,0:T(8,128)} %bitcast.11), custom_call_target="tpu_custom_call" | custom-call | tf_op jit(solution)/shard_map/unpack_faces/pallas_call | solution.py:358
  108.5 9.3 %collect_first.1.first_ref = f32[50,4096]{1,0:T(8,128)} custom-call(s32[6,4096]{1,0:T(8,128)} %bitcast.14, f32[150,4096]{1,0:T(8,128)} %unpack_faces.1.faces_ref), custom_call_target="tpu_custom_call" | custom-call | bytes 1024 | tf_op jit(solution)/shard_map/collect_first/pallas_call | solution.py:464
  117.8 9.9 %all-to-all-start.1 = ((f32[256,2,8,128]{3,2,1,0:T(8,128)}), f32[256,2,8,128]{3,2,1,0:T(8,128)}, u32[]{:S(2)}, u32[]{:S(2)}) async-start(f32[256,2,8,128]{3,2,1,0:T(8,128)} %bitcast.13), calls=%async_computation.1 | async-start | bytes 4194304 | tf_op jit(solution)/shard_map/all_to_all | solution.py:501
  127.7 4.0 %collective-permute-done.1.after_ref = f32[4864,128]{1,0:T(8,128)} collective-permute-done((f32[4864,128]{1,0:T(8,128)S(1)}, f32[4864,128]{1,0:T(8,128)}, u32[]{:S(2)}, u32[]{:S(2)}) %collective-permute-start.1) | collective-permute-done | bytes 2490400 | tf_op jit(solution)/shard_map/ppermute | solution.py:28
  131.8 9.7 %collective-permute-done.before_ref = f32[4864,128]{1,0:T(8,128)} collective-permute-done((f32[4864,128]{1,0:T(8,128)S(1)}, f32[4864,128]{1,0:T(8,128)}, u32[]{:S(2)}, u32[]{:S(2)}) %collective-permute-start) | collective-permute-done | bytes 2490400 | tf_op jit(solution)/shard_map/ppermute | solution.py:28
  141.5 46.1 %collect_neighbours.1 = f32[150,4096]{1,0:T(8,128)} custom-call(s32[6,4096]{1,0:T(8,128)} %bitcast.15, f32[4864,128]{1,0:T(8,128)} %collective-permute-done.before_ref, f32[4864,128]{1,0:T(8,128)} %collective-permute-done.1.after_ref, f32[150,4096]{1,0:T(8,128)} %unpack_faces.1.faces_ref, f32[50,4096]{1,0:T(8,128)} %collect_first.1.first_ref), custom_call_target="tpu_custom_call" | custom-call | flops 999999995904 | bytes 1000000000 | tf_op jit(solution)/shard_map/collect_neighbours/pallas_call | solution.py:481
  187.6 0.0 all-to-all-done.1
  187.6 5.4 %unpack_masses.1 = f32[125,4096]{1,0:T(8,128)} custom-call(f32[4096,128]{1,0:T(8,128)} %bitcast.6.in_ref), custom_call_target="tpu_custom_call" | custom-call | tf_op jit(solution)/shard_map/unpack_masses/pallas_call | solution.py:358
Async XLA Ops:
  20.5 75.8 %all-to-all-start = ((f32[256,19,1,128]{3,2,1,0:T(1,128)}), f32[256,19,1,128]{3,2,1,0:T(1,128)S(1)}, u32[]{:S(2)}, u32[]{:S(2)}) async-start(f32[256,19,1,128]{3,2,1,0:T(1,128)} %bitcast.12), calls=%async_computation | async-start | bytes 4980736 | tf_op jit(solution)/shard_map/all_to_all | solution.py:501
  96.3 5.3 %copy-start = (f32[256,19,1,128]{3,2,1,0:T(1,128)}, f32[256,19,1,128]{3,2,1,0:T(1,128)S(1)}, u32[]{:S(2)}) copy-start(f32[256,19,1,128]{3,2,1,0:T(1,128)S(1)} %all-to-all-done) | copy-start | bytes 7471108
  96.3 35.5 %collective-permute-start.1 = (f32[4864,128]{1,0:T(8,128)S(1)}, f32[4864,128]{1,0:T(8,128)}, u32[]{:S(2)}, u32[]{:S(2)}) collective-permute-start(f32[4864,128]{1,0:T(8,128)S(1)} %bitcast.9), channel_id=1, source_target_pairs={{1,0},{2,1},{3,2},{4,3},{5,4},{6,5},{7,6},{8,7},{9,8},{10,9},{11,1... | collective-permute-start | bytes 7471112 | tf_op jit(solution)/shard_map/ppermute | solution.py:28
  99.6 41.9 %collective-permute-start = (f32[4864,128]{1,0:T(8,128)S(1)}, f32[4864,128]{1,0:T(8,128)}, u32[]{:S(2)}, u32[]{:S(2)}) collective-permute-start(f32[4864,128]{1,0:T(8,128)S(1)} %bitcast.10), channel_id=1, source_target_pairs={{0,1},{1,2},{2,3},{3,4},{4,5},{5,6},{6,7},{7,8},{8,9},{9,10},{10,1... | collective-permute-start | bytes 7471112 | tf_op jit(solution)/shard_map/ppermute | solution.py:28
  117.8 69.8 %all-to-all-start.1 = ((f32[256,2,8,128]{3,2,1,0:T(8,128)}), f32[256,2,8,128]{3,2,1,0:T(8,128)}, u32[]{:S(2)}, u32[]{:S(2)}) async-start(f32[256,2,8,128]{3,2,1,0:T(8,128)} %bitcast.13), calls=%async_computation.1 | async-start | bytes 4194304 | tf_op jit(solution)/shard_map/all_to_all | solution.py:501

commit v10 on v9

--- a/solution.py
+++ b/solution.py
@@ -11,7 +11,7 @@
 
 F32 = jnp.float32
 BF16 = jnp.bfloat16
-FIRST, SECOND = (0, 1), (2, 3, 4, 5)
+FIRST, SECOND = (0, 1, 2), (3, 4, 5)
 PARTS = 2
 VMEM = 60 << 20
 GROUPS = 8

time: 193 us -> 190 us (0.984); the launches traced: 193 us -> 187 us
  waiting for transfers between devices: 56.1 us -> 50 us
    ppermute x2, waiting for transfers between devices: 13.8 us -> 6.12 us  [shifted(): return lax.ppermute(array, axis, pairs)]
    pallas_call x1, Pallas kernels: 9.34 us -> 11.4 us  [collect_own(): pl.pallas_call(functools.partial(own_kernel, chosen), out_shape=jax.Shape...]
  transfers between devices with their start and end apart: 4 -> 4, of which waited for: 3 -> 3; matrix products, arithmetic and copies ran while one was open for 0% -> 0% of each run, Pallas kernels for 42% -> 44%
where the time goes in v10:
time: 190 us; the launch traced here: 187 us
  Pallas kernels  107 us (56%)
  waiting for transfers between devices  50 us (26%)
  starting transfers between devices  29.6 us (16%)
    pallas_call x1, Pallas kernels, collect_neighbours(): pl.pallas_call(neighbour_kernel, out_shape=jax.ShapeDtypeStruct((150, slo...  44.4 us
    all_to_all x2, waiting for transfers between devices, exchanged(): lax.all_to_all(blocks, ('seg', 'rank'), split_axis=0, concat_axis=0, tile...  43.9 us
    pallas_call x2, Pallas kernels, outgoing(): pl.pallas_call(functools.partial(child_kernel, values, rows, chunk, capac...  38.9 us
    all_to_all x2, starting transfers between devices, exchanged(): lax.all_to_all(blocks, ('seg', 'rank'), split_axis=0, concat_axis=0, tile...  24.3 us
    pallas_call x2, Pallas kernels, unpack(): pl.pallas_call(functools.partial(unpack_kernel, rows, chunk, height), out...  12.3 us
    pallas_call x1, Pallas kernels, collect_own(): pl.pallas_call(functools.partial(own_kernel, chosen), out_shape=jax.Shape...  11.4 us
    ppermute x2, waiting for transfers between devices, shifted(): return lax.ppermute(array, axis, pairs)  6.12 us
    ppermute x2, starting transfers between devices, shifted(): return lax.ppermute(array, axis, pairs)  5.25 us
  transfers between devices with their start and end apart: 4, of which 3 were waited for; matrix products, arithmetic and copies ran while one was open for 0% of the time, Pallas kernels for 44%

profile of v10, /device:TPU:32, one launch (start us, length us, event | category | flops | bytes accessed | tf_op | source)
XLA Modules:
  0.0 187.3 jit_solution(17494398603823243004)
XLA Ops:
  0.6 19.9 %faces.1 = f32[4864,128]{1,0:T(8,128)} custom-call(f32[375,2560]{1,0:T(8,128)} %bitcast.7, s32[1,256]{1,0:T(1,128)} %marks_hbm.3, s32[16,128]{1,0:T(8,128)} %bitcast.16, f32[1328,128]{1,0:T(8,128)} %constant.4.clone.table_hbm), custom_call_target="tpu_custom_call" | custom-call | tf_op jit(solution)/shard_map/faces/pallas_call | solution.py:303
  20.5 14.4 %all-to-all-start = ((f32[256,19,1,128]{3,2,1,0:T(1,128)}), f32[256,19,1,128]{3,2,1,0:T(1,128)S(1)}, u32[]{:S(2)}, u32[]{:S(2)}) async-start(f32[256,19,1,128]{3,2,1,0:T(1,128)} %bitcast.12), calls=%async_computation | async-start | bytes 4980736 | tf_op jit(solution)/shard_map/all_to_all | solution.py:501
  34.9 19.0 %masses.1 = f32[4096,128]{1,0:T(8,128)} custom-call(f32[375,2560]{1,0:T(8,128)} %bitcast.8, s32[1,256]{1,0:T(1,128)} %marks_hbm.3, s32[16,128]{1,0:T(8,128)} %bitcast.17, f32[1408,128]{1,0:T(8,128)} %constant.5.clone.table_hbm), custom_call_target="tpu_custom_call" | custom-call | tf_op jit(solution)/shard_map/masses/pallas_call | solution.py:303
  54.0 42.3 %all-to-all-done = f32[256,19,1,128]{3,2,1,0:T(1,128)S(1)} async-done(((f32[256,19,1,128]{3,2,1,0:T(1,128)}), f32[256,19,1,128]{3,2,1,0:T(1,128)S(1)}, u32[]{:S(2)}, u32[]{:S(2)}) %all-to-all-start) | async-done | bytes 2490400 | tf_op jit(solution)/shard_map/all_to_all | solution.py:501
  96.3 0.0 copy-start
  96.3 3.3 %collective-permute-start.1 = (f32[4864,128]{1,0:T(8,128)S(1)}, f32[4864,128]{1,0:T(8,128)}, u32[]{:S(2)}, u32[]{:S(2)}) collective-permute-start(f32[4864,128]{1,0:T(8,128)S(1)} %bitcast.9), channel_id=1, source_target_pairs={{1,0},{2,1},{3,2},{4,3},{5,4},{6,5},{7,6},{8,7},{9,8},{10,9},{11,1... | collective-permute-start | bytes 7471112 | tf_op jit(solution)/shard_map/ppermute | solution.py:28
  99.6 1.9 %collective-permute-start = (f32[4864,128]{1,0:T(8,128)S(1)}, f32[4864,128]{1,0:T(8,128)}, u32[]{:S(2)}, u32[]{:S(2)}) collective-permute-start(f32[4864,128]{1,0:T(8,128)S(1)} %bitcast.10), channel_id=1, source_target_pairs={{0,1},{1,2},{2,3},{3,4},{4,5},{5,6},{6,7},{7,8},{8,9},{9,10},{10,1... | collective-permute-start | bytes 7471112 | tf_op jit(solution)/shard_map/ppermute | solution.py:28
  101.6 0.0 copy-done
  101.6 6.9 %unpack_faces.1.faces_ref = f32[150,4096]{1,0:T(8,128)} custom-call(f32[4864,128]{1,0:T(8,128)} %bitcast.11), custom_call_target="tpu_custom_call" | custom-call | tf_op jit(solution)/shard_map/unpack_faces/pallas_call | solution.py:358
  108.5 11.4 %collect_first.1.first_ref = f32[75,4096]{1,0:T(8,128)} custom-call(s32[6,4096]{1,0:T(8,128)} %bitcast.14, f32[150,4096]{1,0:T(8,128)} %unpack_faces.1.faces_ref), custom_call_target="tpu_custom_call" | custom-call | bytes 1024 | tf_op jit(solution)/shard_map/collect_first/pallas_call | solution.py:464
  119.9 9.9 %all-to-all-start.1 = ((f32[256,2,8,128]{3,2,1,0:T(8,128)}), f32[256,2,8,128]{3,2,1,0:T(8,128)}, u32[]{:S(2)}, u32[]{:S(2)}) async-start(f32[256,2,8,128]{3,2,1,0:T(8,128)} %bitcast.13), calls=%async_computation.1 | async-start | bytes 4194304 | tf_op jit(solution)/shard_map/all_to_all | solution.py:501
  129.8 0.0 collective-permute-done.1.after_ref
  129.8 6.1 %collective-permute-done.before_ref = f32[4864,128]{1,0:T(8,128)} collective-permute-done((f32[4864,128]{1,0:T(8,128)S(1)}, f32[4864,128]{1,0:T(8,128)}, u32[]{:S(2)}, u32[]{:S(2)}) %collective-permute-start) | collective-permute-done | bytes 2490400 | tf_op jit(solution)/shard_map/ppermute | solution.py:28
  136.0 44.4 %collect_neighbours.1 = f32[150,4096]{1,0:T(8,128)} custom-call(s32[6,4096]{1,0:T(8,128)} %bitcast.15, f32[4864,128]{1,0:T(8,128)} %collective-permute-done.before_ref, f32[4864,128]{1,0:T(8,128)} %collective-permute-done.1.after_ref, f32[150,4096]{1,0:T(8,128)} %unpack_faces.1.faces_ref, f32[75,4096]{1,0:T(8,128)} %collect_first.1.first_ref), custom_call_target="tpu_custom_call" | custom-call | flops 999999995904 | bytes 1000000000 | tf_op jit(solution)/shard_map/collect_neighbours/pallas_call | solution.py:481
  180.3 1.5 all-to-all-done.1
  181.9 5.4 %unpack_masses.1 = f32[125,4096]{1,0:T(8,128)} custom-call(f32[4096,128]{1,0:T(8,128)} %bitcast.6.in_ref), custom_call_target="tpu_custom_call" | custom-call | tf_op jit(solution)/shard_map/unpack_masses/pallas_call | solution.py:358
Async XLA Ops:
  20.5 75.8 %all-to-all-start = ((f32[256,19,1,128]{3,2,1,0:T(1,128)}), f32[256,19,1,128]{3,2,1,0:T(1,128)S(1)}, u32[]{:S(2)}, u32[]{:S(2)}) async-start(f32[256,19,1,128]{3,2,1,0:T(1,128)} %bitcast.12), calls=%async_computation | async-start | bytes 4980736 | tf_op jit(solution)/shard_map/all_to_all | solution.py:501
  96.3 5.3 %copy-start = (f32[256,19,1,128]{3,2,1,0:T(1,128)}, f32[256,19,1,128]{3,2,1,0:T(1,128)S(1)}, u32[]{:S(2)}) copy-start(f32[256,19,1,128]{3,2,1,0:T(1,128)S(1)} %all-to-all-done) | copy-start | bytes 7471108
  96.3 33.5 %collective-permute-start.1 = (f32[4864,128]{1,0:T(8,128)S(1)}, f32[4864,128]{1,0:T(8,128)}, u32[]{:S(2)}, u32[]{:S(2)}) collective-permute-start(f32[4864,128]{1,0:T(8,128)S(1)} %bitcast.9), channel_id=1, source_target_pairs={{1,0},{2,1},{3,2},{4,3},{5,4},{6,5},{7,6},{8,7},{9,8},{10,9},{11,1... | collective-permute-start | bytes 7471112 | tf_op jit(solution)/shard_map/ppermute | solution.py:28
  99.6 36.3 %collective-permute-start = (f32[4864,128]{1,0:T(8,128)S(1)}, f32[4864,128]{1,0:T(8,128)}, u32[]{:S(2)}, u32[]{:S(2)}) collective-permute-start(f32[4864,128]{1,0:T(8,128)S(1)} %bitcast.10), channel_id=1, source_target_pairs={{0,1},{1,2},{2,3},{3,4},{4,5},{5,6},{6,7},{7,8},{8,9},{9,10},{10,1... | collective-permute-start | bytes 7471112 | tf_op jit(solution)/shard_map/ppermute | solution.py:28
  119.9 62.0 %all-to-all-start.1 = ((f32[256,2,8,128]{3,2,1,0:T(8,128)}), f32[256,2,8,128]{3,2,1,0:T(8,128)}, u32[]{:S(2)}, u32[]{:S(2)}) async-start(f32[256,2,8,128]{3,2,1,0:T(8,128)} %bitcast.13), calls=%async_computation.1 | async-start | bytes 4194304 | tf_op jit(solution)/shard_map/all_to_all | solution.py:501
